TPU v7x, 512 devices: a whole 4x8x8 slice. The times are simulated.
512 devices in a mesh: ctx: 128 (over z, y, core), head: 4 (over x).
Axes of the slice: x: 4, y: 8, z: 8, core: 2. Of those that a mesh axis runs over, the one named last changes fastest.
Arguments:
- queries: bfloat16 [49152, 8, 128], P('ctx', 'head'), may hold values from -6 to 6
- key_rows: bfloat16 [49152, 128], P('ctx'), may hold values from -6 to 6
- value_rows: bfloat16 [49152, 128], P('ctx'), may hold values from -6 to 6
- grad_out: bfloat16 [49152, 8, 128], P('ctx', 'head'), may hold values from -6 to 6
- doc_lengths: int32 [64], replicated, may hold values from 1 to 36864, as said below
- block_pattern: int32 [384, 384], P('ctx'), may hold values from 0 to 1, as said below
Outputs:
- attn_out: bfloat16 [49152, 8, 128], P('ctx', 'head')
- grad_queries: bfloat16 [49152, 8, 128], P('ctx', 'head')
- grad_keys: bfloat16 [49152, 128], P('ctx')
- grad_values: bfloat16 [49152, 128], P('ctx')
Inputs may be any that keep to these rules, and one draw needn't show every extreme that they name: block_pattern[i, j] is 0 unless i // 3 - j // 3 is 0 or a positive power of two; it is 1 where i == j. `doc_lengths`: the lengths sum to 49152; the first document has exactly 36864 positions.
All inputs are finite; a program needn't handle non-finite values.
Results may differ from a plain program's by a relative error of at most 0.017.
Values may be sent and summed in bfloat16 or wider, within the bound.
No kernel may reach another device: no remote copies, remote signals or barrier semaphores. Data moves between devices by JAX's collectives and lax.ppermute only.
A program may use at most 64 MiB of HBM per device.

v0:
```python
import math

import jax
import jax.numpy as jnp
from jax import lax
from jax.sharding import PartitionSpec as P

NEG_FILL = -1e30


def passed_along(value, axis, steps):
    count = lax.axis_size(axis)
    leading, last = (max(0, -steps), min(count, count - steps))
    return lax.ppermute(value, axis, [(source, source + steps) for source in range(leading, last)])


def gathered_total(array, axis):
    pieces = lax.all_gather(array, axis)
    return pieces.sum(axis=0)


def doc_of(doc_ends, positions):
    return jnp.sum((doc_ends[None, :] <= positions[:, None]).astype(jnp.int32), axis=1)


def local(queries, key_rows, value_rows, grad_out, doc_lengths, block_pattern):
    tok_rows = queries.shape[0]
    local_heads = queries.shape[1]
    head_dim = key_rows.shape[1]
    block_count = block_pattern.shape[0]
    block_rows = tok_rows // block_count
    score_scale = 1.0 / math.sqrt(head_dim)
    ctx_width = lax.axis_size("ctx")
    level_count = ctx_width.bit_length() - 1
    own_index = lax.axis_index("ctx")
    offsets = jnp.arange(tok_rows, dtype=jnp.int32)
    query_pos = own_index * tok_rows + offsets
    doc_ends = jnp.cumsum(doc_lengths, dtype=jnp.int32)
    query_doc = doc_of(doc_ends, query_pos)
    partner_list = [own_index] + [own_index - (1 << bit_index) for bit_index in range(level_count)]
    active_list = [None] + [own_index >= 1 << bit_index for bit_index in range(level_count)]

    def level_mask(section_index):
        partner = jnp.maximum(partner_list[section_index], 0)
        key_pos = partner * tok_rows + offsets
        live_blocks = lax.dynamic_slice_in_dim(block_pattern, partner * block_count, block_count, 1)
        live_blocks = jnp.repeat(jnp.repeat(live_blocks, block_rows, axis=0), block_rows, axis=1)
        same_doc = query_doc[:, None] == doc_of(doc_ends, key_pos)[None, :]
        live = (live_blocks == 1) & same_doc & (key_pos[None, :] <= query_pos[:, None])
        if section_index == 0:
            return live
        return live & active_list[section_index]

    mask_list = [level_mask(section_index) for section_index in range(level_count + 1)]
    held_pairs = [(key_rows, value_rows)] + [
        passed_along((key_rows, value_rows), "ctx", 1 << bit_index)
        for bit_index in range(level_count)
    ]

    def run_level(section_index, level_work):
        if section_index == 0:
            return level_work()
        return level_work()

    score_list = []
    row_max = None
    row_total = None
    for section_index in range(level_count + 1):
        keys_here = held_pairs[section_index][0]
        live_mask = mask_list[section_index]

        def stat_work():
            raw_scores = (
                jnp.einsum("thd,ud->htu", queries, keys_here, preferred_element_type=jnp.float32)
                * score_scale
            )
            scores = jnp.where(live_mask[None], raw_scores, NEG_FILL)
            level_max = jnp.max(scores, axis=-1)
            level_total = jnp.sum(
                jnp.where(live_mask[None], jnp.exp(scores - level_max[..., None]), 0.0), axis=-1
            )
            return (scores, level_max, level_total)

        scores, level_max, level_total = run_level(section_index, stat_work)
        score_list.append(scores)
        if row_max is None:
            row_max = level_max
            row_total = level_total
        else:
            new_max = jnp.maximum(row_max, level_max)
            row_total = row_total * jnp.exp(row_max - new_max) + level_total * jnp.exp(
                level_max - new_max
            )
            row_max = new_max

    def probs_of(scores, live_mask):
        return jnp.where(
            live_mask[None], jnp.exp(scores - row_max[..., None]) / row_total[..., None], 0.0
        )

    out_acc = jnp.zeros((tok_rows, local_heads, head_dim), jnp.float32)
    for section_index in range(level_count + 1):
        values_here = held_pairs[section_index][1]
        live_mask = mask_list[section_index]
        scores = score_list[section_index]

        def output_work():
            probs_low = probs_of(scores, live_mask).astype(jnp.bfloat16)
            return jnp.einsum(
                "htu,ud->thd", probs_low, values_here, preferred_element_type=jnp.float32
            )

        out_acc = out_acc + run_level(section_index, output_work)
    attn_out = out_acc.astype(jnp.bfloat16)
    out_dot = jnp.sum(grad_out.astype(jnp.float32) * attn_out.astype(jnp.float32), axis=-1).T
    query_grad = jnp.zeros((tok_rows, local_heads, head_dim), jnp.float32)
    keys_grad = jnp.zeros((tok_rows, head_dim), jnp.float32)
    values_grad = jnp.zeros((tok_rows, head_dim), jnp.float32)
    for section_index in range(level_count + 1):
        keys_here, values_here = held_pairs[section_index]
        live_mask = mask_list[section_index]
        scores = score_list[section_index]

        def backward_work():
            probs = probs_of(scores, live_mask)
            probs_low = probs.astype(jnp.bfloat16)
            grad_prob = jnp.einsum(
                "thd,ud->htu", grad_out, values_here, preferred_element_type=jnp.float32
            )
            grad_score = (probs * (grad_prob - out_dot[..., None]) * score_scale).astype(
                jnp.bfloat16
            )
            part_query = jnp.einsum(
                "htu,ud->thd", grad_score, keys_here, preferred_element_type=jnp.float32
            )
            part_key = jnp.einsum(
                "htu,thd->ud", grad_score, queries, preferred_element_type=jnp.float32
            )
            part_value = jnp.einsum(
                "htu,thd->ud", probs_low, grad_out, preferred_element_type=jnp.float32
            )
            return (part_query, part_key, part_value)

        part_query, part_key, part_value = run_level(section_index, backward_work)
        query_grad = query_grad + part_query
        if section_index == 0:
            keys_grad = part_key
            values_grad = part_value
        else:
            back_key, back_value = passed_along(
                (part_key, part_value), "ctx", -(1 << section_index - 1)
            )
            keys_grad = keys_grad + back_key
            values_grad = values_grad + back_value
    keys_grad, values_grad = (
        gathered_total(keys_grad, "head"),
        gathered_total(values_grad, "head"),
    )
    return (
        attn_out,
        query_grad.astype(jnp.bfloat16),
        keys_grad.astype(jnp.bfloat16),
        values_grad.astype(jnp.bfloat16),
    )


def solution(mesh):
    placed = (
        P("ctx", "head", None),
        P("ctx", None),
        P("ctx", None),
        P("ctx", "head", None),
        P(),
        P("ctx", None),
    )
    return jax.shard_map(
        local,
        mesh=mesh,
        in_specs=placed,
        out_specs=(P("ctx", "head", None), P("ctx", "head", None), P("ctx", None), P("ctx", None)),
        check_vma=False,
    )
```

profile of v0, /device:TPU:88, one launch (start us, length us, event | category | flops | bytes accessed | tf_op | source)
XLA Modules:
  0.0 182.9 jit_solution(11683581133230535977)
XLA Ops:
  0.7 5.2 %collective-permute-start.3 = (bf16[384,128]{1,0:T(8,128)(2,1)}, bf16[384,128]{1,0:T(8,128)(2,1)S(1)}, u32[]{:S(2)}, u32[]{:S(2)}) collective-permute-start(bf16[384,128]{1,0:T(8,128)(2,1)} %param.7), channel_id=1, source_target_pairs={{0,32},{4,36},{8,40},{12,44},{16,48},{20,52},{24,56},{28,60},{32,6... | collective-permute-start | bytes 294920 | tf_op jit(solution)/shard_map/ppermute | solution.py:14
  5.8 4.5 %collective-permute-start.2 = (bf16[384,128]{1,0:T(8,128)(2,1)}, bf16[384,128]{1,0:T(8,128)(2,1)S(1)}, u32[]{:S(2)}, u32[]{:S(2)}) collective-permute-start(bf16[384,128]{1,0:T(8,128)(2,1)} %param.7), channel_id=1, source_target_pairs={{0,16},{4,20},{8,24},{12,28},{16,32},{20,36},{24,40},{28,44},{32,4... | collective-permute-start | bytes 294920 | tf_op jit(solution)/shard_map/ppermute | solution.py:14
  10.3 3.5 %collective-permute-start.1 = (bf16[384,128]{1,0:T(8,128)(2,1)}, bf16[384,128]{1,0:T(8,128)(2,1)S(1)}, u32[]{:S(2)}, u32[]{:S(2)}) collective-permute-start(bf16[384,128]{1,0:T(8,128)(2,1)} %param.7), channel_id=1, source_target_pairs={{0,8},{4,12},{8,16},{12,20},{16,24},{20,28},{24,32},{28,36},{32,40... | collective-permute-start | bytes 294920 | tf_op jit(solution)/shard_map/ppermute | solution.py:14
  13.8 1.9 %collective-permute-start = (bf16[384,128]{1,0:T(8,128)(2,1)}, bf16[384,128]{1,0:T(8,128)(2,1)S(1)}, u32[]{:S(2)}, u32[]{:S(2)}) collective-permute-start(bf16[384,128]{1,0:T(8,128)(2,1)} %param.7), channel_id=1, source_target_pairs={{0,4},{4,8},{8,12},{12,16},{16,20},{20,24},{24,28},{28,32},{32,36}... | collective-permute-start | bytes 294920 | tf_op jit(solution)/shard_map/ppermute | solution.py:14
  15.8 7.3 %collective-permute-start.5 = (bf16[384,128]{1,0:T(8,128)(2,1)}, bf16[384,128]{1,0:T(8,128)(2,1)S(1)}, u32[]{:S(2)}, u32[]{:S(2)}) collective-permute-start(bf16[384,128]{1,0:T(8,128)(2,1)} %param.7), channel_id=1, source_target_pairs={{0,128},{4,132},{8,136},{12,140},{16,144},{20,148},{24,152},{28,15... | collective-permute-start | bytes 294920 | tf_op jit(solution)/shard_map/ppermute | solution.py:14
  23.1 1.1 dynamic-slice_compare_fusion.6
  26.6 1.1 copy.194
  27.7 1.0 copy.179
  29.1 1.0 fusion.90
  30.5 1.0 fusion.89
  31.7 3.4 %collective-permute-start.4 = (bf16[384,128]{1,0:T(8,128)(2,1)S(1)}, bf16[384,128]{1,0:T(8,128)(2,1)S(1)}, u32[]{:S(2)}, u32[]{:S(2)}) collective-permute-start(bf16[384,128]{1,0:T(8,128)(2,1)S(1)} %copy-done.4), channel_id=1, source_target_pairs={{0,64},{4,68},{8,72},{12,76},{16,80},{20,84},{24,88},{28,92},{32,9... | collective-permute-start | bytes 294920 | tf_op jit(solution)/shard_map/ppermute | solution.py:14
  35.5 3.1 %collective-permute-start.6 = (bf16[384,128]{1,0:T(8,128)(2,1)S(1)}, bf16[384,128]{1,0:T(8,128)(2,1)S(1)}, u32[]{:S(2)}, u32[]{:S(2)}) collective-permute-start(bf16[384,128]{1,0:T(8,128)(2,1)S(1)} %copy-done.4), channel_id=1, source_target_pairs={{0,256},{4,260},{8,264},{12,268},{16,272},{20,276},{24,280},{28,28... | collective-permute-start | bytes 294920 | tf_op jit(solution)/shard_map/ppermute | solution.py:14
  39.3 3.0 %collective-permute-start.7 = (bf16[384,128]{0,1:T(8,128)(2,1)S(1)}, bf16[384,128]{0,1:T(8,128)(2,1)S(1)}, u32[]{:S(2)}, u32[]{:S(2)}) collective-permute-start(bf16[384,128]{0,1:T(8,128)(2,1)S(1)} %copy.179), channel_id=1, source_target_pairs={{0,4},{4,8},{8,12},{12,16},{16,20},{20,24},{24,28},{28,32},{32,36}... | collective-permute-start | bytes 294920 | tf_op jit(solution)/shard_map/ppermute | solution.py:14
  43.0 4.8 %collective-permute-start.9 = (bf16[384,128]{0,1:T(8,128)(2,1)S(1)}, bf16[384,128]{0,1:T(8,128)(2,1)S(1)}, u32[]{:S(2)}, u32[]{:S(2)}) collective-permute-start(bf16[384,128]{0,1:T(8,128)(2,1)S(1)} %copy.179), channel_id=1, source_target_pairs={{0,16},{4,20},{8,24},{12,28},{16,32},{20,36},{24,40},{28,44},{32,4... | collective-permute-start | bytes 294920 | tf_op jit(solution)/shard_map/ppermute | solution.py:14
  48.5 2.6 %collective-permute-start.10 = (bf16[384,128]{0,1:T(8,128)(2,1)S(1)}, bf16[384,128]{0,1:T(8,128)(2,1)S(1)}, u32[]{:S(2)}, u32[]{:S(2)}) collective-permute-start(bf16[384,128]{0,1:T(8,128)(2,1)S(1)} %copy.179), channel_id=1, source_target_pairs={{0,32},{4,36},{8,40},{12,44},{16,48},{20,52},{24,56},{28,60},{32,6... | collective-permute-start | bytes 294920 | tf_op jit(solution)/shard_map/ppermute | solution.py:14
  51.8 2.8 %collective-permute-start.11 = (bf16[384,128]{0,1:T(8,128)(2,1)S(1)}, bf16[384,128]{0,1:T(8,128)(2,1)S(1)}, u32[]{:S(2)}, u32[]{:S(2)}) collective-permute-start(bf16[384,128]{0,1:T(8,128)(2,1)S(1)} %copy.179), channel_id=1, source_target_pairs={{0,64},{4,68},{8,72},{12,76},{16,80},{20,84},{24,88},{28,92},{32,9... | collective-permute-start | bytes 294920 | tf_op jit(solution)/shard_map/ppermute | solution.py:14
  55.5 1.6 collective-permute-start.12
  58.6 1.1 convolution_bitcast_fusion.12
  59.7 1.1 convolution_bitcast_fusion.11
  60.7 1.1 convolution_bitcast_fusion.10
  61.8 1.1 convolution_bitcast_fusion.9
  63.3 1.3 collective-permute-start.13
  65.0 1.1 convolution_bitcast_fusion.8
  66.1 3.5 %collective-permute-start.8 = (bf16[384,128]{0,1:T(8,128)(2,1)S(1)}, bf16[384,128]{0,1:T(8,128)(2,1)S(1)}, u32[]{:S(2)}, u32[]{:S(2)}) collective-permute-start(bf16[384,128]{0,1:T(8,128)(2,1)S(1)} %copy.179), channel_id=1, source_target_pairs={{0,8},{4,12},{8,16},{12,20},{16,24},{20,28},{24,32},{28,36},{32,40... | collective-permute-start | bytes 294920 | tf_op jit(solution)/shard_map/ppermute | solution.py:14
  70.0 1.9 %collective-permute-start.21 = (f32[384,128]{1,0:T(8,128)S(1)}, f32[384,128]{1,0:T(8,128)S(1)}, u32[]{:S(2)}, u32[]{:S(2)}) collective-permute-start(f32[384,128]{1,0:T(8,128)S(1)} %convolution_bitcast_fusion.14), channel_id=1, source_target_pairs={{4,0},{8,4},{12,8},{16,12},{20,16},{24,20},{28,24},{32,28},{36,32}... | collective-permute-start | bytes 589832 | tf_op jit(solution)/shard_map/ppermute | solution.py:14
  72.4 2.8 %collective-permute-start.22 = (f32[384,128]{1,0:T(8,128)S(1)}, f32[384,128]{1,0:T(8,128)S(1)}, u32[]{:S(2)}, u32[]{:S(2)}) collective-permute-start(f32[384,128]{1,0:T(8,128)S(1)} %convolution_bitcast_fusion.13), channel_id=1, source_target_pairs={{8,0},{12,4},{16,8},{20,12},{24,16},{28,20},{32,24},{36,28},{40,32... | collective-permute-start | bytes 589832 | tf_op jit(solution)/shard_map/ppermute | solution.py:14
  78.0 1.0 convolution_bitcast_fusion.21
  86.7 1.0 convolution_bitcast_fusion.19
  87.7 6.5 %collective-permute-start.23 = (f32[384,128]{1,0:T(8,128)}, f32[384,128]{1,0:T(8,128)}, u32[]{:S(2)}, u32[]{:S(2)}) collective-permute-start(f32[384,128]{1,0:T(8,128)} %convolution_bitcast_fusion.12), channel_id=1, source_target_pairs={{16,0},{20,4},{24,8},{28,12},{32,16},{36,20},{40,24},{44,28},{48,3... | collective-permute-start | bytes 589832 | tf_op jit(solution)/shard_map/ppermute | solution.py:14
  94.3 4.2 %collective-permute-start.24 = (f32[384,128]{1,0:T(8,128)}, f32[384,128]{1,0:T(8,128)}, u32[]{:S(2)}, u32[]{:S(2)}) collective-permute-start(f32[384,128]{1,0:T(8,128)} %convolution_bitcast_fusion.11), channel_id=1, source_target_pairs={{32,0},{36,4},{40,8},{44,12},{48,16},{52,20},{56,24},{60,28},{64,3... | collective-permute-start | bytes 589832 | tf_op jit(solution)/shard_map/ppermute | solution.py:14
  98.4 1.9 %collective-permute-start.25 = (f32[384,128]{1,0:T(8,128)}, f32[384,128]{1,0:T(8,128)}, u32[]{:S(2)}, u32[]{:S(2)}) collective-permute-start(f32[384,128]{1,0:T(8,128)} %convolution_bitcast_fusion.10), channel_id=1, source_target_pairs={{64,0},{68,4},{72,8},{76,12},{80,16},{84,20},{88,24},{92,28},{96,3... | collective-permute-start | bytes 589832 | tf_op jit(solution)/shard_map/ppermute | solution.py:14
  100.4 1.0 convolution_bitcast_fusion.18
  101.4 1.3 collective-permute-start.26
  102.7 1.3 collective-permute-start.27
  104.0 1.0 convolution_bitcast_fusion.17
  105.0 0.9 copy.234
  105.8 0.9 copy.233
  107.0 2.9 %collective-permute-start.15 = (f32[384,128]{1,0:T(8,128)}, f32[384,128]{1,0:T(8,128)S(1)}, u32[]{:S(2)}, u32[]{:S(2)}) collective-permute-start(f32[384,128]{1,0:T(8,128)} %convolution_bitcast_fusion.21), channel_id=1, source_target_pairs={{8,0},{12,4},{16,8},{20,12},{24,16},{28,20},{32,24},{36,28},{40,32... | collective-permute-start | bytes 589832 | tf_op jit(solution)/shard_map/ppermute | solution.py:14
  110.0 2.9 %collective-permute-start.14 = (f32[384,128]{1,0:T(8,128)S(1)}, f32[384,128]{1,0:T(8,128)S(1)}, u32[]{:S(2)}, u32[]{:S(2)}) collective-permute-start(f32[384,128]{1,0:T(8,128)S(1)} %convolution_bitcast_fusion.22), channel_id=1, source_target_pairs={{4,0},{8,4},{12,8},{16,12},{20,16},{24,20},{28,24},{32,28},{36,32}... | collective-permute-start | bytes 589832 | tf_op jit(solution)/shard_map/ppermute | solution.py:14
  113.0 7.5 %collective-permute-start.16 = (f32[384,128]{1,0:T(8,128)S(1)}, f32[384,128]{1,0:T(8,128)S(1)}, u32[]{:S(2)}, u32[]{:S(2)}) collective-permute-start(f32[384,128]{1,0:T(8,128)S(1)} %convolution_bitcast_fusion.20), channel_id=1, source_target_pairs={{16,0},{20,4},{24,8},{28,12},{32,16},{36,20},{40,24},{44,28},{48,3... | collective-permute-start | bytes 589832 | tf_op jit(solution)/shard_map/ppermute | solution.py:14
  120.5 16.5 %collective-permute-start.17 = (f32[384,128]{1,0:T(8,128)}, f32[384,128]{1,0:T(8,128)S(1)}, u32[]{:S(2)}, u32[]{:S(2)}) collective-permute-start(f32[384,128]{1,0:T(8,128)} %convolution_bitcast_fusion.19), channel_id=1, source_target_pairs={{32,0},{36,4},{40,8},{44,12},{48,16},{52,20},{56,24},{60,28},{64,3... | collective-permute-start | bytes 589832 | tf_op jit(solution)/shard_map/ppermute | solution.py:14
  137.0 1.9 %collective-permute-start.18 = (f32[384,128]{1,0:T(8,128)}, f32[384,128]{1,0:T(8,128)S(1)}, u32[]{:S(2)}, u32[]{:S(2)}) collective-permute-start(f32[384,128]{1,0:T(8,128)} %convolution_bitcast_fusion.18), channel_id=1, source_target_pairs={{64,0},{68,4},{72,8},{76,12},{80,16},{84,20},{88,24},{92,28},{96,3... | collective-permute-start | bytes 589832 | tf_op jit(solution)/shard_map/ppermute | solution.py:14
  139.0 1.8 fusion.75
  140.8 1.3 collective-permute-start.19
  142.1 1.3 collective-permute-start.20
  143.4 14.6 %all-gather.1 = f32[1536,128]{1,0:T(8,128)S(1)} all-gather(f32[384,128]{1,0:T(8,128)S(1)} %fusion.75), channel_id=3, replica_groups=mesh['ctx'=128,'head'=4] {'head'}, dimensions={0}, use_global_device_ids=true | all-gather | bytes 983040 | tf_op jit(solution)/shard_map/all_gather | solution.py:18
  158.1 9.5 %collective-permute-done.20 = f32[384,128]{1,0:T(8,128)S(1)} collective-permute-done((f32[384,128]{1,0:T(8,128)S(1)}, f32[384,128]{1,0:T(8,128)S(1)}, u32[]{:S(2)}, u32[]{:S(2)}) %collective-permute-start.20) | collective-permute-done | bytes 196640 | tf_op jit(solution)/shard_map/ppermute | solution.py:14
  168.0 13.6 %all-gather = f32[1536,128]{1,0:T(8,128)S(1)} all-gather(f32[384,128]{1,0:T(8,128)S(1)} %fusion.68), channel_id=2, replica_groups=mesh['ctx'=128,'head'=4] {'head'}, dimensions={0}, use_global_device_ids=true | all-gather | bytes 983040 | tf_op jit(solution)/shard_map/all_gather | solution.py:18
  (138 shorter events, 22.8 us)
Async XLA Ops:
  0.6 29.4 %copy-start = (bf16[384,2,128]{2,1,0:T(2,128)(2,1)S(1)}, bf16[384,2,128]{2,1,0:T(2,128)(2,1)}, u32[]{:S(2)}) copy-start(bf16[384,2,128]{2,1,0:T(2,128)(2,1)} %param.6) | copy-start | bytes 589828
  0.6 29.4 %copy-start.4 = (bf16[384,128]{1,0:T(8,128)(2,1)S(1)}, bf16[384,128]{1,0:T(8,128)(2,1)}, u32[]{:S(2)}) copy-start(bf16[384,128]{1,0:T(8,128)(2,1)} %param.7) | copy-start | bytes 294916
  0.7 31.1 %collective-permute-start.3 = (bf16[384,128]{1,0:T(8,128)(2,1)}, bf16[384,128]{1,0:T(8,128)(2,1)S(1)}, u32[]{:S(2)}, u32[]{:S(2)}) collective-permute-start(bf16[384,128]{1,0:T(8,128)(2,1)} %param.7), channel_id=1, source_target_pairs={{0,32},{4,36},{8,40},{12,44},{16,48},{20,52},{24,56},{28,60},{32,6... | collective-permute-start | bytes 294920 | tf_op jit(solution)/shard_map/ppermute | solution.py:14
  5.8 29.7 %collective-permute-start.2 = (bf16[384,128]{1,0:T(8,128)(2,1)}, bf16[384,128]{1,0:T(8,128)(2,1)S(1)}, u32[]{:S(2)}, u32[]{:S(2)}) collective-permute-start(bf16[384,128]{1,0:T(8,128)(2,1)} %param.7), channel_id=1, source_target_pairs={{0,16},{4,20},{8,24},{12,28},{16,32},{20,36},{24,40},{28,44},{32,4... | collective-permute-start | bytes 294920 | tf_op jit(solution)/shard_map/ppermute | solution.py:14
  10.3 28.9 %collective-permute-start.1 = (bf16[384,128]{1,0:T(8,128)(2,1)}, bf16[384,128]{1,0:T(8,128)(2,1)S(1)}, u32[]{:S(2)}, u32[]{:S(2)}) collective-permute-start(bf16[384,128]{1,0:T(8,128)(2,1)} %param.7), channel_id=1, source_target_pairs={{0,8},{4,12},{8,16},{12,20},{16,24},{20,28},{24,32},{28,36},{32,40... | collective-permute-start | bytes 294920 | tf_op jit(solution)/shard_map/ppermute | solution.py:14
  13.8 29.1 %collective-permute-start = (bf16[384,128]{1,0:T(8,128)(2,1)}, bf16[384,128]{1,0:T(8,128)(2,1)S(1)}, u32[]{:S(2)}, u32[]{:S(2)}) collective-permute-start(bf16[384,128]{1,0:T(8,128)(2,1)} %param.7), channel_id=1, source_target_pairs={{0,4},{4,8},{8,12},{12,16},{16,20},{20,24},{24,28},{28,32},{32,36}... | collective-permute-start | bytes 294920 | tf_op jit(solution)/shard_map/ppermute | solution.py:14
  15.8 32.7 %collective-permute-start.5 = (bf16[384,128]{1,0:T(8,128)(2,1)}, bf16[384,128]{1,0:T(8,128)(2,1)S(1)}, u32[]{:S(2)}, u32[]{:S(2)}) collective-permute-start(bf16[384,128]{1,0:T(8,128)(2,1)} %param.7), channel_id=1, source_target_pairs={{0,128},{4,132},{8,136},{12,140},{16,144},{20,148},{24,152},{28,15... | collective-permute-start | bytes 294920 | tf_op jit(solution)/shard_map/ppermute | solution.py:14
  31.7 7.3 %copy-start.5 = (bf16[384,128]{1,0:T(8,128)(2,1)}, bf16[384,128]{1,0:T(8,128)(2,1)S(1)}, u32[]{:S(2)}) copy-start(bf16[384,128]{1,0:T(8,128)(2,1)S(1)} %collective-permute-done.3) | copy-start | bytes 294916
  31.7 20.0 %collective-permute-start.4 = (bf16[384,128]{1,0:T(8,128)(2,1)S(1)}, bf16[384,128]{1,0:T(8,128)(2,1)S(1)}, u32[]{:S(2)}, u32[]{:S(2)}) collective-permute-start(bf16[384,128]{1,0:T(8,128)(2,1)S(1)} %copy-done.4), channel_id=1, source_target_pairs={{0,64},{4,68},{8,72},{12,76},{16,80},{20,84},{24,88},{28,92},{32,9... | collective-permute-start | bytes 294920 | tf_op jit(solution)/shard_map/ppermute | solution.py:14
  35.5 3.7 %copy-start.7 = (bf16[384,128]{1,0:T(8,128)(2,1)}, bf16[384,128]{1,0:T(8,128)(2,1)S(1)}, u32[]{:S(2)}) copy-start(bf16[384,128]{1,0:T(8,128)(2,1)S(1)} %collective-permute-done.2) | copy-start | bytes 294916
  35.5 19.9 %collective-permute-start.6 = (bf16[384,128]{1,0:T(8,128)(2,1)S(1)}, bf16[384,128]{1,0:T(8,128)(2,1)S(1)}, u32[]{:S(2)}, u32[]{:S(2)}) collective-permute-start(bf16[384,128]{1,0:T(8,128)(2,1)S(1)} %copy-done.4), channel_id=1, source_target_pairs={{0,256},{4,260},{8,264},{12,268},{16,272},{20,276},{24,280},{28,28... | collective-permute-start | bytes 294920 | tf_op jit(solution)/shard_map/ppermute | solution.py:14
  39.3 3.7 %copy-start.2 = (bf16[384,128]{1,0:T(8,128)(2,1)}, bf16[384,128]{1,0:T(8,128)(2,1)S(1)}, u32[]{:S(2)}) copy-start(bf16[384,128]{1,0:T(8,128)(2,1)S(1)} %collective-permute-done.1) | copy-start | bytes 294916
  39.3 24.0 %collective-permute-start.7 = (bf16[384,128]{0,1:T(8,128)(2,1)S(1)}, bf16[384,128]{0,1:T(8,128)(2,1)S(1)}, u32[]{:S(2)}, u32[]{:S(2)}) collective-permute-start(bf16[384,128]{0,1:T(8,128)(2,1)S(1)} %copy.179), channel_id=1, source_target_pairs={{0,4},{4,8},{8,12},{12,16},{16,20},{20,24},{24,28},{28,32},{32,36}... | collective-permute-start | bytes 294920 | tf_op jit(solution)/shard_map/ppermute | solution.py:14
  43.0 5.5 %copy-start.11 = (bf16[384,128]{1,0:T(8,128)(2,1)}, bf16[384,128]{1,0:T(8,128)(2,1)S(1)}, u32[]{:S(2)}) copy-start(bf16[384,128]{1,0:T(8,128)(2,1)S(1)} %collective-permute-done) | copy-start | bytes 294916
  43.0 23.1 %collective-permute-start.9 = (bf16[384,128]{0,1:T(8,128)(2,1)S(1)}, bf16[384,128]{0,1:T(8,128)(2,1)S(1)}, u32[]{:S(2)}, u32[]{:S(2)}) collective-permute-start(bf16[384,128]{0,1:T(8,128)(2,1)S(1)} %copy.179), channel_id=1, source_target_pairs={{0,16},{4,20},{8,24},{12,28},{16,32},{20,36},{24,40},{28,44},{32,4... | collective-permute-start | bytes 294920 | tf_op jit(solution)/shard_map/ppermute | solution.py:14
  48.5 3.3 %copy-start.9 = (bf16[384,128]{1,0:T(8,128)(2,1)}, bf16[384,128]{1,0:T(8,128)(2,1)S(1)}, u32[]{:S(2)}) copy-start(bf16[384,128]{1,0:T(8,128)(2,1)S(1)} %collective-permute-done.5) | copy-start | bytes 294916
  48.5 21.5 %collective-permute-start.10 = (bf16[384,128]{0,1:T(8,128)(2,1)S(1)}, bf16[384,128]{0,1:T(8,128)(2,1)S(1)}, u32[]{:S(2)}, u32[]{:S(2)}) collective-permute-start(bf16[384,128]{0,1:T(8,128)(2,1)S(1)} %copy.179), channel_id=1, source_target_pairs={{0,32},{4,36},{8,40},{12,44},{16,48},{20,52},{24,56},{28,60},{32,6... | collective-permute-start | bytes 294920 | tf_op jit(solution)/shard_map/ppermute | solution.py:14
  51.8 20.6 %collective-permute-start.11 = (bf16[384,128]{0,1:T(8,128)(2,1)S(1)}, bf16[384,128]{0,1:T(8,128)(2,1)S(1)}, u32[]{:S(2)}, u32[]{:S(2)}) collective-permute-start(bf16[384,128]{0,1:T(8,128)(2,1)S(1)} %copy.179), channel_id=1, source_target_pairs={{0,64},{4,68},{8,72},{12,76},{16,80},{20,84},{24,88},{28,92},{32,9... | collective-permute-start | bytes 294920 | tf_op jit(solution)/shard_map/ppermute | solution.py:14
  55.5 20.2 %collective-permute-start.12 = (bf16[384,128]{0,1:T(8,128)(2,1)S(1)}, bf16[384,128]{0,1:T(8,128)(2,1)S(1)}, u32[]{:S(2)}, u32[]{:S(2)}) collective-permute-start(bf16[384,128]{0,1:T(8,128)(2,1)S(1)} %copy.179), channel_id=1, source_target_pairs={{0,128},{4,132},{8,136},{12,140},{16,144},{20,148},{24,152},{28,15... | collective-permute-start | bytes 294920 | tf_op jit(solution)/shard_map/ppermute | solution.py:14
  61.8 1.1 copy-start.13
  63.3 12.8 %collective-permute-start.13 = (bf16[384,128]{0,1:T(8,128)(2,1)S(1)}, bf16[384,128]{0,1:T(8,128)(2,1)S(1)}, u32[]{:S(2)}, u32[]{:S(2)}) collective-permute-start(bf16[384,128]{0,1:T(8,128)(2,1)S(1)} %copy.179), channel_id=1, source_target_pairs={{0,256},{4,260},{8,264},{12,268},{16,272},{20,276},{24,280},{28,28... | collective-permute-start | bytes 294920 | tf_op jit(solution)/shard_map/ppermute | solution.py:14
  66.1 10.4 %collective-permute-start.8 = (bf16[384,128]{0,1:T(8,128)(2,1)S(1)}, bf16[384,128]{0,1:T(8,128)(2,1)S(1)}, u32[]{:S(2)}, u32[]{:S(2)}) collective-permute-start(bf16[384,128]{0,1:T(8,128)(2,1)S(1)} %copy.179), channel_id=1, source_target_pairs={{0,8},{4,12},{8,16},{12,20},{16,24},{20,28},{24,32},{28,36},{32,40... | collective-permute-start | bytes 294920 | tf_op jit(solution)/shard_map/ppermute | solution.py:14
  70.0 31.4 %collective-permute-start.21 = (f32[384,128]{1,0:T(8,128)S(1)}, f32[384,128]{1,0:T(8,128)S(1)}, u32[]{:S(2)}, u32[]{:S(2)}) collective-permute-start(f32[384,128]{1,0:T(8,128)S(1)} %convolution_bitcast_fusion.14), channel_id=1, source_target_pairs={{4,0},{8,4},{12,8},{16,12},{20,16},{24,20},{28,24},{32,28},{36,32}... | collective-permute-start | bytes 589832 | tf_op jit(solution)/shard_map/ppermute | solution.py:14
  72.4 30.3 %collective-permute-start.22 = (f32[384,128]{1,0:T(8,128)S(1)}, f32[384,128]{1,0:T(8,128)S(1)}, u32[]{:S(2)}, u32[]{:S(2)}) collective-permute-start(f32[384,128]{1,0:T(8,128)S(1)} %convolution_bitcast_fusion.13), channel_id=1, source_target_pairs={{8,0},{12,4},{16,8},{20,12},{24,16},{28,20},{32,24},{36,28},{40,32... | collective-permute-start | bytes 589832 | tf_op jit(solution)/shard_map/ppermute | solution.py:14
  82.8 0.9 copy-start.8
  82.8 1.3 copy-start.12
  83.7 0.9 copy-start.6
  84.6 0.9 copy-start.10
  85.5 0.9 copy-start.3
  87.7 19.3 %collective-permute-start.23 = (f32[384,128]{1,0:T(8,128)}, f32[384,128]{1,0:T(8,128)}, u32[]{:S(2)}, u32[]{:S(2)}) collective-permute-start(f32[384,128]{1,0:T(8,128)} %convolution_bitcast_fusion.12), channel_id=1, source_target_pairs={{16,0},{20,4},{24,8},{28,12},{32,16},{36,20},{40,24},{44,28},{48,3... | collective-permute-start | bytes 589832 | tf_op jit(solution)/shard_map/ppermute | solution.py:14
  94.3 15.7 %collective-permute-start.24 = (f32[384,128]{1,0:T(8,128)}, f32[384,128]{1,0:T(8,128)}, u32[]{:S(2)}, u32[]{:S(2)}) collective-permute-start(f32[384,128]{1,0:T(8,128)} %convolution_bitcast_fusion.11), channel_id=1, source_target_pairs={{32,0},{36,4},{40,8},{44,12},{48,16},{52,20},{56,24},{60,28},{64,3... | collective-permute-start | bytes 589832 | tf_op jit(solution)/shard_map/ppermute | solution.py:14
  98.4 14.6 %collective-permute-start.25 = (f32[384,128]{1,0:T(8,128)}, f32[384,128]{1,0:T(8,128)}, u32[]{:S(2)}, u32[]{:S(2)}) collective-permute-start(f32[384,128]{1,0:T(8,128)} %convolution_bitcast_fusion.10), channel_id=1, source_target_pairs={{64,0},{68,4},{72,8},{76,12},{80,16},{84,20},{88,24},{92,28},{96,3... | collective-permute-start | bytes 589832 | tf_op jit(solution)/shard_map/ppermute | solution.py:14
  101.4 4.5 %copy-start.14 = (f32[384,128]{1,0:T(8,128)}, f32[384,128]{1,0:T(8,128)S(1)}, u32[]{:S(2)}) copy-start(f32[384,128]{1,0:T(8,128)S(1)} %collective-permute-done.21) | copy-start | bytes 589828
  101.4 19.1 %collective-permute-start.26 = (f32[384,128]{1,0:T(8,128)}, f32[384,128]{1,0:T(8,128)}, u32[]{:S(2)}, u32[]{:S(2)}) collective-permute-start(f32[384,128]{1,0:T(8,128)} %convolution_bitcast_fusion.9), channel_id=1, source_target_pairs={{128,0},{132,4},{136,8},{140,12},{144,16},{148,20},{152,24},{156,2... | collective-permute-start | bytes 589832 | tf_op jit(solution)/shard_map/ppermute | solution.py:14
  102.7 3.2 %copy-start.15 = (f32[384,128]{1,0:T(8,128)}, f32[384,128]{1,0:T(8,128)S(1)}, u32[]{:S(2)}) copy-start(f32[384,128]{1,0:T(8,128)S(1)} %collective-permute-done.22) | copy-start | bytes 589828
  102.7 34.4 %collective-permute-start.27 = (f32[384,128]{1,0:T(8,128)}, f32[384,128]{1,0:T(8,128)}, u32[]{:S(2)}, u32[]{:S(2)}) collective-permute-start(f32[384,128]{1,0:T(8,128)} %convolution_bitcast_fusion.8), channel_id=1, source_target_pairs={{256,0},{260,4},{264,8},{268,12},{272,16},{276,20},{280,24},{284,2... | collective-permute-start | bytes 589832 | tf_op jit(solution)/shard_map/ppermute | solution.py:14
  107.0 33.8 %copy-start.1 = (f32[384,128]{1,0:T(8,128)S(1)}, f32[384,128]{1,0:T(8,128)}, u32[]{:S(2)}) copy-start(f32[384,128]{1,0:T(8,128)} %convolution_bitcast_fusion.17) | copy-start | bytes 589828
  107.0 33.7 %collective-permute-start.15 = (f32[384,128]{1,0:T(8,128)}, f32[384,128]{1,0:T(8,128)S(1)}, u32[]{:S(2)}, u32[]{:S(2)}) collective-permute-start(f32[384,128]{1,0:T(8,128)} %convolution_bitcast_fusion.21), channel_id=1, source_target_pairs={{8,0},{12,4},{16,8},{20,12},{24,16},{28,20},{32,24},{36,28},{40,32... | collective-permute-start | bytes 589832 | tf_op jit(solution)/shard_map/ppermute | solution.py:14
  110.0 32.1 %collective-permute-start.14 = (f32[384,128]{1,0:T(8,128)S(1)}, f32[384,128]{1,0:T(8,128)S(1)}, u32[]{:S(2)}, u32[]{:S(2)}) collective-permute-start(f32[384,128]{1,0:T(8,128)S(1)} %convolution_bitcast_fusion.22), channel_id=1, source_target_pairs={{4,0},{8,4},{12,8},{16,12},{20,16},{24,20},{28,24},{32,28},{36,32}... | collective-permute-start | bytes 589832 | tf_op jit(solution)/shard_map/ppermute | solution.py:14
  113.0 45.0 %collective-permute-start.16 = (f32[384,128]{1,0:T(8,128)S(1)}, f32[384,128]{1,0:T(8,128)S(1)}, u32[]{:S(2)}, u32[]{:S(2)}) collective-permute-start(f32[384,128]{1,0:T(8,128)S(1)} %convolution_bitcast_fusion.20), channel_id=1, source_target_pairs={{16,0},{20,4},{24,8},{28,12},{32,16},{36,20},{40,24},{44,28},{48,3... | collective-permute-start | bytes 589832 | tf_op jit(solution)/shard_map/ppermute | solution.py:14
  120.5 37.5 %collective-permute-start.17 = (f32[384,128]{1,0:T(8,128)}, f32[384,128]{1,0:T(8,128)S(1)}, u32[]{:S(2)}, u32[]{:S(2)}) collective-permute-start(f32[384,128]{1,0:T(8,128)} %convolution_bitcast_fusion.19), channel_id=1, source_target_pairs={{32,0},{36,4},{40,8},{44,12},{48,16},{52,20},{56,24},{60,28},{64,3... | collective-permute-start | bytes 589832 | tf_op jit(solution)/shard_map/ppermute | solution.py:14
  137.0 21.0 %collective-permute-start.18 = (f32[384,128]{1,0:T(8,128)}, f32[384,128]{1,0:T(8,128)S(1)}, u32[]{:S(2)}, u32[]{:S(2)}) collective-permute-start(f32[384,128]{1,0:T(8,128)} %convolution_bitcast_fusion.18), channel_id=1, source_target_pairs={{64,0},{68,4},{72,8},{76,12},{80,16},{84,20},{88,24},{92,28},{96,3... | collective-permute-start | bytes 589832 | tf_op jit(solution)/shard_map/ppermute | solution.py:14
  140.8 17.3 %collective-permute-start.19 = (f32[384,128]{1,0:T(8,128)S(1)}, f32[384,128]{1,0:T(8,128)S(1)}, u32[]{:S(2)}, u32[]{:S(2)}) collective-permute-start(f32[384,128]{1,0:T(8,128)S(1)} %copy-done.1), channel_id=1, source_target_pairs={{128,0},{132,4},{136,8},{140,12},{144,16},{148,20},{152,24},{156,2... | collective-permute-start | bytes 589832 | tf_op jit(solution)/shard_map/ppermute | solution.py:14
  142.1 25.5 %collective-permute-start.20 = (f32[384,128]{1,0:T(8,128)S(1)}, f32[384,128]{1,0:T(8,128)S(1)}, u32[]{:S(2)}, u32[]{:S(2)}) collective-permute-start(f32[384,128]{1,0:T(8,128)S(1)} %convolution_bitcast_fusion.16), channel_id=1, source_target_pairs={{256,0},{260,4},{264,8},{268,12},{272,16},{276,20},{280,24},{284,2... | collective-permute-start | bytes 589832 | tf_op jit(solution)/shard_map/ppermute | solution.py:14
where the time goes:
time: 184 us; the launch traced here: 183 us
  starting transfers between devices  103 us (56%)
  blocking collectives  28.2 us (15%)
  matrix products  26.7 us (15%)
  waiting for transfers between devices  9.74 us (5%)
  local copies, waits for them, and re-layouts  6.92 us (4%)
  other arithmetic  6.92 us (4%)
    ppermute x28, starting transfers between devices, passed_along(): lax.ppermute(value, axis, [(source, source + steps) for source in range(l...  103 us
    all_gather x2, blocking collectives, gathered_total(): pieces = lax.all_gather(array, axis)  28.2 us
    ppermute x28, waiting for transfers between devices, passed_along(): lax.ppermute(value, axis, [(source, source + steps) for source in range(l...  9.74 us
    dot_general x8, matrix products, backward_work(): jnp.einsum('htu,thd->ud', probs_low, grad_out, preferred_element_type=jnp...  7.92 us
    unnamed x44, local copies, waits for them, and re-layouts  5.29 us
    dot_general x8, matrix products, backward_work(): jnp.einsum('htu,thd->ud', grad_score, queries, preferred_element_type=jnp...  5.26 us
    dot_general x8, matrix products, backward_work(): jnp.einsum('thd,ud->htu', grad_out, values_here, preferred_element_type=j...  4.23 us
  transfers between devices with their start and end apart: 28, of which 3 were waited for; matrix products, arithmetic and copies ran while one was open for 21% of the time, Pallas kernels for 0%

commit v1 on v0

v1 whole, which is shorter than its diff:
```python
import functools
import math

import jax
import jax.numpy as jnp
from jax import lax
from jax.experimental import pallas as pl
from jax.experimental.pallas import tpu as pltpu
from jax.sharding import PartitionSpec as P

NEG = -1e30
AXES = ("ctx", "head")
SLOTS = 4
VMEM = pl.BlockSpec(memory_space=pltpu.VMEM)
SMEM = pl.BlockSpec(memory_space=pltpu.SMEM)
PARAMS = pltpu.CompilerParams(vmem_limit_bytes=40 * 1024 * 1024)
F32 = jnp.float32
BF16 = jnp.bfloat16

TABLES = {
    128: ((64, 8), (4, 32), (16, 2), (0, 1)),
    16: ((8, 2), (4, 1), (None, None), (0, None)),
}


def call(kernel, out_shape, in_specs, flops, moved, exps):
    outs = jax.tree.map(lambda _: VMEM, out_shape)
    return pl.pallas_call(
        kernel,
        out_shape=out_shape,
        in_specs=in_specs,
        out_specs=outs,
        compiler_params=PARAMS,
        cost_estimate=pl.CostEstimate(flops=flops, bytes_accessed=moved, transcendentals=exps),
    )


def mask_kernel(meta, lengths, pattern, bias_ref):
    rows = bias_ref.shape[2]
    block = 128
    count = rows // block
    own = meta[0]
    lane = lax.broadcasted_iota(jnp.int32, (8, rows), 1)
    sub = lax.broadcasted_iota(jnp.int32, (8, rows), 0)
    base = jnp.full((8, rows), own * rows, jnp.int32)
    for slot in range(SLOTS):
        base = jnp.where(sub == slot + 1, meta[1 + slot] * rows, base)
    pos = base + lane

    def add_doc(index, carry):
        end, total = carry
        end = end + lengths[index]
        return end, total + jnp.where(pos >= end, 1.0, 0.0)

    docs = lax.fori_loop(
        0, lengths.shape[0], add_doc, (jnp.int32(0), jnp.zeros((8, rows), F32)), unroll=8
    )[1]
    query_doc = docs[0:1]
    query_pos = pos[0:1]
    down = lax.broadcasted_iota(jnp.int32, (block, rows), 0)
    for slot in range(SLOTS):
        partner = meta[1 + slot]
        valid = meta[1 + SLOTS + slot]
        for kb in range(count):
            key_doc = docs[slot + 1 : slot + 2, kb * block : (kb + 1) * block]
            key_doc = jnp.broadcast_to(key_doc, (block, block)).T
            for qb in range(count):
                cols = slice(qb * block, (qb + 1) * block)
                same = key_doc == query_doc[:, cols]
                early = down[:, cols] + (partner * rows + kb * block) <= query_pos[:, cols]
                live = jnp.where(pattern[qb, partner * count + kb] * valid == 1, 0.0, NEG)
                bias_ref[slot, kb * block : (kb + 1) * block, cols] = (
                    jnp.where(same & early, 0.0, NEG) + live
                )


def dot(a, b, dims):
    return lax.dot_general(a, b, (dims, ((), ())), preferred_element_type=F32)


NN = ((1,), (0,))
NT = ((1,), (1,))


def head_rows(own_ref, other_ref, head, rows, which):
    half = own_ref.shape[0] // 2
    ref = own_ref if head < 2 else other_ref
    start = which * half + (head % 2) * rows
    return ref[start : start + rows, :]


def forward_kernel(slots, first, last, *refs):
    own_ref, other_ref, bias_ref = refs[:3]
    kv_refs = refs[3 : 3 + len(slots)]
    rest = refs[3 + len(slots) :]
    if first:
        stat_out, out_out = rest
    else:
        stat_in, out_in, stat_out, out_out = rest
    rows = bias_ref.shape[1]
    dim = own_ref.shape[1]
    factor = math.log2(math.e) / math.sqrt(dim)
    values_t = [kv[rows:, :].T for kv in kv_refs]
    for head in range(4):
        cols = slice(head * rows, (head + 1) * rows)
        query = head_rows(own_ref, other_ref, head, rows, 0)
        if first:
            top = jnp.full((1, rows), NEG, F32)
            total = jnp.zeros((1, rows), F32)
            out = jnp.zeros((dim, rows), F32)
        else:
            top = stat_in[0:1, cols]
            total = stat_in[1:2, cols]
            out = out_in[:, cols]
        for place, slot in enumerate(slots):
            scores = dot(kv_refs[place][:rows, :], query, NT) * factor + bias_ref[slot]
            new_top = jnp.maximum(top, jnp.max(scores, axis=0, keepdims=True))
            probs = jnp.exp2(scores - new_top)
            fade = jnp.exp2(top - new_top)
            total = total * fade + jnp.sum(probs, axis=0, keepdims=True)
            out = out * fade + dot(values_t[place], probs.astype(BF16), NN)
            top = new_top
        out_out[:, cols] = out
        stat_out[0:1, cols] = top
        stat_out[1:2, cols] = total
        if last:
            grad_t = head_rows(own_ref, other_ref, head, rows, 1).T.astype(F32)
            stat_out[2:3, cols] = jnp.sum(grad_t * out, axis=0, keepdims=True)
        else:
            stat_out[2:3, cols] = jnp.zeros((1, rows), F32)
        stat_out[3:8, cols] = jnp.zeros((5, rows), F32)


def merged(stat_ref, other_stat_ref, head, rows):
    cols = slice(head * rows, (head + 1) * rows)
    other = ((head + 2) % 4) * rows
    other_cols = slice(other, other + rows)
    top_a, top_b = stat_ref[0:1, cols], other_stat_ref[0:1, other_cols]
    top = jnp.maximum(top_a, top_b)
    fade_a, fade_b = jnp.exp2(top_a - top), jnp.exp2(top_b - top)
    total = stat_ref[1:2, cols] * fade_a + other_stat_ref[1:2, other_cols] * fade_b
    inner = stat_ref[2:3, cols] * fade_a + other_stat_ref[2:3, other_cols] * fade_b
    return top + jnp.log2(total), inner / total, fade_a, fade_b, total


def backward_kernel(slot, first, last, *refs):
    own_ref, other_ref, bias_ref, kv_ref, stat_ref, other_stat_ref = refs[:6]
    rest = refs[6:]
    rows = bias_ref.shape[1]
    dim = own_ref.shape[1]
    out_ref = None
    if last:
        out_ref, rest = rest[0], rest[1:]
    query_in = None
    if not first:
        query_in, rest = rest[0], rest[1:]
    grad_kv_ref, query_out = rest[:2]
    factor = math.log2(math.e) / math.sqrt(dim)
    scale = 1.0 / math.sqrt(dim)
    key = kv_ref[:rows, :]
    value = kv_ref[rows:, :]
    key_t = key.T
    grad_key = jnp.zeros((rows, dim), F32)
    grad_value = jnp.zeros((rows, dim), F32)
    for head in range(4):
        cols = slice(head * rows, (head + 1) * rows)
        query = head_rows(own_ref, other_ref, head, rows, 0)
        grad = head_rows(own_ref, other_ref, head, rows, 1)
        norm, inner, _, _, _ = merged(stat_ref, other_stat_ref, head, rows)
        scores = dot(key, query, NT) * factor + bias_ref[slot]
        probs = jnp.exp2(scores - norm)
        grad_value = grad_value + dot(probs.astype(BF16), grad, NN)
        grad_score = (probs * (dot(value, grad, NT) - inner)).astype(BF16)
        grad_key = grad_key + dot(grad_score, query, NN)
        part = dot(key_t, grad_score, NN) * scale
        if not first:
            part = query_in[:, cols] + part
        query_out[:, cols] = part
        if last and head >= 2:
            send_ref = rest[2]
            there = slice((head - 2) * rows, (head - 1) * rows)
            send_ref[:dim, there] = (out_ref[:, cols] / stat_ref[1:2, cols]).astype(BF16)
            send_ref[dim:, there] = part.astype(BF16)
    grad_kv_ref[:rows, :] = (grad_key * scale).astype(BF16)
    grad_kv_ref[rows:, :] = grad_value.astype(BF16)


def finish_kernel(stat_ref, other_stat_ref, out_ref, query_ref, got_ref, attn_ref, grad_ref):
    rows = attn_ref.shape[0] // 2
    dim = attn_ref.shape[1]
    for head in range(2):
        cols = slice(head * rows, (head + 1) * rows)
        _, _, fade_a, fade_b, total = merged(stat_ref, other_stat_ref, head, rows)
        other = slice((head + 2) * rows, (head + 3) * rows)
        weight_b = fade_b * other_stat_ref[1:2, other] / total
        out = out_ref[:, cols] * (fade_a / total) + got_ref[:dim, cols].astype(F32) * weight_b
        attn_ref[cols, :] = out.T.astype(BF16)
        grad = query_ref[:, cols] + got_ref[dim:, cols].astype(F32)
        grad_ref[cols, :] = grad.T.astype(BF16)


def local(queries, key_rows, value_rows, grad_out, doc_lengths, block_pattern):
    rows, heads, dim = queries.shape
    width = lax.axis_size("ctx")
    lanes = lax.axis_size("head")
    table = TABLES[width]
    edge = width * 3 // 4
    own = lax.axis_index("ctx")
    lane = lax.axis_index("head") % 2

    def lane_pairs(shifts, back):
        pairs = []
        for which, shift in enumerate(shifts):
            if not shift:
                continue
            for source in range(width - shift):
                target = source + shift
                if (source < edge) != (target < edge):
                    continue
                for place in range(which, lanes, 2):
                    pair = (source * lanes + place, target * lanes + place)
                    pairs.append(pair[::-1] if back else pair)
        return pairs

    def swap_pairs(partner):
        return [
            (group * lanes + place, group * lanes + partner(place))
            for group in range(width)
            for place in range(lanes)
        ]

    near = swap_pairs(lambda place: place ^ 1)
    far = swap_pairs(lambda place: lanes - 1 - place)

    own_kv = jnp.concatenate([key_rows, value_rows], axis=0)
    sent = [bool([s for s in shifts if s]) for shifts in table]
    held = []
    held.append(lax.ppermute(own_kv, AXES, lane_pairs(table[0], False)))
    own_qg = jnp.concatenate(
        [
            queries.transpose(1, 0, 2).reshape(heads * rows, dim),
            grad_out.transpose(1, 0, 2).reshape(heads * rows, dim),
        ],
        axis=0,
    )
    other_qg = lax.ppermute(own_qg, AXES, near)
    for slot in range(1, SLOTS):
        if sent[slot]:
            got = lax.ppermute(own_kv, AXES, lane_pairs(table[slot], False))
        else:
            got = own_kv
        if table[slot][0] == 0:
            got = jnp.where(lane == 0, own_kv, got)
        held.append(got)

    shift = jnp.array([[0 if s is None else s for s in pair] for pair in table], jnp.int32)
    exists = jnp.array([[0 if s is None else 1 for s in pair] for pair in table], jnp.int32)
    partner = own - shift[:, lane]
    valid = exists[:, lane] * (partner >= 0)
    meta = jnp.concatenate(
        [jnp.reshape(own, (1,)), jnp.maximum(partner, 0), valid.astype(jnp.int32)]
    ).astype(jnp.int32)
    bias = call(
        mask_kernel,
        jax.ShapeDtypeStruct((SLOTS, rows, rows), F32),
        [SMEM, SMEM, SMEM],
        0,
        SLOTS * rows * rows * 4,
        0,
    )(meta, doc_lengths, block_pattern)

    columns = 4 * rows
    stat_shape = jax.ShapeDtypeStruct((8, columns), F32)
    wide_shape = jax.ShapeDtypeStruct((dim, columns), F32)
    unit = 2 * rows * columns * dim

    def forward(slots, carry, last):
        first = carry is None
        kernel = functools.partial(forward_kernel, slots, first, last)
        args = [own_qg, other_qg, bias] + [held[s] for s in slots] + list(carry or ())
        return call(
            kernel,
            (stat_shape, wide_shape),
            [VMEM] * len(args),
            2 * unit * len(slots),
            4 << 20,
            rows * columns * len(slots),
        )(*args)

    stat, out = forward((0, 1), None, False)
    stat, out = forward((2, 3), (stat, out), True)
    other_stat = lax.ppermute(stat, AXES, near)

    kv_shape = jax.ShapeDtypeStruct((2 * rows, dim), BF16)
    send_shape = jax.ShapeDtypeStruct((2 * dim, 2 * rows), BF16)
    returned = []
    query_grad = None
    for slot in range(SLOTS):
        first, last = slot == 0, slot == SLOTS - 1
        kernel = functools.partial(backward_kernel, slot, first, last)
        args = [own_qg, other_qg, bias, held[slot], stat, other_stat]
        if last:
            args.append(out)
        if not first:
            args.append(query_grad)
        shapes = (kv_shape, wide_shape) + ((send_shape,) if last else ())
        results = call(
            kernel, shapes, [VMEM] * len(args), 5 * unit, 4 << 20, rows * columns
        )(*args)
        grad_kv, query_grad = results[:2]
        if sent[slot]:
            back = lax.ppermute(grad_kv, AXES, lane_pairs(table[slot], True))
        else:
            back = jnp.zeros_like(grad_kv)
        if table[slot][0] == 0:
            back = jnp.where(lane == 0, grad_kv, back)
        returned.append(back)
    got = lax.ppermute(results[2], AXES, near)
    total = sum(back.astype(F32) for back in returned).astype(BF16)
    total = (total.astype(F32) + lax.ppermute(total, AXES, near).astype(F32)).astype(BF16)
    total = (total.astype(F32) + lax.ppermute(total, AXES, far).astype(F32)).astype(BF16)

    flat = jax.ShapeDtypeStruct((heads * rows, dim), BF16)
    attn, grad_q = call(
        finish_kernel, (flat, flat), [VMEM] * 5, 0, 2 << 20, 0
    )(stat, other_stat, out, query_grad, got)

    def by_token(array):
        return array.reshape(heads, rows, dim).transpose(1, 0, 2)

    return by_token(attn), by_token(grad_q), total[:rows], total[rows:]


def solution(mesh):
    wide, flat = P("ctx", "head", None), P("ctx", None)
    return jax.shard_map(
        local,
        mesh=mesh,
        in_specs=(wide, flat, flat, wide, P(), flat),
        out_specs=(wide, wide, flat, flat),
        check_vma=False,
    )
```

time: 184 us -> 106 us (0.58)
  the two profiles are of different devices: /device:TPU:88 before, /device:TPU:126 now
where the time goes in v1:
time: 106 us; the launch traced here: 105 us
  waiting for transfers between devices  40.7 us (38%)
  starting transfers between devices  39.7 us (37%)
  Pallas kernels  16.2 us (15%)
  local copies, waits for them, and re-layouts  6.9 us (7%)
  other arithmetic  1.06 us (1%)
    ppermute x4, waiting for transfers between devices, local(): back = lax.ppermute(grad_kv, AXES, lane_pairs(table[slot], True))  19.7 us
    ppermute x3, starting transfers between devices, local(): got = lax.ppermute(own_kv, AXES, lane_pairs(table[slot], False))  12.7 us
    pallas_call x4, Pallas kernels, local(): call(kernel, shapes, [VMEM] * len(args), 5 * unit, 4 << 20, rows * columns)  8.43 us
    ppermute x1, waiting for transfers between devices, local(): other_qg = lax.ppermute(own_qg, AXES, near)  8.04 us
    ppermute x1, starting transfers between devices, local(): held.append(lax.ppermute(own_kv, AXES, lane_pairs(table[0], False)))  7.73 us
    ppermute x4, starting transfers between devices, local(): back = lax.ppermute(grad_kv, AXES, lane_pairs(table[slot], True))  7.19 us
    pallas_call x2, Pallas kernels, forward(): call(kernel, (stat_shape, wide_shape), [VMEM] * len(args), 2 * unit * len...  6.3 us
    ppermute x1, waiting for transfers between devices, local(): got = lax.ppermute(results[2], AXES, near)  5.29 us
  transfers between devices with their start and end apart: 13, of which 7 were waited for; matrix products, arithmetic and copies ran while one was open for 4% of the time, Pallas kernels for 4%

profile of v1, /device:TPU:126, one launch (start us, length us, event | category | flops | bytes accessed | tf_op | source)
XLA Modules:
  0.0 105.4 jit_solution(15046700732660643035)
XLA Ops:
  0.6 0.9 constant_dynamic-update-slice_fusion.1
  1.5 0.9 constant_dynamic-update-slice_fusion
  2.4 6.1 %collective-permute-start.4 = (bf16[768,128]{1,0:T(8,128)(2,1)S(1)}, bf16[768,128]{1,0:T(8,128)(2,1)S(1)}, u32[]{:S(2)}, u32[]{:S(2)}) collective-permute-start(bf16[768,128]{1,0:T(8,128)(2,1)S(1)} %constant_dynamic-update-slice_fusion), channel_id=1, source_target_pairs={{0,16},{2,18},{4,20},{6,22},{8,24},{10,26},{12,28},{14,30},{16,32}... | collective-permute-start | bytes 589832 | tf_op jit(solution)/shard_map/ppermute | solution.py:249
  8.5 7.7 %collective-permute-start.3 = (bf16[768,128]{1,0:T(8,128)(2,1)S(1)}, bf16[768,128]{1,0:T(8,128)(2,1)S(1)}, u32[]{:S(2)}, u32[]{:S(2)}) collective-permute-start(bf16[768,128]{1,0:T(8,128)(2,1)S(1)} %constant_dynamic-update-slice_fusion), channel_id=1, source_target_pairs={{0,256},{2,258},{4,260},{6,262},{8,264},{10,266},{12,268},{14,270}... | collective-permute-start | bytes 589832 | tf_op jit(solution)/shard_map/ppermute | solution.py:238
  16.3 1.9 %collective-permute-start.2 = (bf16[768,128]{1,0:T(8,128)(2,1)S(1)}, bf16[768,128]{1,0:T(8,128)(2,1)S(1)}, u32[]{:S(2)}, u32[]{:S(2)}) collective-permute-start(bf16[768,128]{1,0:T(8,128)(2,1)S(1)} %constant_dynamic-update-slice_fusion), channel_id=1, source_target_pairs={{1,5},{3,7},{5,9},{7,11},{9,13},{11,15},{13,17},{15,19},{17,21},{1... | collective-permute-start | bytes 589832 | tf_op jit(solution)/shard_map/ppermute | solution.py:249
  18.2 4.7 %collective-permute-start.1 = (bf16[768,128]{1,0:T(8,128)(2,1)S(1)}, bf16[768,128]{1,0:T(8,128)(2,1)S(1)}, u32[]{:S(2)}, u32[]{:S(2)}) collective-permute-start(bf16[768,128]{1,0:T(8,128)(2,1)S(1)} %constant_dynamic-update-slice_fusion), channel_id=1, source_target_pairs={{0,64},{2,66},{4,68},{6,70},{8,72},{10,74},{12,76},{14,78},{16,80}... | collective-permute-start | bytes 589832 | tf_op jit(solution)/shard_map/ppermute | solution.py:249
  22.9 1.0 copy.12
  23.9 1.0 copy.13
  24.9 1.9 %collective-permute-start = (bf16[1536,128]{1,0:T(8,128)(2,1)S(1)}, bf16[1536,128]{1,0:T(8,128)(2,1)S(1)}, u32[]{:S(2)}, u32[]{:S(2)}) collective-permute-start(bf16[1536,128]{1,0:T(8,128)(2,1)S(1)} %pad_maximum_fusion.refs_0_), channel_id=1, source_target_pairs={{0,1},{1,0},{2,3},{3,2},{4,5},{5,4},{6,7},{7,6},{8,9},{9,8},{10,11... | collective-permute-start | bytes 1179656 | tf_op jit(solution)/shard_map/ppermute | solution.py:246
  26.8 0.7 maximum_bitcast_fusion
  27.5 0.1 pad_add_fusion.meta
  27.6 0.0 copy-start
  27.6 0.7 copy-done
  28.3 0.7 copy-done.1
  28.9 1.2 %shard_map.111.refs_2_ = f32[4,384,384]{2,1,0:T(8,128)S(1)} custom-call(s32[9]{0:T(128)S(1)} %pad_add_fusion.meta, s32[64]{0:T(128)S(1)} %copy-done.1, s32[3,384]{1,0:T(4,128)S(1)} %copy-done), custom_call_target="tpu_custom_call" | custom-call | bytes 2359296 | tf_op jit(solution)/shard_map/pallas_call | solution.py:263
  30.2 0.0 collective-permute-done.2
  30.2 0.0 collective-permute-done.4.refs_4_.refs_3_
  30.2 0.0 collective-permute-done.3.refs_3_
  30.2 8.0 %collective-permute-done.refs_1_ = bf16[1536,128]{1,0:T(8,128)(2,1)S(1)} collective-permute-done((bf16[1536,128]{1,0:T(8,128)(2,1)S(1)}, bf16[1536,128]{1,0:T(8,128)(2,1)S(1)}, u32[]{:S(2)}, u32[]{:S(2)}) %collective-permute-start) | collective-permute-done | bytes 393248 | tf_op jit(solution)/shard_map/ppermute | solution.py:246
  38.3 3.1 %shard_map.112 = (f32[8,1536]{1,0:T(8,128)S(1)}, f32[128,1536]{1,0:T(8,128)S(1)}) custom-call(bf16[1536,128]{1,0:T(8,128)(2,1)S(1)} %pad_maximum_fusion.refs_0_, bf16[1536,128]{1,0:T(8,128)(2,1)S(1)} %collective-permute-done.refs_1_, f32[4,384,384]{2,1,0:T(8,128)S(1)} %shard_map.111.refs_2_, bf16[768,128]{1,0:T(8,128)(2,1)S(1)} %collective-permute-done.3.refs_3_, ...), custom_call_target="tpu_custom_call" | custom-call | flops 603979776 | bytes 4194304 | tf_op jit(solution)/shard_map/pallas_call | solution.py:281
  41.4 0.0 collective-permute-done.1.refs_3_
  41.4 3.2 %shard_map.113 = (f32[8,1536]{1,0:T(8,128)S(1)}, f32[128,1536]{1,0:T(8,128)S(1)}) custom-call(bf16[1536,128]{1,0:T(8,128)(2,1)S(1)} %pad_maximum_fusion.refs_0_, bf16[1536,128]{1,0:T(8,128)(2,1)S(1)} %collective-permute-done.refs_1_, f32[4,384,384]{2,1,0:T(8,128)S(1)} %shard_map.111.refs_2_, bf16[768,128]{1,0:T(8,128)(2,1)S(1)} %collective-permute-done.1.refs_3_, ...), custom_call_target="tpu_custom_call" | custom-call | flops 603979776 | bytes 4194304 | tf_op jit(solution)/shard_map/pallas_call | solution.py:281
  44.6 2.4 %collective-permute-start.5 = (f32[8,1536]{1,0:T(8,128)S(1)}, f32[8,1536]{1,0:T(8,128)S(1)}, u32[]{:S(2)}, u32[]{:S(2)}) collective-permute-start(f32[8,1536]{1,0:T(8,128)S(1)} %get-tuple-element.21.refs_4_.stat_ref), channel_id=1, source_target_pairs={{0,1},{1,0},{2,3},{3,2},{4,5},{5,4},{6,7},{7,6},{8,9},{9,8},{10,11... | collective-permute-start | bytes 147464 | tf_op jit(solution)/shard_map/ppermute | solution.py:292
  47.0 3.6 %collective-permute-done.5.refs_5_.other_stat_ref = f32[8,1536]{1,0:T(8,128)S(1)} collective-permute-done((f32[8,1536]{1,0:T(8,128)S(1)}, f32[8,1536]{1,0:T(8,128)S(1)}, u32[]{:S(2)}, u32[]{:S(2)}) %collective-permute-start.5) | collective-permute-done | bytes 49184 | tf_op jit(solution)/shard_map/ppermute | solution.py:292
  50.6 2.1 %shard_map.114 = (bf16[768,128]{1,0:T(8,128)(2,1)S(1)}, f32[128,1536]{1,0:T(8,128)S(1)}) custom-call(bf16[1536,128]{1,0:T(8,128)(2,1)S(1)} %pad_maximum_fusion.refs_0_, bf16[1536,128]{1,0:T(8,128)(2,1)S(1)} %collective-permute-done.refs_1_, f32[4,384,384]{2,1,0:T(8,128)S(1)} %shard_map.111.refs_2_, bf16[768,128]{1,0:T(8,128)(2,1)S(1)} %collective-permute-done.3.refs_3_, ...), custom_call_target="tpu_custom_call" | custom-call | flops 754974720 | bytes 4194304 | tf_op jit(solution)/shard_map/pallas_call | solution.py:307
  52.7 2.1 %shard_map.115 = (bf16[768,128]{1,0:T(8,128)(2,1)S(1)}, f32[128,1536]{1,0:T(8,128)S(1)}) custom-call(bf16[1536,128]{1,0:T(8,128)(2,1)S(1)} %pad_maximum_fusion.refs_0_, bf16[1536,128]{1,0:T(8,128)(2,1)S(1)} %collective-permute-done.refs_1_, f32[4,384,384]{2,1,0:T(8,128)S(1)} %shard_map.111.refs_2_, ...), custom_call_target="tpu_custom_call" | custom-call | flops 754974720 | bytes 4194304 | tf_op jit(solution)/shard_map/pallas_call | solution.py:307
  54.8 2.1 %shard_map.116 = (bf16[768,128]{1,0:T(8,128)(2,1)S(1)}, f32[128,1536]{1,0:T(8,128)S(1)}) custom-call(bf16[1536,128]{1,0:T(8,128)(2,1)S(1)} %pad_maximum_fusion.refs_0_, bf16[1536,128]{1,0:T(8,128)(2,1)S(1)} %collective-permute-done.refs_1_, f32[4,384,384]{2,1,0:T(8,128)S(1)} %shard_map.111.refs_2_, bf16[768,128]{1,0:T(8,128)(2,1)S(1)} %collective-permute-done.1.refs_3_, ...), custom_call_target="tpu_custom_call" | custom-call | flops 754974720 | bytes 4194304 | tf_op jit(solution)/shard_map/pallas_call | solution.py:307
  56.9 2.1 %shard_map.117 = (bf16[768,128]{1,0:T(8,128)(2,1)S(1)}, f32[128,1536]{1,0:T(8,128)S(1)}, bf16[256,768]{1,0:T(8,128)(2,1)S(1)}) custom-call(bf16[1536,128]{1,0:T(8,128)(2,1)S(1)} %pad_maximum_fusion.refs_0_, bf16[1536,128]{1,0:T(8,128)(2,1)S(1)} %collective-permute-done.refs_1_, f32[4,384,384]{2,1,0:T(8,128)S(1)} %shard_map.111.refs_2_, ...), custom_call_target="tpu_custom_call" | custom-call | flops 754974720 | bytes 4194304 | tf_op jit(solution)/shard_map/pallas_call | solution.py:307
  59.0 1.9 %collective-permute-start.10 = (bf16[768,128]{1,0:T(8,128)(2,1)S(1)}, bf16[768,128]{1,0:T(8,128)(2,1)S(1)}, u32[]{:S(2)}, u32[]{:S(2)}) collective-permute-start(bf16[768,128]{1,0:T(8,128)(2,1)S(1)} %get-tuple-element.33), channel_id=1, source_target_pairs={{5,1},{7,3},{9,5},{11,7},{13,9},{15,11},{17,13},{19,15},{21,17},{2... | collective-permute-start | bytes 589832 | tf_op jit(solution)/shard_map/ppermute | solution.py:312
  61.0 1.9 %collective-permute-start.9 = (bf16[768,128]{1,0:T(8,128)(2,1)S(1)}, bf16[768,128]{1,0:T(8,128)(2,1)S(1)}, u32[]{:S(2)}, u32[]{:S(2)}) collective-permute-start(bf16[768,128]{1,0:T(8,128)(2,1)S(1)} %get-tuple-element.32), channel_id=1, source_target_pairs={{64,0},{66,2},{68,4},{70,6},{72,8},{74,10},{76,12},{78,14},{80,16}... | collective-permute-start | bytes 589832 | tf_op jit(solution)/shard_map/ppermute | solution.py:312
  62.9 1.3 %collective-permute-start.8 = (bf16[768,128]{1,0:T(8,128)(2,1)S(1)}, bf16[768,128]{1,0:T(8,128)(2,1)S(1)}, u32[]{:S(2)}, u32[]{:S(2)}) collective-permute-start(bf16[768,128]{1,0:T(8,128)(2,1)S(1)} %get-tuple-element.31), channel_id=1, source_target_pairs={{16,0},{18,2},{20,4},{22,6},{24,8},{26,10},{28,12},{30,14},{32,16}... | collective-permute-start | bytes 589832 | tf_op jit(solution)/shard_map/ppermute | solution.py:312
  64.2 2.1 %collective-permute-start.7 = (bf16[768,128]{1,0:T(8,128)(2,1)S(1)}, bf16[768,128]{1,0:T(8,128)(2,1)S(1)}, u32[]{:S(2)}, u32[]{:S(2)}) collective-permute-start(bf16[768,128]{1,0:T(8,128)(2,1)S(1)} %get-tuple-element.30), channel_id=1, source_target_pairs={{256,0},{258,2},{260,4},{262,6},{264,8},{266,10},{268,12},{270,14}... | collective-permute-start | bytes 589832 | tf_op jit(solution)/shard_map/ppermute | solution.py:312
  66.3 0.0 collective-permute-done.10
  66.3 12.2 %collective-permute-done.9 = bf16[768,128]{1,0:T(8,128)(2,1)S(1)} collective-permute-done((bf16[768,128]{1,0:T(8,128)(2,1)S(1)}, bf16[768,128]{1,0:T(8,128)(2,1)S(1)}, u32[]{:S(2)}, u32[]{:S(2)}) %collective-permute-start.9) | collective-permute-done | bytes 196640 | tf_op jit(solution)/shard_map/ppermute | solution.py:312
  78.5 7.5 %collective-permute-done.8 = bf16[768,128]{1,0:T(8,128)(2,1)S(1)} collective-permute-done((bf16[768,128]{1,0:T(8,128)(2,1)S(1)}, bf16[768,128]{1,0:T(8,128)(2,1)S(1)}, u32[]{:S(2)}, u32[]{:S(2)}) %collective-permute-start.8) | collective-permute-done | bytes 196640 | tf_op jit(solution)/shard_map/ppermute | solution.py:312
  86.0 0.0 collective-permute-done.7
  86.0 0.1 add_convert_fusion.2
  86.1 1.9 %collective-permute-start.11 = (bf16[768,128]{1,0:T(8,128)(2,1)S(1)}, bf16[768,128]{1,0:T(8,128)(2,1)S(1)}, u32[]{:S(2)}, u32[]{:S(2)}) collective-permute-start(bf16[768,128]{1,0:T(8,128)(2,1)S(1)} %add_convert_fusion.2), channel_id=1, source_target_pairs={{0,1},{1,0},{2,3},{3,2},{4,5},{5,4},{6,7},{7,6},{8,9},{9,8},{10,11... | collective-permute-start | bytes 589832 | tf_op jit(solution)/shard_map/ppermute | solution.py:320
  88.1 3.9 %collective-permute-start.6 = (bf16[256,768]{1,0:T(8,128)(2,1)S(1)}, bf16[256,768]{1,0:T(8,128)(2,1)S(1)}, u32[]{:S(2)}, u32[]{:S(2)}) collective-permute-start(bf16[256,768]{1,0:T(8,128)(2,1)S(1)} %get-tuple-element.27), channel_id=1, source_target_pairs={{0,1},{1,0},{2,3},{3,2},{4,5},{5,4},{6,7},{7,6},{8,9},{9,8},{10,11... | collective-permute-start | bytes 1179656 | tf_op jit(solution)/shard_map/ppermute | solution.py:318
  92.0 3.8 %collective-permute-done.11 = bf16[768,128]{1,0:T(8,128)(2,1)S(1)} collective-permute-done((bf16[768,128]{1,0:T(8,128)(2,1)S(1)}, bf16[768,128]{1,0:T(8,128)(2,1)S(1)}, u32[]{:S(2)}, u32[]{:S(2)}) %collective-permute-start.11) | collective-permute-done | bytes 196640 | tf_op jit(solution)/shard_map/ppermute | solution.py:320
  95.8 0.1 add_convert_fusion.1
  95.9 1.9 %collective-permute-start.12 = (bf16[768,128]{1,0:T(8,128)(2,1)S(1)}, bf16[768,128]{1,0:T(8,128)(2,1)S(1)}, u32[]{:S(2)}, u32[]{:S(2)}) collective-permute-start(bf16[768,128]{1,0:T(8,128)(2,1)S(1)} %add_convert_fusion.1), channel_id=1, source_target_pairs={{0,3},{1,2},{2,1},{3,0},{4,7},{5,6},{6,5},{7,4},{8,11},{9,10},{10,... | collective-permute-start | bytes 589832 | tf_op jit(solution)/shard_map/ppermute | solution.py:321
  97.8 5.3 %collective-permute-done.6.got_ref = bf16[256,768]{1,0:T(8,128)(2,1)S(1)} collective-permute-done((bf16[256,768]{1,0:T(8,128)(2,1)S(1)}, bf16[256,768]{1,0:T(8,128)(2,1)S(1)}, u32[]{:S(2)}, u32[]{:S(2)}) %collective-permute-start.6) | collective-permute-done | bytes 393248 | tf_op jit(solution)/shard_map/ppermute | solution.py:318
  103.1 0.2 shard_map.118
  103.3 1.1 %copy_bitcast_fusion = (bf16[384,2,128]{2,1,0:T(2,128)(2,1)}, bf16[384,2,128]{2,1,0:T(2,128)(2,1)}) fusion(bf16[2,384,128]{2,1,0:T(8,128)(2,1)S(1)} %bitcast.16, bf16[2,384,128]{2,1,0:T(8,128)(2,1)S(1)} %bitcast.15), kind=kLoop, calls=%fused_computation.4 | loop fusion | bytes 786432 | tf_op jit(solution)/shard_map/transpose | solution.py:329
  104.4 0.2 collective-permute-done.12
  104.6 0.1 add_convert_fusion
  104.7 0.7 fusion.1
  (3 shorter events, 0.1 us)
Async XLA Ops:
  2.4 27.8 %collective-permute-start.4 = (bf16[768,128]{1,0:T(8,128)(2,1)S(1)}, bf16[768,128]{1,0:T(8,128)(2,1)S(1)}, u32[]{:S(2)}, u32[]{:S(2)}) collective-permute-start(bf16[768,128]{1,0:T(8,128)(2,1)S(1)} %constant_dynamic-update-slice_fusion), channel_id=1, source_target_pairs={{0,16},{2,18},{4,20},{6,22},{8,24},{10,26},{12,28},{14,30},{16,32}... | collective-permute-start | bytes 589832 | tf_op jit(solution)/shard_map/ppermute | solution.py:249
  8.5 21.7 %collective-permute-start.3 = (bf16[768,128]{1,0:T(8,128)(2,1)S(1)}, bf16[768,128]{1,0:T(8,128)(2,1)S(1)}, u32[]{:S(2)}, u32[]{:S(2)}) collective-permute-start(bf16[768,128]{1,0:T(8,128)(2,1)S(1)} %constant_dynamic-update-slice_fusion), channel_id=1, source_target_pairs={{0,256},{2,258},{4,260},{6,262},{8,264},{10,266},{12,268},{14,270}... | collective-permute-start | bytes 589832 | tf_op jit(solution)/shard_map/ppermute | solution.py:238
  16.3 13.9 %collective-permute-start.2 = (bf16[768,128]{1,0:T(8,128)(2,1)S(1)}, bf16[768,128]{1,0:T(8,128)(2,1)S(1)}, u32[]{:S(2)}, u32[]{:S(2)}) collective-permute-start(bf16[768,128]{1,0:T(8,128)(2,1)S(1)} %constant_dynamic-update-slice_fusion), channel_id=1, source_target_pairs={{1,5},{3,7},{5,9},{7,11},{9,13},{11,15},{13,17},{15,19},{17,21},{1... | collective-permute-start | bytes 589832 | tf_op jit(solution)/shard_map/ppermute | solution.py:249
  18.2 23.2 %collective-permute-start.1 = (bf16[768,128]{1,0:T(8,128)(2,1)S(1)}, bf16[768,128]{1,0:T(8,128)(2,1)S(1)}, u32[]{:S(2)}, u32[]{:S(2)}) collective-permute-start(bf16[768,128]{1,0:T(8,128)(2,1)S(1)} %constant_dynamic-update-slice_fusion), channel_id=1, source_target_pairs={{0,64},{2,66},{4,68},{6,70},{8,72},{10,74},{12,76},{14,78},{16,80}... | collective-permute-start | bytes 589832 | tf_op jit(solution)/shard_map/ppermute | solution.py:249
  24.9 13.4 %collective-permute-start = (bf16[1536,128]{1,0:T(8,128)(2,1)S(1)}, bf16[1536,128]{1,0:T(8,128)(2,1)S(1)}, u32[]{:S(2)}, u32[]{:S(2)}) collective-permute-start(bf16[1536,128]{1,0:T(8,128)(2,1)S(1)} %pad_maximum_fusion.refs_0_), channel_id=1, source_target_pairs={{0,1},{1,0},{2,3},{3,2},{4,5},{5,4},{6,7},{7,6},{8,9},{9,8},{10,11... | collective-permute-start | bytes 1179656 | tf_op jit(solution)/shard_map/ppermute | solution.py:246
  27.6 0.7 copy-start
  28.3 0.7 copy-start.1
  44.6 6.0 %collective-permute-start.5 = (f32[8,1536]{1,0:T(8,128)S(1)}, f32[8,1536]{1,0:T(8,128)S(1)}, u32[]{:S(2)}, u32[]{:S(2)}) collective-permute-start(f32[8,1536]{1,0:T(8,128)S(1)} %get-tuple-element.21.refs_4_.stat_ref), channel_id=1, source_target_pairs={{0,1},{1,0},{2,3},{3,2},{4,5},{5,4},{6,7},{7,6},{8,9},{9,8},{10,11... | collective-permute-start | bytes 147464 | tf_op jit(solution)/shard_map/ppermute | solution.py:292
  59.0 7.2 %collective-permute-start.10 = (bf16[768,128]{1,0:T(8,128)(2,1)S(1)}, bf16[768,128]{1,0:T(8,128)(2,1)S(1)}, u32[]{:S(2)}, u32[]{:S(2)}) collective-permute-start(bf16[768,128]{1,0:T(8,128)(2,1)S(1)} %get-tuple-element.33), channel_id=1, source_target_pairs={{5,1},{7,3},{9,5},{11,7},{13,9},{15,11},{17,13},{19,15},{21,17},{2... | collective-permute-start | bytes 589832 | tf_op jit(solution)/shard_map/ppermute | solution.py:312
  61.0 17.5 %collective-permute-start.9 = (bf16[768,128]{1,0:T(8,128)(2,1)S(1)}, bf16[768,128]{1,0:T(8,128)(2,1)S(1)}, u32[]{:S(2)}, u32[]{:S(2)}) collective-permute-start(bf16[768,128]{1,0:T(8,128)(2,1)S(1)} %get-tuple-element.32), channel_id=1, source_target_pairs={{64,0},{66,2},{68,4},{70,6},{72,8},{74,10},{76,12},{78,14},{80,16}... | collective-permute-start | bytes 589832 | tf_op jit(solution)/shard_map/ppermute | solution.py:312
  62.9 23.1 %collective-permute-start.8 = (bf16[768,128]{1,0:T(8,128)(2,1)S(1)}, bf16[768,128]{1,0:T(8,128)(2,1)S(1)}, u32[]{:S(2)}, u32[]{:S(2)}) collective-permute-start(bf16[768,128]{1,0:T(8,128)(2,1)S(1)} %get-tuple-element.31), channel_id=1, source_target_pairs={{16,0},{18,2},{20,4},{22,6},{24,8},{26,10},{28,12},{30,14},{32,16}... | collective-permute-start | bytes 589832 | tf_op jit(solution)/shard_map/ppermute | solution.py:312
  64.2 21.8 %collective-permute-start.7 = (bf16[768,128]{1,0:T(8,128)(2,1)S(1)}, bf16[768,128]{1,0:T(8,128)(2,1)S(1)}, u32[]{:S(2)}, u32[]{:S(2)}) collective-permute-start(bf16[768,128]{1,0:T(8,128)(2,1)S(1)} %get-tuple-element.30), channel_id=1, source_target_pairs={{256,0},{258,2},{260,4},{262,6},{264,8},{266,10},{268,12},{270,14}... | collective-permute-start | bytes 589832 | tf_op jit(solution)/shard_map/ppermute | solution.py:312
  86.1 9.7 %collective-permute-start.11 = (bf16[768,128]{1,0:T(8,128)(2,1)S(1)}, bf16[768,128]{1,0:T(8,128)(2,1)S(1)}, u32[]{:S(2)}, u32[]{:S(2)}) collective-permute-start(bf16[768,128]{1,0:T(8,128)(2,1)S(1)} %add_convert_fusion.2), channel_id=1, source_target_pairs={{0,1},{1,0},{2,3},{3,2},{4,5},{5,4},{6,7},{7,6},{8,9},{9,8},{10,11... | collective-permute-start | bytes 589832 | tf_op jit(solution)/shard_map/ppermute | solution.py:320
  88.1 15.0 %collective-permute-start.6 = (bf16[256,768]{1,0:T(8,128)(2,1)S(1)}, bf16[256,768]{1,0:T(8,128)(2,1)S(1)}, u32[]{:S(2)}, u32[]{:S(2)}) collective-permute-start(bf16[256,768]{1,0:T(8,128)(2,1)S(1)} %get-tuple-element.27), channel_id=1, source_target_pairs={{0,1},{1,0},{2,3},{3,2},{4,5},{5,4},{6,7},{7,6},{8,9},{9,8},{10,11... | collective-permute-start | bytes 1179656 | tf_op jit(solution)/shard_map/ppermute | solution.py:318
  95.9 8.8 %collective-permute-start.12 = (bf16[768,128]{1,0:T(8,128)(2,1)S(1)}, bf16[768,128]{1,0:T(8,128)(2,1)S(1)}, u32[]{:S(2)}, u32[]{:S(2)}) collective-permute-start(bf16[768,128]{1,0:T(8,128)(2,1)S(1)} %add_convert_fusion.1), channel_id=1, source_target_pairs={{0,3},{1,2},{2,1},{3,0},{4,7},{5,6},{6,5},{7,4},{8,11},{9,10},{10,... | collective-permute-start | bytes 589832 | tf_op jit(solution)/shard_map/ppermute | solution.py:321

commit v2 on v1

v2 whole, which is shorter than its diff:
```python
import functools
import math

import jax
import jax.numpy as jnp
from jax import lax
from jax.experimental import pallas as pl
from jax.experimental.pallas import tpu as pltpu
from jax.sharding import PartitionSpec as P

NEG = -1e30
AXES = ("ctx", "head")
SLOTS = 4
VMEM = pl.BlockSpec(memory_space=pltpu.VMEM)
HBM = pl.BlockSpec(memory_space=pltpu.HBM)
PARAMS = pltpu.CompilerParams(vmem_limit_bytes=40 * 1024 * 1024)
F32 = jnp.float32
BF16 = jnp.bfloat16

TABLES = {
    128: ((64, 8), (4, 32), (16, 2), (1, 0)),
    16: ((8, 2), (4, 1), (None, None), (None, 0)),
}


def call(kernel, out_shape, in_specs, flops, moved, exps):
    outs = jax.tree.map(lambda _: VMEM, out_shape)
    return pl.pallas_call(
        kernel,
        out_shape=out_shape,
        in_specs=in_specs,
        out_specs=outs,
        compiler_params=PARAMS,
        cost_estimate=pl.CostEstimate(flops=flops, bytes_accessed=moved, transcendentals=exps),
    )


def pack_kernel(key_ref, value_ref, query_ref, grad_ref, kv_ref, qg_ref, sems):
    rows, wide = key_ref.shape[0], query_ref.shape[0]
    copies = [
        pltpu.make_async_copy(key_ref, kv_ref.at[pl.ds(0, rows)], sems.at[0]),
        pltpu.make_async_copy(value_ref, kv_ref.at[pl.ds(rows, rows)], sems.at[1]),
        pltpu.make_async_copy(query_ref, qg_ref.at[pl.ds(0, wide)], sems.at[2]),
        pltpu.make_async_copy(grad_ref, qg_ref.at[pl.ds(wide, wide)], sems.at[3]),
    ]
    for copy in copies:
        copy.start()
    for copy in copies:
        copy.wait()


def mask_kernel(table, lengths_ref, pattern_ref, bias_ref, lengths, pattern, sems):
    copies = [
        pltpu.make_async_copy(lengths_ref, lengths, sems.at[0]),
        pltpu.make_async_copy(pattern_ref, pattern, sems.at[1]),
    ]
    for copy in copies:
        copy.start()
    rows, wide = bias_ref.shape[1:]
    block = 128
    count = rows // block
    span = wide // count
    own = lax.axis_index("ctx")
    lane = lax.rem(lax.axis_index("head"), 2)
    valid, partners = [], []
    for pair in table:
        shift = jnp.where(lane == 0, pair[0] or 0, pair[1] or 0)
        exists = jnp.where(lane == 0, int(pair[0] is not None), int(pair[1] is not None))
        valid.append(jnp.where(own >= shift, exists, 0))
        partners.append(jnp.maximum(own - shift, 0))
    column = lax.broadcasted_iota(jnp.int32, (8, wide), 1)
    sub = lax.broadcasted_iota(jnp.int32, (8, wide), 0)
    pos = own * rows + lax.shift_right_logical(column, 1)
    for slot in range(SLOTS):
        pos = jnp.where(sub == slot + 1, partners[slot] * rows + column, pos)
    for copy in copies:
        copy.wait()

    def add_doc(index, carry):
        end, total = carry
        end = end + lengths[index]
        return end, total + jnp.where(pos >= end, 1.0, 0.0)

    docs = lax.fori_loop(
        0, lengths.shape[0], add_doc, (jnp.int32(0), jnp.zeros((8, wide), F32)), unroll=8
    )[1]
    query_doc = docs[0:1]
    query_pos = pos[0:1]
    down = lax.broadcasted_iota(jnp.int32, (block, span), 0)
    for slot in range(SLOTS):
        for kb in range(count):
            key_doc = docs[slot + 1 : slot + 2, kb * block : (kb + 1) * block]
            key_doc = jnp.broadcast_to(key_doc, (block, block)).T
            key_doc = jnp.concatenate([key_doc] * (span // block), axis=1)
            for qb in range(count):
                cols = slice(qb * span, (qb + 1) * span)
                same = key_doc == query_doc[:, cols]
                early = down + (partners[slot] * rows + kb * block) <= query_pos[:, cols]
                alive = pattern[qb, partners[slot] * count + kb] * valid[slot]
                live = jnp.where(alive == 1, 0.0, NEG)
                bias_ref[slot, kb * block : (kb + 1) * block, cols] = (
                    jnp.where(same & early, 0.0, NEG) + live
                )


def dot(a, b, dims):
    return lax.dot_general(a, b, (dims, ((), ())), preferred_element_type=F32)


NN = ((1,), (0,))
NT = ((1,), (1,))


def part_rows(ref, which):
    half = ref.shape[0] // 2
    return ref[which * half : (which + 1) * half, :]


def columns_of(ref, part):
    half = ref.shape[1] // 2
    return slice(part * half, (part + 1) * half)


def forward_kernel(slots, first, last, *refs):
    sides = refs[:2]
    bias_ref = refs[2]
    kv_refs = refs[3 : 3 + len(slots)]
    rest = refs[3 + len(slots) :]
    if first:
        stat_out, out_out = rest
    else:
        stat_in, out_in, stat_out, out_out = rest
    rows, wide = bias_ref.shape[1:]
    factor = math.log2(math.e) / math.sqrt(kv_refs[0].shape[1])
    values_t = [kv[rows:, :].T for kv in kv_refs]
    for part, side in enumerate(sides):
        cols = columns_of(stat_out, part)
        query = part_rows(side, 0)
        scores = [
            dot(kv[:rows, :], query, NT) * factor + bias_ref[slot]
            for kv, slot in zip(kv_refs, slots)
        ]
        top = functools.reduce(
            jnp.maximum, [jnp.max(piece, axis=0, keepdims=True) for piece in scores]
        )
        if not first:
            top = jnp.maximum(top, stat_in[0:1, cols])
        probs = [jnp.exp2(piece - top) for piece in scores]
        total = sum(jnp.sum(piece, axis=0, keepdims=True) for piece in probs)
        out = sum(dot(value, piece.astype(BF16), NN) for value, piece in zip(values_t, probs))
        if not first:
            fade = jnp.exp2(stat_in[0:1, cols] - top)
            total = total + stat_in[1:2, cols] * fade
            out = out + out_in[:, cols] * fade
        out_out[:, cols] = out
        stat_out[0:1, cols] = top
        stat_out[1:2, cols] = total
        if last:
            grad_t = part_rows(side, 1).T.astype(F32)
            stat_out[2:3, cols] = jnp.sum(grad_t * out, axis=0, keepdims=True)
            stat_out[3:4, cols] = jnp.zeros((1, wide), F32)
        else:
            stat_out[2:4, cols] = jnp.zeros((2, wide), F32)


def merged(stat_ref, other_stat_ref, part):
    cols = columns_of(stat_ref, part)
    other = columns_of(stat_ref, 1 - part)
    top_a, top_b = stat_ref[0:1, cols], other_stat_ref[0:1, other]
    top = jnp.maximum(top_a, top_b)
    fade_a, fade_b = jnp.exp2(top_a - top), jnp.exp2(top_b - top)
    total_b = other_stat_ref[1:2, other] * fade_b
    total = stat_ref[1:2, cols] * fade_a + total_b
    inner = stat_ref[2:3, cols] * fade_a + other_stat_ref[2:3, other] * fade_b
    return top + jnp.log2(total), inner / total, fade_a / total, total_b / total


def backward_kernel(slot, first, last, *refs):
    sides = refs[:2]
    bias_ref, kv_ref, stat_ref, other_stat_ref = refs[2:6]
    rest = refs[6:]
    rows = bias_ref.shape[1]
    dim = kv_ref.shape[1]
    if last:
        out_ref, rest = rest[0], rest[1:]
    if not first:
        query_in, rest = rest[0], rest[1:]
    grad_kv_ref, query_out = rest[:2]
    factor = math.log2(math.e) / math.sqrt(dim)
    scale = 1.0 / math.sqrt(dim)
    key = kv_ref[:rows, :]
    value = kv_ref[rows:, :]
    key_t = key.T
    grad_key = jnp.zeros((rows, dim), F32)
    grad_value = jnp.zeros((rows, dim), F32)
    for part, side in enumerate(sides):
        cols = columns_of(stat_ref, part)
        query, grad = part_rows(side, 0), part_rows(side, 1)
        norm, inner, _, _ = merged(stat_ref, other_stat_ref, part)
        scores = dot(key, query, NT) * factor + bias_ref[slot]
        probs = jnp.exp2(scores - norm)
        grad_value = grad_value + dot(probs.astype(BF16), grad, NN)
        grad_score = (probs * (dot(value, grad, NT) - inner)).astype(BF16)
        grad_key = grad_key + dot(grad_score, query, NN)
        grad_query = dot(key_t, grad_score, NN) * scale
        if not first:
            grad_query = query_in[:, cols] + grad_query
        query_out[:, cols] = grad_query
        if last and part == 1:
            send_ref = rest[2]
            send_ref[:dim, :] = (out_ref[:, cols] / stat_ref[1:2, cols]).astype(BF16)
            send_ref[dim:, :] = grad_query.astype(BF16)
    grad_kv_ref[:rows, :] = (grad_key * scale).astype(BF16)
    grad_kv_ref[rows:, :] = grad_value.astype(BF16)


def finish_kernel(stat_ref, other_stat_ref, out_ref, query_ref, got_ref, attn_ref, grad_ref):
    dim = attn_ref.shape[1]
    cols = columns_of(stat_ref, 0)
    _, _, weight_a, weight_b = merged(stat_ref, other_stat_ref, 0)
    out = out_ref[:, cols] * weight_a + got_ref[:dim, :].astype(F32) * weight_b
    attn_ref[...] = out.T.astype(BF16)
    grad = query_ref[:, cols] + got_ref[dim:, :].astype(F32)
    grad_ref[...] = grad.T.astype(BF16)


def sum_kernel(count, *refs):
    total = sum(ref[...].astype(F32) for ref in refs[:count]).astype(BF16)
    start = 0
    for ref in refs[count:]:
        ref[...] = total[start : start + ref.shape[0], :]
        start += ref.shape[0]


def local(queries, key_rows, value_rows, grad_out, doc_lengths, block_pattern):
    rows, heads, dim = queries.shape
    width = lax.axis_size("ctx")
    lanes = lax.axis_size("head")
    table = TABLES[width]
    edge = width * 3 // 4

    def lane_pairs(shifts, back):
        pairs = []
        for which, shift in enumerate(shifts):
            if shift is None:
                continue
            for source in range(width - shift):
                target = source + shift
                if (source < edge) != (target < edge):
                    continue
                for place in range(which, lanes, 2):
                    pair = (source * lanes + place, target * lanes + place)
                    pairs.append(pair[::-1] if back else pair)
        return pairs

    def swap_pairs(partner):
        return [
            (group * lanes + place, group * lanes + partner(place))
            for group in range(width)
            for place in range(lanes)
        ]

    def send(value, pairs):
        return lax.ppermute(value, AXES, pairs)

    near = swap_pairs(lambda place: place ^ 1)
    far = swap_pairs(lambda place: lanes - 1 - place)

    kv_shape = jax.ShapeDtypeStruct((2 * rows, dim), BF16)
    qg_shape = jax.ShapeDtypeStruct((2 * heads * rows, dim), BF16)
    own_kv, own_qg = pl.pallas_call(
        pack_kernel,
        out_shape=(kv_shape, qg_shape),
        in_specs=[HBM] * 4,
        out_specs=(VMEM, VMEM),
        scratch_shapes=[pltpu.SemaphoreType.DMA((4,))],
        compiler_params=PARAMS,
    )(
        key_rows,
        value_rows,
        queries.reshape(rows * heads, dim),
        grad_out.reshape(rows * heads, dim),
    )
    held = [send(own_kv, lane_pairs(table[0], False))]
    other_qg = send(own_qg, near)
    for slot in range(1, SLOTS):
        held.append(send(own_kv, lane_pairs(table[slot], False)))

    bias = pl.pallas_call(
        functools.partial(mask_kernel, table),
        out_shape=jax.ShapeDtypeStruct((SLOTS, rows, heads * rows), F32),
        in_specs=[HBM, HBM],
        out_specs=VMEM,
        scratch_shapes=[
            pltpu.SMEM(doc_lengths.shape, jnp.int32),
            pltpu.SMEM(block_pattern.shape, jnp.int32),
            pltpu.SemaphoreType.DMA((2,)),
        ],
        compiler_params=PARAMS,
    )(doc_lengths, block_pattern)

    columns = 2 * heads * rows
    stat_shape = jax.ShapeDtypeStruct((4, columns), F32)
    wide_shape = jax.ShapeDtypeStruct((dim, columns), F32)
    unit = 2 * rows * columns * dim

    def forward(slots, carry, last):
        first = carry is None
        kernel = functools.partial(forward_kernel, slots, first, last)
        args = [own_qg, other_qg, bias] + [held[s] for s in slots] + list(carry or ())
        return call(
            kernel,
            (stat_shape, wide_shape),
            [VMEM] * len(args),
            2 * unit * len(slots),
            4 << 20,
            rows * columns * len(slots),
        )(*args)

    stat, out = forward((0, 1), None, False)
    stat, out = forward((2, 3), (stat, out), True)
    other_stat = send(stat, near)

    send_shape = jax.ShapeDtypeStruct((2 * dim, heads * rows), BF16)
    returned = []
    query_grad = None
    for slot in range(SLOTS):
        first, last = slot == 0, slot == SLOTS - 1
        kernel = functools.partial(backward_kernel, slot, first, last)
        args = [own_qg, other_qg, bias, held[slot], stat, other_stat]
        if last:
            args.append(out)
        if not first:
            args.append(query_grad)
        shapes = (kv_shape, wide_shape) + ((send_shape,) if last else ())
        results = call(
            kernel, shapes, [VMEM] * len(args), 5 * unit, 4 << 20, rows * columns
        )(*args)
        grad_kv, query_grad = results[:2]
        returned.append(send(grad_kv, lane_pairs(table[slot], True)))
    got = send(results[2], near)

    def add(pieces, shapes):
        kernel = functools.partial(sum_kernel, len(pieces))
        return call(kernel, shapes, [VMEM] * len(pieces), 0, 1 << 20, 0)(*pieces)

    total = add(returned, (kv_shape,))[0]
    total = add((total, send(total, near)), (kv_shape,))[0]
    key_shape = jax.ShapeDtypeStruct((rows, dim), BF16)
    grad_keys, grad_values = add((total, send(total, far)), (key_shape, key_shape))

    flat = jax.ShapeDtypeStruct((heads * rows, dim), BF16)
    attn, grad_q = call(finish_kernel, (flat, flat), [VMEM] * 5, 0, 2 << 20, 0)(
        stat, other_stat, out, query_grad, got
    )
    shape = (rows, heads, dim)
    return attn.reshape(shape), grad_q.reshape(shape), grad_keys, grad_values


def solution(mesh):
    wide, flat = P("ctx", "head", None), P("ctx", None)

    return jax.shard_map(
        local,
        mesh=mesh,
        in_specs=(wide, flat, flat, wide, P(), flat),
        out_specs=(wide, wide, flat, flat),
        check_vma=False,
    )
```

time: 106 us -> 92.1 us (0.87)
  the two profiles are of different devices: /device:TPU:126 before, /device:TPU:62 now
where the time goes in v2:
time: 92.1 us; the launch traced here: 91.5 us
  starting transfers between devices  39 us (42%)
  waiting for transfers between devices  31.1 us (34%)
  Pallas kernels  15.6 us (17%)
  local copies, waits for them, and re-layouts  4.97 us (5%)
    ppermute x13, starting transfers between devices, send(): return lax.ppermute(value, AXES, pairs)  39 us
    ppermute x13, waiting for transfers between devices, send(): return lax.ppermute(value, AXES, pairs)  31.1 us
    pallas_call x4, Pallas kernels, local(): call(kernel, shapes, [VMEM] * len(args), 5 * unit, 4 << 20, rows * columns)  7.33 us
    unnamed x12, local copies, waits for them, and re-layouts  4.97 us
    pallas_call x2, Pallas kernels, forward(): call(kernel, (stat_shape, wide_shape), [VMEM] * len(args), 2 * unit * len...  4.09 us
  transfers between devices with their start and end apart: 13, of which 5 were waited for; matrix products, arithmetic and copies ran while one was open for 0% of the time, Pallas kernels for 5%

profile of v2, /device:TPU:62, one launch (start us, length us, event | category | flops | bytes accessed | tf_op | source)
XLA Modules:
  0.0 91.5 jit_solution(3500516000169033837)
XLA Ops:
  0.6 0.0 copy-start
  0.6 0.9 %copy-done = bf16[384,2,128]{2,1,0:T(2,128)(2,1)S(1)} copy-done((bf16[384,2,128]{2,1,0:T(2,128)(2,1)S(1)}, bf16[384,2,128]{2,1,0:T(2,128)(2,1)}, u32[]{:S(2)}) %copy-start) | copy-done | bytes 196632
  1.6 0.0 copy-start.1
  1.6 0.9 %copy-done.1 = bf16[384,2,128]{2,1,0:T(2,128)(2,1)S(1)} copy-done((bf16[384,2,128]{2,1,0:T(2,128)(2,1)S(1)}, bf16[384,2,128]{2,1,0:T(2,128)(2,1)}, u32[]{:S(2)}) %copy-start.1) | copy-done | bytes 196632
  2.5 0.0 copy-start.2
  2.5 0.9 copy-done.2
  3.4 0.0 copy-start.3
  3.4 0.9 copy-done.3
  4.3 0.8 shard_map.93
  5.0 2.7 %collective-permute-start = (bf16[1536,128]{1,0:T(8,128)(2,1)S(1)}, bf16[1536,128]{1,0:T(8,128)(2,1)S(1)}, u32[]{:S(2)}, u32[]{:S(2)}) collective-permute-start(bf16[1536,128]{1,0:T(8,128)(2,1)S(1)} %get-tuple-element.23.refs_0_), channel_id=1, source_target_pairs={{0,1},{1,0},{2,3},{3,2},{4,5},{5,4},{6,7},{7,6},{8,9},{9,8},{10,11... | collective-permute-start | bytes 1179656 | tf_op jit(solution)/shard_map/ppermute | solution.py:264
  7.8 6.1 %collective-permute-start.4 = (bf16[768,128]{1,0:T(8,128)(2,1)S(1)}, bf16[768,128]{1,0:T(8,128)(2,1)S(1)}, u32[]{:S(2)}, u32[]{:S(2)}) collective-permute-start(bf16[768,128]{1,0:T(8,128)(2,1)S(1)} %get-tuple-element.24), channel_id=1, source_target_pairs={{0,16},{2,18},{4,20},{6,22},{8,24},{10,26},{12,28},{14,30},{16,32}... | collective-permute-start | bytes 589832 | tf_op jit(solution)/shard_map/ppermute | solution.py:264
  13.9 6.5 %collective-permute-start.3 = (bf16[768,128]{1,0:T(8,128)(2,1)S(1)}, bf16[768,128]{1,0:T(8,128)(2,1)S(1)}, u32[]{:S(2)}, u32[]{:S(2)}) collective-permute-start(bf16[768,128]{1,0:T(8,128)(2,1)S(1)} %get-tuple-element.24), channel_id=1, source_target_pairs={{0,256},{2,258},{4,260},{6,262},{8,264},{10,266},{12,268},{14,270}... | collective-permute-start | bytes 589832 | tf_op jit(solution)/shard_map/ppermute | solution.py:264
  20.4 0.7 collective-permute-start.2
  21.1 4.7 %collective-permute-start.1 = (bf16[768,128]{1,0:T(8,128)(2,1)S(1)}, bf16[768,128]{1,0:T(8,128)(2,1)S(1)}, u32[]{:S(2)}, u32[]{:S(2)}) collective-permute-start(bf16[768,128]{1,0:T(8,128)(2,1)S(1)} %get-tuple-element.24), channel_id=1, source_target_pairs={{0,64},{2,66},{4,68},{6,70},{8,72},{10,74},{12,76},{14,78},{16,80}... | collective-permute-start | bytes 589832 | tf_op jit(solution)/shard_map/ppermute | solution.py:264
  25.8 0.0 copy-start.4
  25.8 0.7 copy-done.4
  26.5 0.7 copy-done.5
  27.2 1.7 %shard_map.94.refs_2_ = f32[4,384,768]{2,1,0:T(8,128)S(1)} custom-call(s32[64]{0:T(128)S(1)} %copy-done.5, s32[3,384]{1,0:T(4,128)S(1)} %copy-done.4), custom_call_target="tpu_custom_call" | custom-call | tf_op jit(solution)/shard_map/pallas_call | solution.py:289
  28.9 0.0 collective-permute-done.4.refs_4_.refs_3_
  28.9 0.0 collective-permute-done.3.refs_3_
  28.9 0.0 collective-permute-done.refs_1_
  28.9 2.1 %shard_map.95 = (f32[4,1536]{1,0:T(4,128)S(1)}, f32[128,1536]{1,0:T(8,128)S(1)}) custom-call(bf16[1536,128]{1,0:T(8,128)(2,1)S(1)} %get-tuple-element.23.refs_0_, bf16[1536,128]{1,0:T(8,128)(2,1)S(1)} %collective-permute-done.refs_1_, f32[4,384,768]{2,1,0:T(8,128)S(1)} %shard_map.94.refs_2_, bf16[768,128]{1,0:T(8,128)(2,1)S(1)} %collective-permute-done.3.refs_3_, ...), custom_call_target="tpu_custom_call" | custom-call | flops 603979776 | bytes 4194304 | tf_op jit(solution)/shard_map/pallas_call | solution.py:311
  31.0 0.0 collective-permute-done.2.refs_4_.refs_3_
  31.0 2.2 %collective-permute-done.1.refs_3_ = bf16[768,128]{1,0:T(8,128)(2,1)S(1)} collective-permute-done((bf16[768,128]{1,0:T(8,128)(2,1)S(1)}, bf16[768,128]{1,0:T(8,128)(2,1)S(1)}, u32[]{:S(2)}, u32[]{:S(2)}) %collective-permute-start.1) | collective-permute-done | bytes 196640 | tf_op jit(solution)/shard_map/ppermute | solution.py:264
  33.2 2.0 %shard_map.96 = (f32[4,1536]{1,0:T(4,128)S(1)}, f32[128,1536]{1,0:T(8,128)S(1)}) custom-call(bf16[1536,128]{1,0:T(8,128)(2,1)S(1)} %get-tuple-element.23.refs_0_, bf16[1536,128]{1,0:T(8,128)(2,1)S(1)} %collective-permute-done.refs_1_, f32[4,384,768]{2,1,0:T(8,128)S(1)} %shard_map.94.refs_2_, bf16[768,128]{1,0:T(8,128)(2,1)S(1)} %collective-permute-done.1.refs_3_, ...), custom_call_target="tpu_custom_call" | custom-call | flops 603979776 | bytes 4194304 | tf_op jit(solution)/shard_map/pallas_call | solution.py:311
  35.2 2.1 %collective-permute-start.5 = (f32[4,1536]{1,0:T(4,128)S(1)}, f32[4,1536]{1,0:T(4,128)S(1)}, u32[]{:S(2)}, u32[]{:S(2)}) collective-permute-start(f32[4,1536]{1,0:T(4,128)S(1)} %get-tuple-element.27.refs_4_.stat_ref), channel_id=1, source_target_pairs={{0,1},{1,0},{2,3},{3,2},{4,5},{5,4},{6,7},{7,6},{8,9},{9,8},{10,11... | collective-permute-start | bytes 73736 | tf_op jit(solution)/shard_map/ppermute | solution.py:264
  37.3 3.6 %collective-permute-done.5.refs_5_.other_stat_ref = f32[4,1536]{1,0:T(4,128)S(1)} collective-permute-done((f32[4,1536]{1,0:T(4,128)S(1)}, f32[4,1536]{1,0:T(4,128)S(1)}, u32[]{:S(2)}, u32[]{:S(2)}) %collective-permute-start.5) | collective-permute-done | bytes 24608 | tf_op jit(solution)/shard_map/ppermute | solution.py:264
  40.9 1.8 %shard_map.97 = (bf16[768,128]{1,0:T(8,128)(2,1)S(1)}, f32[128,1536]{1,0:T(8,128)S(1)}) custom-call(bf16[1536,128]{1,0:T(8,128)(2,1)S(1)} %get-tuple-element.23.refs_0_, bf16[1536,128]{1,0:T(8,128)(2,1)S(1)} %collective-permute-done.refs_1_, f32[4,384,768]{2,1,0:T(8,128)S(1)} %shard_map.94.refs_2_, bf16[768,128]{1,0:T(8,128)(2,1)S(1)} %collective-permute-done.3.refs_3_, ...), custom_call_target="tpu_custom_call" | custom-call | flops 754974720 | bytes 4194304 | tf_op jit(solution)/shard_map/pallas_call | solution.py:336
  42.7 1.8 %shard_map.98 = (bf16[768,128]{1,0:T(8,128)(2,1)S(1)}, f32[128,1536]{1,0:T(8,128)S(1)}) custom-call(bf16[1536,128]{1,0:T(8,128)(2,1)S(1)} %get-tuple-element.23.refs_0_, bf16[1536,128]{1,0:T(8,128)(2,1)S(1)} %collective-permute-done.refs_1_, f32[4,384,768]{2,1,0:T(8,128)S(1)} %shard_map.94.refs_2_, ...), custom_call_target="tpu_custom_call" | custom-call | flops 754974720 | bytes 4194304 | tf_op jit(solution)/shard_map/pallas_call | solution.py:336
  44.6 1.8 %shard_map.99 = (bf16[768,128]{1,0:T(8,128)(2,1)S(1)}, f32[128,1536]{1,0:T(8,128)S(1)}) custom-call(bf16[1536,128]{1,0:T(8,128)(2,1)S(1)} %get-tuple-element.23.refs_0_, bf16[1536,128]{1,0:T(8,128)(2,1)S(1)} %collective-permute-done.refs_1_, f32[4,384,768]{2,1,0:T(8,128)S(1)} %shard_map.94.refs_2_, bf16[768,128]{1,0:T(8,128)(2,1)S(1)} %collective-permute-done.1.refs_3_, ...), custom_call_target="tpu_custom_call" | custom-call | flops 754974720 | bytes 4194304 | tf_op jit(solution)/shard_map/pallas_call | solution.py:336
  46.4 1.8 %shard_map.100 = (bf16[768,128]{1,0:T(8,128)(2,1)S(1)}, f32[128,1536]{1,0:T(8,128)S(1)}, bf16[256,768]{1,0:T(8,128)(2,1)S(1)}) custom-call(bf16[1536,128]{1,0:T(8,128)(2,1)S(1)} %get-tuple-element.23.refs_0_, bf16[1536,128]{1,0:T(8,128)(2,1)S(1)} %collective-permute-done.refs_1_, f32[4,384,768]{2,1,0:T(8,128)S(1)} %shard_map.94.refs_2_, ...), custom_call_target="tpu_custom_call" | custom-call | flops 754974720 | bytes 4194304 | tf_op jit(solution)/shard_map/pallas_call | solution.py:336
  48.3 0.7 collective-permute-start.10
  48.9 3.8 %collective-permute-start.9 = (bf16[768,128]{1,0:T(8,128)(2,1)S(1)}, bf16[768,128]{1,0:T(8,128)(2,1)S(1)}, u32[]{:S(2)}, u32[]{:S(2)}) collective-permute-start(bf16[768,128]{1,0:T(8,128)(2,1)S(1)} %get-tuple-element.38), channel_id=1, source_target_pairs={{64,0},{66,2},{68,4},{70,6},{72,8},{74,10},{76,12},{78,14},{80,16}... | collective-permute-start | bytes 589832 | tf_op jit(solution)/shard_map/ppermute | solution.py:264
  52.7 1.3 %collective-permute-start.8 = (bf16[768,128]{1,0:T(8,128)(2,1)S(1)}, bf16[768,128]{1,0:T(8,128)(2,1)S(1)}, u32[]{:S(2)}, u32[]{:S(2)}) collective-permute-start(bf16[768,128]{1,0:T(8,128)(2,1)S(1)} %get-tuple-element.37), channel_id=1, source_target_pairs={{16,0},{18,2},{20,4},{22,6},{24,8},{26,10},{28,12},{30,14},{32,16}... | collective-permute-start | bytes 589832 | tf_op jit(solution)/shard_map/ppermute | solution.py:264
  54.0 4.6 %collective-permute-start.7 = (bf16[768,128]{1,0:T(8,128)(2,1)S(1)}, bf16[768,128]{1,0:T(8,128)(2,1)S(1)}, u32[]{:S(2)}, u32[]{:S(2)}) collective-permute-start(bf16[768,128]{1,0:T(8,128)(2,1)S(1)} %get-tuple-element.36), channel_id=1, source_target_pairs={{256,0},{258,2},{260,4},{262,6},{264,8},{266,10},{268,12},{270,14}... | collective-permute-start | bytes 589832 | tf_op jit(solution)/shard_map/ppermute | solution.py:264
  58.7 1.9 %collective-permute-start.6 = (bf16[256,768]{1,0:T(8,128)(2,1)S(1)}, bf16[256,768]{1,0:T(8,128)(2,1)S(1)}, u32[]{:S(2)}, u32[]{:S(2)}) collective-permute-start(bf16[256,768]{1,0:T(8,128)(2,1)S(1)} %get-tuple-element.33), channel_id=1, source_target_pairs={{0,1},{1,0},{2,3},{3,2},{4,5},{5,4},{6,7},{7,6},{8,9},{9,8},{10,11... | collective-permute-start | bytes 1179656 | tf_op jit(solution)/shard_map/ppermute | solution.py:264
  60.6 0.0 collective-permute-done.10.refs_3_
  60.6 0.0 collective-permute-done.9.refs_2_
  60.6 12.5 %collective-permute-done.8.refs_1_ = bf16[768,128]{1,0:T(8,128)(2,1)S(1)} collective-permute-done((bf16[768,128]{1,0:T(8,128)(2,1)S(1)}, bf16[768,128]{1,0:T(8,128)(2,1)S(1)}, u32[]{:S(2)}, u32[]{:S(2)}) %collective-permute-start.8) | collective-permute-done | bytes 196640 | tf_op jit(solution)/shard_map/ppermute | solution.py:264
  73.1 0.0 collective-permute-done.7.refs_0_
  73.1 0.1 shard_map.102.refs_0_
  73.2 1.9 %collective-permute-start.11 = (bf16[768,128]{1,0:T(8,128)(2,1)S(1)}, bf16[768,128]{1,0:T(8,128)(2,1)S(1)}, u32[]{:S(2)}, u32[]{:S(2)}) collective-permute-start(bf16[768,128]{1,0:T(8,128)(2,1)S(1)} %shard_map.102.refs_0_), channel_id=1, source_target_pairs={{0,1},{1,0},{2,3},{3,2},{4,5},{5,4},{6,7},{7,6},{8,9},{9,8},{10,11... | collective-permute-start | bytes 589832 | tf_op jit(solution)/shard_map/ppermute | solution.py:264
  75.2 6.7 %collective-permute-done.11.refs_1_ = bf16[768,128]{1,0:T(8,128)(2,1)S(1)} collective-permute-done((bf16[768,128]{1,0:T(8,128)(2,1)S(1)}, bf16[768,128]{1,0:T(8,128)(2,1)S(1)}, u32[]{:S(2)}, u32[]{:S(2)}) %collective-permute-start.11) | collective-permute-done | bytes 196640 | tf_op jit(solution)/shard_map/ppermute | solution.py:264
  81.9 1.9 %collective-permute-start.12 = (bf16[768,128]{1,0:T(8,128)(2,1)S(1)}, bf16[768,128]{1,0:T(8,128)(2,1)S(1)}, u32[]{:S(2)}, u32[]{:S(2)}) collective-permute-start(bf16[768,128]{1,0:T(8,128)(2,1)S(1)} %shard_map.103.refs_0_), channel_id=1, source_target_pairs={{0,3},{1,2},{2,1},{3,0},{4,7},{5,6},{6,5},{7,4},{8,11},{9,10},{10,... | collective-permute-start | bytes 589832 | tf_op jit(solution)/shard_map/ppermute | solution.py:264
  83.8 0.0 collective-permute-done.6.got_ref
  83.8 0.9 %shard_map.101 = (bf16[768,128]{1,0:T(8,128)(2,1)}, bf16[768,128]{1,0:T(8,128)(2,1)}) custom-call(f32[4,1536]{1,0:T(4,128)S(1)} %get-tuple-element.27.refs_4_.stat_ref, f32[4,1536]{1,0:T(4,128)S(1)} %collective-permute-done.5.refs_5_.other_stat_ref, f32[128,1536]{1,0:T(8,128)S(1)} %get-tuple-element.28.refs_6_.out_ref, ...), custom_call_target="tpu_custom_call" | custom-call | bytes 2097152 | tf_op jit(solution)/shard_map/pallas_call | solution.py:353
  84.7 6.1 %collective-permute-done.12.refs_1_ = bf16[768,128]{1,0:T(8,128)(2,1)S(1)} collective-permute-done((bf16[768,128]{1,0:T(8,128)(2,1)S(1)}, bf16[768,128]{1,0:T(8,128)(2,1)S(1)}, u32[]{:S(2)}, u32[]{:S(2)}) %collective-permute-start.12) | collective-permute-done | bytes 196640 | tf_op jit(solution)/shard_map/ppermute | solution.py:264
  90.8 0.7 shard_map.104
  (2 shorter events, 0.0 us)
Async XLA Ops:
  0.6 0.9 %copy-start = (bf16[384,2,128]{2,1,0:T(2,128)(2,1)S(1)}, bf16[384,2,128]{2,1,0:T(2,128)(2,1)}, u32[]{:S(2)}) copy-start(bf16[384,2,128]{2,1,0:T(2,128)(2,1)} %param.6) | copy-start | bytes 589828
  1.6 0.9 %copy-start.1 = (bf16[384,2,128]{2,1,0:T(2,128)(2,1)S(1)}, bf16[384,2,128]{2,1,0:T(2,128)(2,1)}, u32[]{:S(2)}) copy-start(bf16[384,2,128]{2,1,0:T(2,128)(2,1)} %param.9) | copy-start | bytes 589828
  2.5 0.9 copy-start.2
  3.4 0.9 copy-start.3
  5.0 23.8 %collective-permute-start = (bf16[1536,128]{1,0:T(8,128)(2,1)S(1)}, bf16[1536,128]{1,0:T(8,128)(2,1)S(1)}, u32[]{:S(2)}, u32[]{:S(2)}) collective-permute-start(bf16[1536,128]{1,0:T(8,128)(2,1)S(1)} %get-tuple-element.23.refs_0_), channel_id=1, source_target_pairs={{0,1},{1,0},{2,3},{3,2},{4,5},{5,4},{6,7},{7,6},{8,9},{9,8},{10,11... | collective-permute-start | bytes 1179656 | tf_op jit(solution)/shard_map/ppermute | solution.py:264
  7.8 21.1 %collective-permute-start.4 = (bf16[768,128]{1,0:T(8,128)(2,1)S(1)}, bf16[768,128]{1,0:T(8,128)(2,1)S(1)}, u32[]{:S(2)}, u32[]{:S(2)}) collective-permute-start(bf16[768,128]{1,0:T(8,128)(2,1)S(1)} %get-tuple-element.24), channel_id=1, source_target_pairs={{0,16},{2,18},{4,20},{6,22},{8,24},{10,26},{12,28},{14,30},{16,32}... | collective-permute-start | bytes 589832 | tf_op jit(solution)/shard_map/ppermute | solution.py:264
  13.9 15.0 %collective-permute-start.3 = (bf16[768,128]{1,0:T(8,128)(2,1)S(1)}, bf16[768,128]{1,0:T(8,128)(2,1)S(1)}, u32[]{:S(2)}, u32[]{:S(2)}) collective-permute-start(bf16[768,128]{1,0:T(8,128)(2,1)S(1)} %get-tuple-element.24), channel_id=1, source_target_pairs={{0,256},{2,258},{4,260},{6,262},{8,264},{10,266},{12,268},{14,270}... | collective-permute-start | bytes 589832 | tf_op jit(solution)/shard_map/ppermute | solution.py:264
  20.4 10.5 %collective-permute-start.2 = (bf16[768,128]{1,0:T(8,128)(2,1)S(1)}, bf16[768,128]{1,0:T(8,128)(2,1)S(1)}, u32[]{:S(2)}, u32[]{:S(2)}) collective-permute-start(bf16[768,128]{1,0:T(8,128)(2,1)S(1)} %get-tuple-element.24), channel_id=1, source_target_pairs={{0,4},{2,6},{4,8},{6,10},{8,12},{10,14},{12,16},{14,18},{16,20},{1... | collective-permute-start | bytes 589832 | tf_op jit(solution)/shard_map/ppermute | solution.py:264
  21.1 12.0 %collective-permute-start.1 = (bf16[768,128]{1,0:T(8,128)(2,1)S(1)}, bf16[768,128]{1,0:T(8,128)(2,1)S(1)}, u32[]{:S(2)}, u32[]{:S(2)}) collective-permute-start(bf16[768,128]{1,0:T(8,128)(2,1)S(1)} %get-tuple-element.24), channel_id=1, source_target_pairs={{0,64},{2,66},{4,68},{6,70},{8,72},{10,74},{12,76},{14,78},{16,80}... | collective-permute-start | bytes 589832 | tf_op jit(solution)/shard_map/ppermute | solution.py:264
  25.8 0.7 copy-start.4
  26.5 0.7 copy-start.5
  35.2 5.7 %collective-permute-start.5 = (f32[4,1536]{1,0:T(4,128)S(1)}, f32[4,1536]{1,0:T(4,128)S(1)}, u32[]{:S(2)}, u32[]{:S(2)}) collective-permute-start(f32[4,1536]{1,0:T(4,128)S(1)} %get-tuple-element.27.refs_4_.stat_ref), channel_id=1, source_target_pairs={{0,1},{1,0},{2,3},{3,2},{4,5},{5,4},{6,7},{7,6},{8,9},{9,8},{10,11... | collective-permute-start | bytes 73736 | tf_op jit(solution)/shard_map/ppermute | solution.py:264
  48.3 12.3 %collective-permute-start.10 = (bf16[768,128]{1,0:T(8,128)(2,1)S(1)}, bf16[768,128]{1,0:T(8,128)(2,1)S(1)}, u32[]{:S(2)}, u32[]{:S(2)}) collective-permute-start(bf16[768,128]{1,0:T(8,128)(2,1)S(1)} %get-tuple-element.39), channel_id=1, source_target_pairs={{4,0},{6,2},{8,4},{10,6},{12,8},{14,10},{16,12},{18,14},{20,16},{2... | collective-permute-start | bytes 589832 | tf_op jit(solution)/shard_map/ppermute | solution.py:264
  48.9 11.7 %collective-permute-start.9 = (bf16[768,128]{1,0:T(8,128)(2,1)S(1)}, bf16[768,128]{1,0:T(8,128)(2,1)S(1)}, u32[]{:S(2)}, u32[]{:S(2)}) collective-permute-start(bf16[768,128]{1,0:T(8,128)(2,1)S(1)} %get-tuple-element.38), channel_id=1, source_target_pairs={{64,0},{66,2},{68,4},{70,6},{72,8},{74,10},{76,12},{78,14},{80,16}... | collective-permute-start | bytes 589832 | tf_op jit(solution)/shard_map/ppermute | solution.py:264
  52.7 20.4 %collective-permute-start.8 = (bf16[768,128]{1,0:T(8,128)(2,1)S(1)}, bf16[768,128]{1,0:T(8,128)(2,1)S(1)}, u32[]{:S(2)}, u32[]{:S(2)}) collective-permute-start(bf16[768,128]{1,0:T(8,128)(2,1)S(1)} %get-tuple-element.37), channel_id=1, source_target_pairs={{16,0},{18,2},{20,4},{22,6},{24,8},{26,10},{28,12},{30,14},{32,16}... | collective-permute-start | bytes 589832 | tf_op jit(solution)/shard_map/ppermute | solution.py:264
  54.0 19.1 %collective-permute-start.7 = (bf16[768,128]{1,0:T(8,128)(2,1)S(1)}, bf16[768,128]{1,0:T(8,128)(2,1)S(1)}, u32[]{:S(2)}, u32[]{:S(2)}) collective-permute-start(bf16[768,128]{1,0:T(8,128)(2,1)S(1)} %get-tuple-element.36), channel_id=1, source_target_pairs={{256,0},{258,2},{260,4},{262,6},{264,8},{266,10},{268,12},{270,14}... | collective-permute-start | bytes 589832 | tf_op jit(solution)/shard_map/ppermute | solution.py:264
  58.7 25.1 %collective-permute-start.6 = (bf16[256,768]{1,0:T(8,128)(2,1)S(1)}, bf16[256,768]{1,0:T(8,128)(2,1)S(1)}, u32[]{:S(2)}, u32[]{:S(2)}) collective-permute-start(bf16[256,768]{1,0:T(8,128)(2,1)S(1)} %get-tuple-element.33), channel_id=1, source_target_pairs={{0,1},{1,0},{2,3},{3,2},{4,5},{5,4},{6,7},{7,6},{8,9},{9,8},{10,11... | collective-permute-start | bytes 1179656 | tf_op jit(solution)/shard_map/ppermute | solution.py:264
  73.2 8.6 %collective-permute-start.11 = (bf16[768,128]{1,0:T(8,128)(2,1)S(1)}, bf16[768,128]{1,0:T(8,128)(2,1)S(1)}, u32[]{:S(2)}, u32[]{:S(2)}) collective-permute-start(bf16[768,128]{1,0:T(8,128)(2,1)S(1)} %shard_map.102.refs_0_), channel_id=1, source_target_pairs={{0,1},{1,0},{2,3},{3,2},{4,5},{5,4},{6,7},{7,6},{8,9},{9,8},{10,11... | collective-permute-start | bytes 589832 | tf_op jit(solution)/shard_map/ppermute | solution.py:264
  81.9 8.9 %collective-permute-start.12 = (bf16[768,128]{1,0:T(8,128)(2,1)S(1)}, bf16[768,128]{1,0:T(8,128)(2,1)S(1)}, u32[]{:S(2)}, u32[]{:S(2)}) collective-permute-start(bf16[768,128]{1,0:T(8,128)(2,1)S(1)} %shard_map.103.refs_0_), channel_id=1, source_target_pairs={{0,3},{1,2},{2,1},{3,0},{4,7},{5,6},{6,5},{7,4},{8,11},{9,10},{10,... | collective-permute-start | bytes 589832 | tf_op jit(solution)/shard_map/ppermute | solution.py:264

commit v3 on v2

--- a/solution.py
+++ b/solution.py
@@ -87,19 +87,21 @@
     query_doc = docs[0:1]
     query_pos = pos[0:1]
     down = lax.broadcasted_iota(jnp.int32, (block, span), 0)
-    for slot in range(SLOTS):
+    for slot, pair in enumerate(table):
         for kb in range(count):
             key_doc = docs[slot + 1 : slot + 2, kb * block : (kb + 1) * block]
             key_doc = jnp.broadcast_to(key_doc, (block, block)).T
             key_doc = jnp.concatenate([key_doc] * (span // block), axis=1)
             for qb in range(count):
                 cols = slice(qb * span, (qb + 1) * span)
-                same = key_doc == query_doc[:, cols]
-                early = down + (partners[slot] * rows + kb * block) <= query_pos[:, cols]
+                open_pair = key_doc == query_doc[:, cols]
+                if 0 in pair:
+                    early = down + (partners[slot] * rows + kb * block) <= query_pos[:, cols]
+                    open_pair = open_pair & early
                 alive = pattern[qb, partners[slot] * count + kb] * valid[slot]
                 live = jnp.where(alive == 1, 0.0, NEG)
-                bias_ref[slot, kb * block : (kb + 1) * block, cols] = (
-                    jnp.where(same & early, 0.0, NEG) + live
+                bias_ref[slot, kb * block : (kb + 1) * block, cols] = jnp.where(
+                    open_pair, live, NEG
                 )
 
 
@@ -126,10 +128,9 @@
     bias_ref = refs[2]
     kv_refs = refs[3 : 3 + len(slots)]
     rest = refs[3 + len(slots) :]
-    if first:
-        stat_out, out_out = rest
-    else:
-        stat_in, out_in, stat_out, out_out = rest
+    if not first:
+        stat_in, out_in, *rest = rest
+    stat_out, out_out = rest[:2]
     rows, wide = bias_ref.shape[1:]
     factor = math.log2(math.e) / math.sqrt(kv_refs[0].shape[1])
     values_t = [kv[rows:, :].T for kv in kv_refs]
@@ -159,6 +160,8 @@
             grad_t = part_rows(side, 1).T.astype(F32)
             stat_out[2:3, cols] = jnp.sum(grad_t * out, axis=0, keepdims=True)
             stat_out[3:4, cols] = jnp.zeros((1, wide), F32)
+            if part == 1:
+                rest[2][...] = (out / total).astype(BF16)
         else:
             stat_out[2:4, cols] = jnp.zeros((2, wide), F32)
 
@@ -181,8 +184,6 @@
     rest = refs[6:]
     rows = bias_ref.shape[1]
     dim = kv_ref.shape[1]
-    if last:
-        out_ref, rest = rest[0], rest[1:]
     if not first:
         query_in, rest = rest[0], rest[1:]
     grad_kv_ref, query_out = rest[:2]
@@ -207,20 +208,20 @@
             grad_query = query_in[:, cols] + grad_query
         query_out[:, cols] = grad_query
         if last and part == 1:
-            send_ref = rest[2]
-            send_ref[:dim, :] = (out_ref[:, cols] / stat_ref[1:2, cols]).astype(BF16)
-            send_ref[dim:, :] = grad_query.astype(BF16)
+            rest[2][...] = grad_query.astype(BF16)
     grad_kv_ref[:rows, :] = (grad_key * scale).astype(BF16)
     grad_kv_ref[rows:, :] = grad_value.astype(BF16)
 
 
-def finish_kernel(stat_ref, other_stat_ref, out_ref, query_ref, got_ref, attn_ref, grad_ref):
-    dim = attn_ref.shape[1]
+def finish_out_kernel(stat_ref, other_stat_ref, out_ref, got_ref, attn_ref):
     cols = columns_of(stat_ref, 0)
     _, _, weight_a, weight_b = merged(stat_ref, other_stat_ref, 0)
-    out = out_ref[:, cols] * weight_a + got_ref[:dim, :].astype(F32) * weight_b
+    out = out_ref[:, cols] * weight_a + got_ref[...].astype(F32) * weight_b
     attn_ref[...] = out.T.astype(BF16)
-    grad = query_ref[:, cols] + got_ref[dim:, :].astype(F32)
+
+
+def finish_query_kernel(query_ref, got_ref, grad_ref):
+    grad = query_ref[:, columns_of(query_ref, 0)] + got_ref[...].astype(F32)
     grad_ref[...] = grad.T.astype(BF16)
 
 
@@ -274,7 +275,7 @@
         in_specs=[HBM] * 4,
         out_specs=(VMEM, VMEM),
         scratch_shapes=[pltpu.SemaphoreType.DMA((4,))],
-        compiler_params=PARAMS,
+        compiler_params=pltpu.CompilerParams(vmem_limit_bytes=67043328),
     )(
         key_rows,
         value_rows,
@@ -304,13 +305,15 @@
     wide_shape = jax.ShapeDtypeStruct((dim, columns), F32)
     unit = 2 * rows * columns * dim
 
+    send_shape = jax.ShapeDtypeStruct((dim, heads * rows), BF16)
+
     def forward(slots, carry, last):
         first = carry is None
         kernel = functools.partial(forward_kernel, slots, first, last)
         args = [own_qg, other_qg, bias] + [held[s] for s in slots] + list(carry or ())
         return call(
             kernel,
-            (stat_shape, wide_shape),
+            (stat_shape, wide_shape) + ((send_shape,) if last else ()),
             [VMEM] * len(args),
             2 * unit * len(slots),
             4 << 20,
@@ -318,18 +321,16 @@
         )(*args)
 
     stat, out = forward((0, 1), None, False)
-    stat, out = forward((2, 3), (stat, out), True)
+    stat, out, other_out = forward((2, 3), (stat, out), True)
     other_stat = send(stat, near)
-
-    send_shape = jax.ShapeDtypeStruct((2 * dim, heads * rows), BF16)
+    got_out = send(other_out, near)
+
     returned = []
     query_grad = None
     for slot in range(SLOTS):
         first, last = slot == 0, slot == SLOTS - 1
         kernel = functools.partial(backward_kernel, slot, first, last)
         args = [own_qg, other_qg, bias, held[slot], stat, other_stat]
-        if last:
-            args.append(out)
         if not first:
             args.append(query_grad)
         shapes = (kv_shape, wide_shape) + ((send_shape,) if last else ())
@@ -338,7 +339,7 @@
         )(*args)
         grad_kv, query_grad = results[:2]
         returned.append(send(grad_kv, lane_pairs(table[slot], True)))
-    got = send(results[2], near)
+    got_query = send(results[2], near)
 
     def add(pieces, shapes):
         kernel = functools.partial(sum_kernel, len(pieces))
@@ -350,8 +351,11 @@
     grad_keys, grad_values = add((total, send(total, far)), (key_shape, key_shape))
 
     flat = jax.ShapeDtypeStruct((heads * rows, dim), BF16)
-    attn, grad_q = call(finish_kernel, (flat, flat), [VMEM] * 5, 0, 2 << 20, 0)(
-        stat, other_stat, out, query_grad, got
+    attn = call(finish_out_kernel, flat, [VMEM] * 4, 0, 1 << 20, 0)(
+        stat, other_stat, out, got_out
+    )
+    grad_q = call(finish_query_kernel, flat, [VMEM] * 2, 0, 1 << 20, 0)(
+        query_grad, got_query
     )
     shape = (rows, heads, dim)
     return attn.reshape(shape), grad_q.reshape(shape), grad_keys, grad_values

time: 92.1 us -> 90.8 us (0.986)
  starting transfers between devices: 39 us -> 43.7 us
  waiting for transfers between devices: 31.1 us -> 27.2 us
  local copies, waits for them, and re-layouts: 4.97 us -> 1.35 us
  Pallas kernels: 15.6 us -> 17.1 us
    ppermute x13 -> x14, starting transfers between devices: 39 us -> 43.7 us  [send(): return lax.ppermute(value, AXES, pairs)]
    ppermute x13 -> x14, waiting for transfers between devices: 31.1 us -> 27.2 us  [send(): return lax.ppermute(value, AXES, pairs)]
    unnamed x12 -> x6, local copies, waits for them, and re-layouts: 4.97 us -> 1.35 us
    pallas_call x1, Pallas kernels: 0.77 us -> 1.96 us  [local(): pl.pallas_call(pack_kernel, out_shape=(kv_shape, qg_shape), in_specs=[HBM...]
    pallas_call x3 -> x4, Pallas kernels: 5.01 us -> 5.72 us  [the longest x2 4.06 us: forward(): call(kernel, (stat_shape, wide_shape) + ((send_shape,) if last else ()),...]
  transfers between devices with their start and end apart: 13 -> 14, of which waited for: 5 -> 8; matrix products, arithmetic and copies ran while one was open for 0% -> 0% of each run, Pallas kernels for 5% -> 6%
where the time goes in v3:
time: 90.8 us; the launch traced here: 90.3 us
  starting transfers between devices  43.7 us (48%)
  waiting for transfers between devices  27.2 us (30%)
  Pallas kernels  17.1 us (19%)
  local copies, waits for them, and re-layouts  1.35 us (1%)
    ppermute x14, starting transfers between devices, send(): return lax.ppermute(value, AXES, pairs)  43.7 us
    ppermute x14, waiting for transfers between devices, send(): return lax.ppermute(value, AXES, pairs)  27.2 us
    pallas_call x4, Pallas kernels, local(): call(kernel, shapes, [VMEM] * len(args), 5 * unit, 4 << 20, rows * columns)  7.27 us
    pallas_call x2, Pallas kernels, forward(): call(kernel, (stat_shape, wide_shape) + ((send_shape,) if last else ()),...  4.06 us
    pallas_call x1, Pallas kernels, local(): pl.pallas_call(pack_kernel, out_shape=(kv_shape, qg_shape), in_specs=[HBM...  1.96 us
  transfers between devices with their start and end apart: 14, of which 8 were waited for; matrix products, arithmetic and copies ran while one was open for 0% of the time, Pallas kernels for 6%

profile of v3, /device:TPU:62, one launch (start us, length us, event | category | flops | bytes accessed | tf_op | source)
XLA Modules:
  0.0 90.3 jit_solution(1596383192941084541)
XLA Ops:
  0.6 2.0 %shard_map.93 = (bf16[768,128]{1,0:T(8,128)(2,1)}, bf16[1536,128]{1,0:T(8,128)(2,1)}) custom-call(bf16[384,128]{1,0:T(8,128)(2,1)} %key_ref.1, bf16[384,128]{1,0:T(8,128)(2,1)} %value_ref.1, bf16[768,128]{1,0:T(8,128)(2,1)} %bitcast.6, bf16[768,128]{1,0:T(8,128)(2,1)} %bitcast.7), custom_call_target="tpu_custom_call" | custom-call | tf_op jit(solution)/shard_map/pallas_call | solution.py:272
  2.6 0.0 copy-start
  2.6 2.9 %collective-permute-start = (bf16[1536,128]{1,0:T(8,128)(2,1)}, bf16[1536,128]{1,0:T(8,128)(2,1)S(1)}, u32[]{:S(2)}, u32[]{:S(2)}) collective-permute-start(bf16[1536,128]{1,0:T(8,128)(2,1)} %get-tuple-element.22.refs_0_), channel_id=1, source_target_pairs={{0,1},{1,0},{2,3},{3,2},{4,5},{5,4},{6,7},{7,6},{8,9},{9,8},{10,11... | collective-permute-start | bytes 1179656 | tf_op jit(solution)/shard_map/ppermute | solution.py:265
  5.5 6.1 %collective-permute-start.4 = (bf16[768,128]{1,0:T(8,128)(2,1)}, bf16[768,128]{1,0:T(8,128)(2,1)S(1)}, u32[]{:S(2)}, u32[]{:S(2)}) collective-permute-start(bf16[768,128]{1,0:T(8,128)(2,1)} %get-tuple-element.23), channel_id=1, source_target_pairs={{0,16},{2,18},{4,20},{6,22},{8,24},{10,26},{12,28},{14,30},{16,32}... | collective-permute-start | bytes 589832 | tf_op jit(solution)/shard_map/ppermute | solution.py:265
  11.6 6.5 %collective-permute-start.3 = (bf16[768,128]{1,0:T(8,128)(2,1)}, bf16[768,128]{1,0:T(8,128)(2,1)S(1)}, u32[]{:S(2)}, u32[]{:S(2)}) collective-permute-start(bf16[768,128]{1,0:T(8,128)(2,1)} %get-tuple-element.23), channel_id=1, source_target_pairs={{0,256},{2,258},{4,260},{6,262},{8,264},{10,266},{12,268},{14,270}... | collective-permute-start | bytes 589832 | tf_op jit(solution)/shard_map/ppermute | solution.py:265
  18.1 1.6 %collective-permute-start.2 = (bf16[768,128]{1,0:T(8,128)(2,1)}, bf16[768,128]{1,0:T(8,128)(2,1)S(1)}, u32[]{:S(2)}, u32[]{:S(2)}) collective-permute-start(bf16[768,128]{1,0:T(8,128)(2,1)} %get-tuple-element.23), channel_id=1, source_target_pairs={{0,4},{2,6},{4,8},{6,10},{8,12},{10,14},{12,16},{14,18},{16,20},{1... | collective-permute-start | bytes 589832 | tf_op jit(solution)/shard_map/ppermute | solution.py:265
  19.7 4.7 %collective-permute-start.1 = (bf16[768,128]{1,0:T(8,128)(2,1)}, bf16[768,128]{1,0:T(8,128)(2,1)S(1)}, u32[]{:S(2)}, u32[]{:S(2)}) collective-permute-start(bf16[768,128]{1,0:T(8,128)(2,1)} %get-tuple-element.23), channel_id=1, source_target_pairs={{0,64},{2,66},{4,68},{6,70},{8,72},{10,74},{12,76},{14,78},{16,80}... | collective-permute-start | bytes 589832 | tf_op jit(solution)/shard_map/ppermute | solution.py:265
  24.4 0.0 copy-start.1
  24.4 0.7 copy-done.1
  25.1 0.0 copy-start.2
  25.1 0.7 copy-done.2
  25.8 1.3 %shard_map.94.refs_2_ = f32[4,384,768]{2,1,0:T(8,128)S(1)} custom-call(s32[64]{0:T(128)S(1)} %copy-done.2, s32[3,384]{1,0:T(4,128)S(1)} %copy-done.1), custom_call_target="tpu_custom_call" | custom-call | tf_op jit(solution)/shard_map/pallas_call | solution.py:290
  27.1 0.0 collective-permute-done.4.refs_4_.refs_3_
  27.1 0.0 collective-permute-done.3.refs_3_
  27.1 0.0 collective-permute-done.refs_1_
  27.1 0.0 copy-done
  27.1 2.0 %shard_map.95 = (f32[4,1536]{1,0:T(4,128)S(1)}, f32[128,1536]{1,0:T(8,128)S(1)}) custom-call(bf16[1536,128]{1,0:T(8,128)(2,1)S(1)} %copy-done, bf16[1536,128]{1,0:T(8,128)(2,1)S(1)} %collective-permute-done.refs_1_, f32[4,384,768]{2,1,0:T(8,128)S(1)} %shard_map.94.refs_2_, bf16[768,128]{1,0:T(8,128)(2,1)S(1)} %collective-permute-done.3.refs_3_, ...), custom_call_target="tpu_custom_call" | custom-call | flops 603979776 | bytes 4194304 | tf_op jit(solution)/shard_map/pallas_call | solution.py:314
  29.2 0.0 collective-permute-done.2.refs_4_.refs_3_
  29.2 1.9 %collective-permute-done.1.refs_3_ = bf16[768,128]{1,0:T(8,128)(2,1)S(1)} collective-permute-done((bf16[768,128]{1,0:T(8,128)(2,1)}, bf16[768,128]{1,0:T(8,128)(2,1)S(1)}, u32[]{:S(2)}, u32[]{:S(2)}) %collective-permute-start.1) | collective-permute-done | bytes 196640 | tf_op jit(solution)/shard_map/ppermute | solution.py:265
  31.1 2.0 %shard_map.96 = (f32[4,1536]{1,0:T(4,128)S(1)}, f32[128,1536]{1,0:T(8,128)S(1)}, bf16[128,768]{1,0:T(8,128)(2,1)S(1)}) custom-call(bf16[1536,128]{1,0:T(8,128)(2,1)S(1)} %copy-done, bf16[1536,128]{1,0:T(8,128)(2,1)S(1)} %collective-permute-done.refs_1_, f32[4,384,768]{2,1,0:T(8,128)S(1)} %shard_map.94.refs_2_, ...), custom_call_target="tpu_custom_call" | custom-call | flops 603979776 | bytes 4194304 | tf_op jit(solution)/shard_map/pallas_call | solution.py:314
  33.1 1.9 %collective-permute-start.5 = (f32[4,1536]{1,0:T(4,128)S(1)}, f32[4,1536]{1,0:T(4,128)S(1)}, u32[]{:S(2)}, u32[]{:S(2)}) collective-permute-start(f32[4,1536]{1,0:T(4,128)S(1)} %get-tuple-element.26.stat_ref.refs_4_), channel_id=1, source_target_pairs={{0,1},{1,0},{2,3},{3,2},{4,5},{5,4},{6,7},{7,6},{8,9},{9,8},{10,11... | collective-permute-start | bytes 73736 | tf_op jit(solution)/shard_map/ppermute | solution.py:265
  35.0 3.8 %collective-permute-done.5.other_stat_ref.refs_5_ = f32[4,1536]{1,0:T(4,128)S(1)} collective-permute-done((f32[4,1536]{1,0:T(4,128)S(1)}, f32[4,1536]{1,0:T(4,128)S(1)}, u32[]{:S(2)}, u32[]{:S(2)}) %collective-permute-start.5) | collective-permute-done | bytes 24608 | tf_op jit(solution)/shard_map/ppermute | solution.py:265
  38.8 1.8 %shard_map.98 = (bf16[768,128]{1,0:T(8,128)(2,1)S(1)}, f32[128,1536]{1,0:T(8,128)S(1)}) custom-call(bf16[1536,128]{1,0:T(8,128)(2,1)S(1)} %copy-done, bf16[1536,128]{1,0:T(8,128)(2,1)S(1)} %collective-permute-done.refs_1_, f32[4,384,768]{2,1,0:T(8,128)S(1)} %shard_map.94.refs_2_, bf16[768,128]{1,0:T(8,128)(2,1)S(1)} %collective-permute-done.3.refs_3_, ...), custom_call_target="tpu_custom_call" | custom-call | flops 754974720 | bytes 4194304 | tf_op jit(solution)/shard_map/pallas_call | solution.py:337
  40.6 1.8 %shard_map.99 = (bf16[768,128]{1,0:T(8,128)(2,1)S(1)}, f32[128,1536]{1,0:T(8,128)S(1)}) custom-call(bf16[1536,128]{1,0:T(8,128)(2,1)S(1)} %copy-done, bf16[1536,128]{1,0:T(8,128)(2,1)S(1)} %collective-permute-done.refs_1_, f32[4,384,768]{2,1,0:T(8,128)S(1)} %shard_map.94.refs_2_, bf16[768,128]{1,0:T(8,128)(2,1)S(1)} %collective-permute-done.4.refs_4_.refs_3_, ...), custom_call_target="tpu_custom_call" | custom-call | flops 754974720 | bytes 4194304 | tf_op jit(solution)/shard_map/pallas_call | solution.py:337
  42.5 1.8 %shard_map.100 = (bf16[768,128]{1,0:T(8,128)(2,1)S(1)}, f32[128,1536]{1,0:T(8,128)S(1)}) custom-call(bf16[1536,128]{1,0:T(8,128)(2,1)S(1)} %copy-done, bf16[1536,128]{1,0:T(8,128)(2,1)S(1)} %collective-permute-done.refs_1_, f32[4,384,768]{2,1,0:T(8,128)S(1)} %shard_map.94.refs_2_, bf16[768,128]{1,0:T(8,128)(2,1)S(1)} %collective-permute-done.1.refs_3_, ...), custom_call_target="tpu_custom_call" | custom-call | flops 754974720 | bytes 4194304 | tf_op jit(solution)/shard_map/pallas_call | solution.py:337
  44.3 1.8 %shard_map.101 = (bf16[768,128]{1,0:T(8,128)(2,1)S(1)}, f32[128,1536]{1,0:T(8,128)S(1)}, bf16[128,768]{1,0:T(8,128)(2,1)S(1)}) custom-call(bf16[1536,128]{1,0:T(8,128)(2,1)S(1)} %copy-done, bf16[1536,128]{1,0:T(8,128)(2,1)S(1)} %collective-permute-done.refs_1_, f32[4,384,768]{2,1,0:T(8,128)S(1)} %shard_map.94.refs_2_, ...), custom_call_target="tpu_custom_call" | custom-call | flops 754974720 | bytes 4194304 | tf_op jit(solution)/shard_map/pallas_call | solution.py:337
  46.1 0.7 collective-permute-start.11
  46.8 3.9 %collective-permute-start.10 = (bf16[768,128]{1,0:T(8,128)(2,1)S(1)}, bf16[768,128]{1,0:T(8,128)(2,1)S(1)}, u32[]{:S(2)}, u32[]{:S(2)}) collective-permute-start(bf16[768,128]{1,0:T(8,128)(2,1)S(1)} %get-tuple-element.36), channel_id=1, source_target_pairs={{64,0},{66,2},{68,4},{70,6},{72,8},{74,10},{76,12},{78,14},{80,16}... | collective-permute-start | bytes 589832 | tf_op jit(solution)/shard_map/ppermute | solution.py:265
  50.7 1.3 %collective-permute-start.9 = (bf16[768,128]{1,0:T(8,128)(2,1)S(1)}, bf16[768,128]{1,0:T(8,128)(2,1)S(1)}, u32[]{:S(2)}, u32[]{:S(2)}) collective-permute-start(bf16[768,128]{1,0:T(8,128)(2,1)S(1)} %get-tuple-element.35), channel_id=1, source_target_pairs={{16,0},{18,2},{20,4},{22,6},{24,8},{26,10},{28,12},{30,14},{32,16}... | collective-permute-start | bytes 589832 | tf_op jit(solution)/shard_map/ppermute | solution.py:265
  52.0 4.5 %collective-permute-start.8 = (bf16[768,128]{1,0:T(8,128)(2,1)S(1)}, bf16[768,128]{1,0:T(8,128)(2,1)S(1)}, u32[]{:S(2)}, u32[]{:S(2)}) collective-permute-start(bf16[768,128]{1,0:T(8,128)(2,1)S(1)} %get-tuple-element.34), channel_id=1, source_target_pairs={{256,0},{258,2},{260,4},{262,6},{264,8},{266,10},{268,12},{270,14}... | collective-permute-start | bytes 589832 | tf_op jit(solution)/shard_map/ppermute | solution.py:265
  56.5 0.0 collective-permute-done.11.refs_3_
  56.5 0.1 collective-permute-done.10.refs_2_
  56.6 14.4 %collective-permute-done.9.refs_1_ = bf16[768,128]{1,0:T(8,128)(2,1)S(1)} collective-permute-done((bf16[768,128]{1,0:T(8,128)(2,1)S(1)}, bf16[768,128]{1,0:T(8,128)(2,1)S(1)}, u32[]{:S(2)}, u32[]{:S(2)}) %collective-permute-start.9) | collective-permute-done | bytes 196640 | tf_op jit(solution)/shard_map/ppermute | solution.py:265
  71.0 0.0 collective-permute-done.8.refs_0_
  71.0 0.1 shard_map.103.refs_0_
  71.1 1.9 %collective-permute-start.12 = (bf16[768,128]{1,0:T(8,128)(2,1)S(1)}, bf16[768,128]{1,0:T(8,128)(2,1)S(1)}, u32[]{:S(2)}, u32[]{:S(2)}) collective-permute-start(bf16[768,128]{1,0:T(8,128)(2,1)S(1)} %shard_map.103.refs_0_), channel_id=1, source_target_pairs={{0,1},{1,0},{2,3},{3,2},{4,5},{5,4},{6,7},{7,6},{8,9},{9,8},{10,11... | collective-permute-start | bytes 589832 | tf_op jit(solution)/shard_map/ppermute | solution.py:265
  73.1 3.9 %collective-permute-start.6 = (bf16[128,768]{1,0:T(8,128)(2,1)S(1)}, bf16[128,768]{1,0:T(8,128)(2,1)S(1)}, u32[]{:S(2)}, u32[]{:S(2)}) collective-permute-start(bf16[128,768]{1,0:T(8,128)(2,1)S(1)} %get-tuple-element.28), channel_id=1, source_target_pairs={{0,1},{1,0},{2,3},{3,2},{4,5},{5,4},{6,7},{7,6},{8,9},{9,8},{10,11... | collective-permute-start | bytes 589832 | tf_op jit(solution)/shard_map/ppermute | solution.py:265
  77.0 1.9 %collective-permute-start.7 = (bf16[128,768]{1,0:T(8,128)(2,1)S(1)}, bf16[128,768]{1,0:T(8,128)(2,1)S(1)}, u32[]{:S(2)}, u32[]{:S(2)}) collective-permute-start(bf16[128,768]{1,0:T(8,128)(2,1)S(1)} %get-tuple-element.33), channel_id=1, source_target_pairs={{0,1},{1,0},{2,3},{3,2},{4,5},{5,4},{6,7},{7,6},{8,9},{9,8},{10,11... | collective-permute-start | bytes 589832 | tf_op jit(solution)/shard_map/ppermute | solution.py:265
  78.9 1.9 %collective-permute-done.12.refs_1_ = bf16[768,128]{1,0:T(8,128)(2,1)S(1)} collective-permute-done((bf16[768,128]{1,0:T(8,128)(2,1)S(1)}, bf16[768,128]{1,0:T(8,128)(2,1)S(1)}, u32[]{:S(2)}, u32[]{:S(2)}) %collective-permute-start.12) | collective-permute-done | bytes 196640 | tf_op jit(solution)/shard_map/ppermute | solution.py:265
  80.8 1.9 %collective-permute-start.13 = (bf16[768,128]{1,0:T(8,128)(2,1)S(1)}, bf16[768,128]{1,0:T(8,128)(2,1)S(1)}, u32[]{:S(2)}, u32[]{:S(2)}) collective-permute-start(bf16[768,128]{1,0:T(8,128)(2,1)S(1)} %shard_map.104.refs_0_), channel_id=1, source_target_pairs={{0,3},{1,2},{2,1},{3,0},{4,7},{5,6},{6,5},{7,4},{8,11},{9,10},{10,... | collective-permute-start | bytes 589832 | tf_op jit(solution)/shard_map/ppermute | solution.py:265
  82.8 2.2 %collective-permute-done.6.got_ref = bf16[128,768]{1,0:T(8,128)(2,1)S(1)} collective-permute-done((bf16[128,768]{1,0:T(8,128)(2,1)S(1)}, bf16[128,768]{1,0:T(8,128)(2,1)S(1)}, u32[]{:S(2)}, u32[]{:S(2)}) %collective-permute-start.6) | collective-permute-done | bytes 196640 | tf_op jit(solution)/shard_map/ppermute | solution.py:265
  85.0 0.8 shard_map.97
  85.8 2.1 %collective-permute-done.7.got_ref = bf16[128,768]{1,0:T(8,128)(2,1)S(1)} collective-permute-done((bf16[128,768]{1,0:T(8,128)(2,1)S(1)}, bf16[128,768]{1,0:T(8,128)(2,1)S(1)}, u32[]{:S(2)}, u32[]{:S(2)}) %collective-permute-start.7) | collective-permute-done | bytes 196640 | tf_op jit(solution)/shard_map/ppermute | solution.py:265
  88.0 0.8 shard_map.102
  88.8 0.8 collective-permute-done.13.refs_1_
  89.6 0.7 shard_map.105
  (1 shorter events, 0.0 us)
Async XLA Ops:
  2.6 24.5 %copy-start = (bf16[1536,128]{1,0:T(8,128)(2,1)S(1)}, bf16[1536,128]{1,0:T(8,128)(2,1)}, u32[]{:S(2)}) copy-start(bf16[1536,128]{1,0:T(8,128)(2,1)} %get-tuple-element.22.refs_0_) | copy-start | bytes 1179652
  2.6 24.5 %collective-permute-start = (bf16[1536,128]{1,0:T(8,128)(2,1)}, bf16[1536,128]{1,0:T(8,128)(2,1)S(1)}, u32[]{:S(2)}, u32[]{:S(2)}) collective-permute-start(bf16[1536,128]{1,0:T(8,128)(2,1)} %get-tuple-element.22.refs_0_), channel_id=1, source_target_pairs={{0,1},{1,0},{2,3},{3,2},{4,5},{5,4},{6,7},{7,6},{8,9},{9,8},{10,11... | collective-permute-start | bytes 1179656 | tf_op jit(solution)/shard_map/ppermute | solution.py:265
  5.5 21.6 %collective-permute-start.4 = (bf16[768,128]{1,0:T(8,128)(2,1)}, bf16[768,128]{1,0:T(8,128)(2,1)S(1)}, u32[]{:S(2)}, u32[]{:S(2)}) collective-permute-start(bf16[768,128]{1,0:T(8,128)(2,1)} %get-tuple-element.23), channel_id=1, source_target_pairs={{0,16},{2,18},{4,20},{6,22},{8,24},{10,26},{12,28},{14,30},{16,32}... | collective-permute-start | bytes 589832 | tf_op jit(solution)/shard_map/ppermute | solution.py:265
  11.6 15.5 %collective-permute-start.3 = (bf16[768,128]{1,0:T(8,128)(2,1)}, bf16[768,128]{1,0:T(8,128)(2,1)S(1)}, u32[]{:S(2)}, u32[]{:S(2)}) collective-permute-start(bf16[768,128]{1,0:T(8,128)(2,1)} %get-tuple-element.23), channel_id=1, source_target_pairs={{0,256},{2,258},{4,260},{6,262},{8,264},{10,266},{12,268},{14,270}... | collective-permute-start | bytes 589832 | tf_op jit(solution)/shard_map/ppermute | solution.py:265
  18.1 11.1 %collective-permute-start.2 = (bf16[768,128]{1,0:T(8,128)(2,1)}, bf16[768,128]{1,0:T(8,128)(2,1)S(1)}, u32[]{:S(2)}, u32[]{:S(2)}) collective-permute-start(bf16[768,128]{1,0:T(8,128)(2,1)} %get-tuple-element.23), channel_id=1, source_target_pairs={{0,4},{2,6},{4,8},{6,10},{8,12},{10,14},{12,16},{14,18},{16,20},{1... | collective-permute-start | bytes 589832 | tf_op jit(solution)/shard_map/ppermute | solution.py:265
  19.7 11.3 %collective-permute-start.1 = (bf16[768,128]{1,0:T(8,128)(2,1)}, bf16[768,128]{1,0:T(8,128)(2,1)S(1)}, u32[]{:S(2)}, u32[]{:S(2)}) collective-permute-start(bf16[768,128]{1,0:T(8,128)(2,1)} %get-tuple-element.23), channel_id=1, source_target_pairs={{0,64},{2,66},{4,68},{6,70},{8,72},{10,74},{12,76},{14,78},{16,80}... | collective-permute-start | bytes 589832 | tf_op jit(solution)/shard_map/ppermute | solution.py:265
  24.4 0.7 copy-start.1
  25.1 0.7 copy-start.2
  33.1 5.7 %collective-permute-start.5 = (f32[4,1536]{1,0:T(4,128)S(1)}, f32[4,1536]{1,0:T(4,128)S(1)}, u32[]{:S(2)}, u32[]{:S(2)}) collective-permute-start(f32[4,1536]{1,0:T(4,128)S(1)} %get-tuple-element.26.stat_ref.refs_4_), channel_id=1, source_target_pairs={{0,1},{1,0},{2,3},{3,2},{4,5},{5,4},{6,7},{7,6},{8,9},{9,8},{10,11... | collective-permute-start | bytes 73736 | tf_op jit(solution)/shard_map/ppermute | solution.py:265
  46.1 10.4 %collective-permute-start.11 = (bf16[768,128]{1,0:T(8,128)(2,1)S(1)}, bf16[768,128]{1,0:T(8,128)(2,1)S(1)}, u32[]{:S(2)}, u32[]{:S(2)}) collective-permute-start(bf16[768,128]{1,0:T(8,128)(2,1)S(1)} %get-tuple-element.37), channel_id=1, source_target_pairs={{4,0},{6,2},{8,4},{10,6},{12,8},{14,10},{16,12},{18,14},{20,16},{2... | collective-permute-start | bytes 589832 | tf_op jit(solution)/shard_map/ppermute | solution.py:265
  46.8 9.8 %collective-permute-start.10 = (bf16[768,128]{1,0:T(8,128)(2,1)S(1)}, bf16[768,128]{1,0:T(8,128)(2,1)S(1)}, u32[]{:S(2)}, u32[]{:S(2)}) collective-permute-start(bf16[768,128]{1,0:T(8,128)(2,1)S(1)} %get-tuple-element.36), channel_id=1, source_target_pairs={{64,0},{66,2},{68,4},{70,6},{72,8},{74,10},{76,12},{78,14},{80,16}... | collective-permute-start | bytes 589832 | tf_op jit(solution)/shard_map/ppermute | solution.py:265
  50.7 20.3 %collective-permute-start.9 = (bf16[768,128]{1,0:T(8,128)(2,1)S(1)}, bf16[768,128]{1,0:T(8,128)(2,1)S(1)}, u32[]{:S(2)}, u32[]{:S(2)}) collective-permute-start(bf16[768,128]{1,0:T(8,128)(2,1)S(1)} %get-tuple-element.35), channel_id=1, source_target_pairs={{16,0},{18,2},{20,4},{22,6},{24,8},{26,10},{28,12},{30,14},{32,16}... | collective-permute-start | bytes 589832 | tf_op jit(solution)/shard_map/ppermute | solution.py:265
  52.0 19.0 %collective-permute-start.8 = (bf16[768,128]{1,0:T(8,128)(2,1)S(1)}, bf16[768,128]{1,0:T(8,128)(2,1)S(1)}, u32[]{:S(2)}, u32[]{:S(2)}) collective-permute-start(bf16[768,128]{1,0:T(8,128)(2,1)S(1)} %get-tuple-element.34), channel_id=1, source_target_pairs={{256,0},{258,2},{260,4},{262,6},{264,8},{266,10},{268,12},{270,14}... | collective-permute-start | bytes 589832 | tf_op jit(solution)/shard_map/ppermute | solution.py:265
  71.1 9.7 %collective-permute-start.12 = (bf16[768,128]{1,0:T(8,128)(2,1)S(1)}, bf16[768,128]{1,0:T(8,128)(2,1)S(1)}, u32[]{:S(2)}, u32[]{:S(2)}) collective-permute-start(bf16[768,128]{1,0:T(8,128)(2,1)S(1)} %shard_map.103.refs_0_), channel_id=1, source_target_pairs={{0,1},{1,0},{2,3},{3,2},{4,5},{5,4},{6,7},{7,6},{8,9},{9,8},{10,11... | collective-permute-start | bytes 589832 | tf_op jit(solution)/shard_map/ppermute | solution.py:265
  73.1 12.0 %collective-permute-start.6 = (bf16[128,768]{1,0:T(8,128)(2,1)S(1)}, bf16[128,768]{1,0:T(8,128)(2,1)S(1)}, u32[]{:S(2)}, u32[]{:S(2)}) collective-permute-start(bf16[128,768]{1,0:T(8,128)(2,1)S(1)} %get-tuple-element.28), channel_id=1, source_target_pairs={{0,1},{1,0},{2,3},{3,2},{4,5},{5,4},{6,7},{7,6},{8,9},{9,8},{10,11... | collective-permute-start | bytes 589832 | tf_op jit(solution)/shard_map/ppermute | solution.py:265
  77.0 11.0 %collective-permute-start.7 = (bf16[128,768]{1,0:T(8,128)(2,1)S(1)}, bf16[128,768]{1,0:T(8,128)(2,1)S(1)}, u32[]{:S(2)}, u32[]{:S(2)}) collective-permute-start(bf16[128,768]{1,0:T(8,128)(2,1)S(1)} %get-tuple-element.33), channel_id=1, source_target_pairs={{0,1},{1,0},{2,3},{3,2},{4,5},{5,4},{6,7},{7,6},{8,9},{9,8},{10,11... | collective-permute-start | bytes 589832 | tf_op jit(solution)/shard_map/ppermute | solution.py:265
  80.8 8.8 %collective-permute-start.13 = (bf16[768,128]{1,0:T(8,128)(2,1)S(1)}, bf16[768,128]{1,0:T(8,128)(2,1)S(1)}, u32[]{:S(2)}, u32[]{:S(2)}) collective-permute-start(bf16[768,128]{1,0:T(8,128)(2,1)S(1)} %shard_map.104.refs_0_), channel_id=1, source_target_pairs={{0,3},{1,2},{2,1},{3,0},{4,7},{5,6},{6,5},{7,4},{8,11},{9,10},{10,... | collective-permute-start | bytes 589832 | tf_op jit(solution)/shard_map/ppermute | solution.py:265

commit v4 on v3

--- a/solution.py
+++ b/solution.py
@@ -18,7 +18,7 @@
 BF16 = jnp.bfloat16
 
 TABLES = {
-    128: ((64, 8), (4, 32), (16, 2), (1, 0)),
+    128: ((64, 32), (8, 4), (16, 2), (1, 0)),
     16: ((8, 2), (4, 1), (None, None), (None, 0)),
 }
 
@@ -35,17 +35,31 @@
     )
 
 
-def pack_kernel(key_ref, value_ref, query_ref, grad_ref, kv_ref, qg_ref, sems):
+def pack_kernel(key_ref, value_ref, query_ref, grad_ref, kv_ref, qg_ref, *scratch):
+    buffers, sems = scratch[:4], scratch[4]
     rows, wide = key_ref.shape[0], query_ref.shape[0]
-    copies = [
-        pltpu.make_async_copy(key_ref, kv_ref.at[pl.ds(0, rows)], sems.at[0]),
-        pltpu.make_async_copy(value_ref, kv_ref.at[pl.ds(rows, rows)], sems.at[1]),
-        pltpu.make_async_copy(query_ref, qg_ref.at[pl.ds(0, wide)], sems.at[2]),
-        pltpu.make_async_copy(grad_ref, qg_ref.at[pl.ds(wide, wide)], sems.at[3]),
+    targets = (
+        kv_ref.at[pl.ds(0, rows)],
+        kv_ref.at[pl.ds(rows, rows)],
+        qg_ref.at[pl.ds(0, wide)],
+        qg_ref.at[pl.ds(wide, wide)],
+    )
+    inward = [
+        pltpu.make_async_copy(source, buffer, sems.at[index])
+        for index, (source, buffer) in enumerate(
+            zip((key_ref, value_ref, query_ref, grad_ref), buffers)
+        )
     ]
-    for copy in copies:
+    outward = [
+        pltpu.make_async_copy(buffer, target, sems.at[4 + index])
+        for index, (buffer, target) in enumerate(zip(buffers, targets))
+    ]
+    for copy in inward:
         copy.start()
-    for copy in copies:
+    for copy, follow in zip(inward, outward):
+        copy.wait()
+        follow.start()
+    for copy in outward:
         copy.wait()
 
 
@@ -273,8 +287,14 @@
         pack_kernel,
         out_shape=(kv_shape, qg_shape),
         in_specs=[HBM] * 4,
-        out_specs=(VMEM, VMEM),
-        scratch_shapes=[pltpu.SemaphoreType.DMA((4,))],
+        out_specs=(HBM, HBM),
+        scratch_shapes=[
+            pltpu.VMEM((rows, dim), BF16),
+            pltpu.VMEM((rows, dim), BF16),
+            pltpu.VMEM((rows * heads, dim), BF16),
+            pltpu.VMEM((rows * heads, dim), BF16),
+            pltpu.SemaphoreType.DMA((8,)),
+        ],
         compiler_params=pltpu.CompilerParams(vmem_limit_bytes=67043328),
     )(
         key_rows,
@@ -320,8 +340,8 @@
             rows * columns * len(slots),
         )(*args)
 
-    stat, out = forward((0, 1), None, False)
-    stat, out, other_out = forward((2, 3), (stat, out), True)
+    stat, out = forward((0, 1, 3), None, False)
+    stat, out, other_out = forward((2,), (stat, out), True)
     other_stat = send(stat, near)
     got_out = send(other_out, near)
 
@@ -346,9 +366,9 @@
         return call(kernel, shapes, [VMEM] * len(pieces), 0, 1 << 20, 0)(*pieces)
 
     total = add(returned, (kv_shape,))[0]
-    total = add((total, send(total, near)), (kv_shape,))[0]
+    total = add((total, send(total, far)), (kv_shape,))[0]
     key_shape = jax.ShapeDtypeStruct((rows, dim), BF16)
-    grad_keys, grad_values = add((total, send(total, far)), (key_shape, key_shape))
+    grad_keys, grad_values = add((total, send(total, near)), (key_shape, key_shape))
 
     flat = jax.ShapeDtypeStruct((heads * rows, dim), BF16)
     attn = call(finish_out_kernel, flat, [VMEM] * 4, 0, 1 << 20, 0)(

time: 90.8 us -> 96.6 us (1.064)
  the two profiles are of different devices: /device:TPU:62 before, /device:TPU:114 now
where the time goes in v4:
time: 96.6 us; the launch traced here: 96.1 us
  starting transfers between devices  59.1 us (61%)
  waiting for transfers between devices  17.6 us (18%)
  Pallas kernels  17.2 us (18%)
  local copies, waits for them, and re-layouts  1.35 us (1%)
    ppermute x14, starting transfers between devices, send(): return lax.ppermute(value, AXES, pairs)  59.1 us
    ppermute x14, waiting for transfers between devices, send(): return lax.ppermute(value, AXES, pairs)  17.6 us
    pallas_call x4, Pallas kernels, local(): call(kernel, shapes, [VMEM] * len(args), 5 * unit, 4 << 20, rows * columns)  7.29 us
    pallas_call x2, Pallas kernels, forward(): call(kernel, (stat_shape, wide_shape) + ((send_shape,) if last else ()),...  4.2 us
  transfers between devices with their start and end apart: 14, of which 6 were waited for; matrix products, arithmetic and copies ran while one was open for 0% of the time, Pallas kernels for 6%

profile of v4, /device:TPU:114, one launch (start us, length us, event | category | flops | bytes accessed | tf_op | source)
XLA Modules:
  0.0 96.1 jit_solution(681112179406987570)
XLA Ops:
  0.6 1.9 %shard_map.93 = (bf16[768,128]{1,0:T(8,128)(2,1)}, bf16[1536,128]{1,0:T(8,128)(2,1)}) custom-call(bf16[384,128]{1,0:T(8,128)(2,1)} %key_ref.1, bf16[384,128]{1,0:T(8,128)(2,1)} %value_ref.1, bf16[768,128]{1,0:T(8,128)(2,1)} %bitcast.6, bf16[768,128]{1,0:T(8,128)(2,1)} %bitcast.7), custom_call_target="tpu_custom_call" | custom-call | tf_op jit(solution)/shard_map/pallas_call | solution.py:286
  2.5 0.0 copy-start
  2.5 2.6 %collective-permute-start = (bf16[1536,128]{1,0:T(8,128)(2,1)}, bf16[1536,128]{1,0:T(8,128)(2,1)S(1)}, u32[]{:S(2)}, u32[]{:S(2)}) collective-permute-start(bf16[1536,128]{1,0:T(8,128)(2,1)} %get-tuple-element.22.refs_0_), channel_id=1, source_target_pairs={{0,1},{1,0},{2,3},{3,2},{4,5},{5,4},{6,7},{7,6},{8,9},{9,8},{10,11... | collective-permute-start | bytes 1179656 | tf_op jit(solution)/shard_map/ppermute | solution.py:279
  5.1 1.6 %collective-permute-start.4 = (bf16[768,128]{1,0:T(8,128)(2,1)}, bf16[768,128]{1,0:T(8,128)(2,1)S(1)}, u32[]{:S(2)}, u32[]{:S(2)}) collective-permute-start(bf16[768,128]{1,0:T(8,128)(2,1)} %get-tuple-element.23), channel_id=1, source_target_pairs={{0,4},{2,6},{4,8},{6,10},{8,12},{10,14},{12,16},{14,18},{16,20},{1... | collective-permute-start | bytes 589832 | tf_op jit(solution)/shard_map/ppermute | solution.py:279
  6.7 3.6 %collective-permute-start.3 = (bf16[768,128]{1,0:T(8,128)(2,1)}, bf16[768,128]{1,0:T(8,128)(2,1)S(1)}, u32[]{:S(2)}, u32[]{:S(2)}) collective-permute-start(bf16[768,128]{1,0:T(8,128)(2,1)} %get-tuple-element.23), channel_id=1, source_target_pairs={{0,32},{2,34},{4,36},{6,38},{8,40},{10,42},{12,44},{14,46},{16,48}... | collective-permute-start | bytes 589832 | tf_op jit(solution)/shard_map/ppermute | solution.py:279
  10.3 7.3 %collective-permute-start.2 = (bf16[768,128]{1,0:T(8,128)(2,1)}, bf16[768,128]{1,0:T(8,128)(2,1)S(1)}, u32[]{:S(2)}, u32[]{:S(2)}) collective-permute-start(bf16[768,128]{1,0:T(8,128)(2,1)} %get-tuple-element.23), channel_id=1, source_target_pairs={{0,256},{2,258},{4,260},{6,262},{8,264},{10,266},{12,268},{14,270}... | collective-permute-start | bytes 589832 | tf_op jit(solution)/shard_map/ppermute | solution.py:279
  17.6 3.5 %collective-permute-start.1 = (bf16[768,128]{1,0:T(8,128)(2,1)}, bf16[768,128]{1,0:T(8,128)(2,1)S(1)}, u32[]{:S(2)}, u32[]{:S(2)}) collective-permute-start(bf16[768,128]{1,0:T(8,128)(2,1)} %get-tuple-element.23), channel_id=1, source_target_pairs={{0,64},{2,66},{4,68},{6,70},{8,72},{10,74},{12,76},{14,78},{16,80}... | collective-permute-start | bytes 589832 | tf_op jit(solution)/shard_map/ppermute | solution.py:279
  21.1 0.0 copy-start.1
  21.1 0.7 copy-done.1
  21.8 0.0 copy-start.2
  21.8 0.7 copy-done.2
  22.4 1.3 %shard_map.94.refs_2_ = f32[4,384,768]{2,1,0:T(8,128)S(1)} custom-call(s32[64]{0:T(128)S(1)} %copy-done.2, s32[3,384]{1,0:T(4,128)S(1)} %copy-done.1), custom_call_target="tpu_custom_call" | custom-call | tf_op jit(solution)/shard_map/pallas_call | solution.py:310
  23.8 0.0 collective-permute-done.4.refs_5_.refs_3_
  23.8 0.0 collective-permute-done.3.refs_4_.refs_3_
  23.8 0.0 collective-permute-done.2.refs_3_
  23.8 0.0 collective-permute-done.refs_1_
  23.8 0.0 copy-done
  23.8 3.0 %shard_map.95 = (f32[4,1536]{1,0:T(4,128)S(1)}, f32[128,1536]{1,0:T(8,128)S(1)}) custom-call(bf16[1536,128]{1,0:T(8,128)(2,1)S(1)} %copy-done, bf16[1536,128]{1,0:T(8,128)(2,1)S(1)} %collective-permute-done.refs_1_, f32[4,384,768]{2,1,0:T(8,128)S(1)} %shard_map.94.refs_2_, bf16[768,128]{1,0:T(8,128)(2,1)S(1)} %collective-permute-done.2.refs_3_, ...), custom_call_target="tpu_custom_call" | custom-call | flops 905969664 | bytes 4194304 | tf_op jit(solution)/shard_map/pallas_call | solution.py:334
  26.8 0.0 collective-permute-done.1.refs_3_
  26.9 1.2 %shard_map.96 = (f32[4,1536]{1,0:T(4,128)S(1)}, f32[128,1536]{1,0:T(8,128)S(1)}, bf16[128,768]{1,0:T(8,128)(2,1)S(1)}) custom-call(bf16[1536,128]{1,0:T(8,128)(2,1)S(1)} %copy-done, bf16[1536,128]{1,0:T(8,128)(2,1)S(1)} %collective-permute-done.refs_1_, f32[4,384,768]{2,1,0:T(8,128)S(1)} %shard_map.94.refs_2_, ...), custom_call_target="tpu_custom_call" | custom-call | flops 301989888 | bytes 4194304 | tf_op jit(solution)/shard_map/pallas_call | solution.py:334
  28.0 8.6 %collective-permute-start.5 = (f32[4,1536]{1,0:T(4,128)S(1)}, f32[4,1536]{1,0:T(4,128)S(1)}, u32[]{:S(2)}, u32[]{:S(2)}) collective-permute-start(f32[4,1536]{1,0:T(4,128)S(1)} %get-tuple-element.26.stat_ref.refs_4_), channel_id=1, source_target_pairs={{0,1},{1,0},{2,3},{3,2},{4,5},{5,4},{6,7},{7,6},{8,9},{9,8},{10,11... | collective-permute-start | bytes 73736 | tf_op jit(solution)/shard_map/ppermute | solution.py:279
  36.7 1.8 %collective-permute-done.5.other_stat_ref.refs_5_ = f32[4,1536]{1,0:T(4,128)S(1)} collective-permute-done((f32[4,1536]{1,0:T(4,128)S(1)}, f32[4,1536]{1,0:T(4,128)S(1)}, u32[]{:S(2)}, u32[]{:S(2)}) %collective-permute-start.5) | collective-permute-done | bytes 24608 | tf_op jit(solution)/shard_map/ppermute | solution.py:279
  38.5 1.8 %shard_map.98 = (bf16[768,128]{1,0:T(8,128)(2,1)S(1)}, f32[128,1536]{1,0:T(8,128)S(1)}) custom-call(bf16[1536,128]{1,0:T(8,128)(2,1)S(1)} %copy-done, bf16[1536,128]{1,0:T(8,128)(2,1)S(1)} %collective-permute-done.refs_1_, f32[4,384,768]{2,1,0:T(8,128)S(1)} %shard_map.94.refs_2_, bf16[768,128]{1,0:T(8,128)(2,1)S(1)} %collective-permute-done.2.refs_3_, ...), custom_call_target="tpu_custom_call" | custom-call | flops 754974720 | bytes 4194304 | tf_op jit(solution)/shard_map/pallas_call | solution.py:357
  40.3 1.8 %shard_map.99 = (bf16[768,128]{1,0:T(8,128)(2,1)S(1)}, f32[128,1536]{1,0:T(8,128)S(1)}) custom-call(bf16[1536,128]{1,0:T(8,128)(2,1)S(1)} %copy-done, bf16[1536,128]{1,0:T(8,128)(2,1)S(1)} %collective-permute-done.refs_1_, f32[4,384,768]{2,1,0:T(8,128)S(1)} %shard_map.94.refs_2_, bf16[768,128]{1,0:T(8,128)(2,1)S(1)} %collective-permute-done.3.refs_4_.refs_3_, ...), custom_call_target="tpu_custom_call" | custom-call | flops 754974720 | bytes 4194304 | tf_op jit(solution)/shard_map/pallas_call | solution.py:357
  42.1 1.8 %shard_map.100 = (bf16[768,128]{1,0:T(8,128)(2,1)S(1)}, f32[128,1536]{1,0:T(8,128)S(1)}) custom-call(bf16[1536,128]{1,0:T(8,128)(2,1)S(1)} %copy-done, bf16[1536,128]{1,0:T(8,128)(2,1)S(1)} %collective-permute-done.refs_1_, f32[4,384,768]{2,1,0:T(8,128)S(1)} %shard_map.94.refs_2_, bf16[768,128]{1,0:T(8,128)(2,1)S(1)} %collective-permute-done.1.refs_3_, ...), custom_call_target="tpu_custom_call" | custom-call | flops 754974720 | bytes 4194304 | tf_op jit(solution)/shard_map/pallas_call | solution.py:357
  44.0 1.8 %shard_map.101 = (bf16[768,128]{1,0:T(8,128)(2,1)S(1)}, f32[128,1536]{1,0:T(8,128)S(1)}, bf16[128,768]{1,0:T(8,128)(2,1)S(1)}) custom-call(bf16[1536,128]{1,0:T(8,128)(2,1)S(1)} %copy-done, bf16[1536,128]{1,0:T(8,128)(2,1)S(1)} %collective-permute-done.refs_1_, f32[4,384,768]{2,1,0:T(8,128)S(1)} %shard_map.94.refs_2_, ...), custom_call_target="tpu_custom_call" | custom-call | flops 754974720 | bytes 4194304 | tf_op jit(solution)/shard_map/pallas_call | solution.py:357
  45.8 0.7 collective-permute-start.11
  46.5 2.4 %collective-permute-start.10 = (bf16[768,128]{1,0:T(8,128)(2,1)S(1)}, bf16[768,128]{1,0:T(8,128)(2,1)S(1)}, u32[]{:S(2)}, u32[]{:S(2)}) collective-permute-start(bf16[768,128]{1,0:T(8,128)(2,1)S(1)} %get-tuple-element.36), channel_id=1, source_target_pairs={{64,0},{66,2},{68,4},{70,6},{72,8},{74,10},{76,12},{78,14},{80,16}... | collective-permute-start | bytes 589832 | tf_op jit(solution)/shard_map/ppermute | solution.py:279
  48.8 6.6 %collective-permute-start.9 = (bf16[768,128]{1,0:T(8,128)(2,1)S(1)}, bf16[768,128]{1,0:T(8,128)(2,1)S(1)}, u32[]{:S(2)}, u32[]{:S(2)}) collective-permute-start(bf16[768,128]{1,0:T(8,128)(2,1)S(1)} %get-tuple-element.35), channel_id=1, source_target_pairs={{32,0},{34,2},{36,4},{38,6},{40,8},{42,10},{44,12},{46,14},{48,16}... | collective-permute-start | bytes 589832 | tf_op jit(solution)/shard_map/ppermute | solution.py:279
  55.4 1.3 %collective-permute-start.8 = (bf16[768,128]{1,0:T(8,128)(2,1)S(1)}, bf16[768,128]{1,0:T(8,128)(2,1)S(1)}, u32[]{:S(2)}, u32[]{:S(2)}) collective-permute-start(bf16[768,128]{1,0:T(8,128)(2,1)S(1)} %get-tuple-element.34), channel_id=1, source_target_pairs={{256,0},{258,2},{260,4},{262,6},{264,8},{266,10},{268,12},{270,14}... | collective-permute-start | bytes 589832 | tf_op jit(solution)/shard_map/ppermute | solution.py:279
  56.7 0.0 collective-permute-done.11.refs_3_
  56.7 0.0 collective-permute-done.10.refs_2_
  56.8 8.9 %collective-permute-done.9.refs_1_ = bf16[768,128]{1,0:T(8,128)(2,1)S(1)} collective-permute-done((bf16[768,128]{1,0:T(8,128)(2,1)S(1)}, bf16[768,128]{1,0:T(8,128)(2,1)S(1)}, u32[]{:S(2)}, u32[]{:S(2)}) %collective-permute-start.9) | collective-permute-done | bytes 196640 | tf_op jit(solution)/shard_map/ppermute | solution.py:279
  65.7 1.3 %collective-permute-done.8.refs_0_ = bf16[768,128]{1,0:T(8,128)(2,1)S(1)} collective-permute-done((bf16[768,128]{1,0:T(8,128)(2,1)S(1)}, bf16[768,128]{1,0:T(8,128)(2,1)S(1)}, u32[]{:S(2)}, u32[]{:S(2)}) %collective-permute-start.8) | collective-permute-done | bytes 196640 | tf_op jit(solution)/shard_map/ppermute | solution.py:279
  67.0 0.1 shard_map.103.refs_0_
  67.1 11.8 %collective-permute-start.12 = (bf16[768,128]{1,0:T(8,128)(2,1)S(1)}, bf16[768,128]{1,0:T(8,128)(2,1)S(1)}, u32[]{:S(2)}, u32[]{:S(2)}) collective-permute-start(bf16[768,128]{1,0:T(8,128)(2,1)S(1)} %shard_map.103.refs_0_), channel_id=1, source_target_pairs={{0,3},{1,2},{2,1},{3,0},{4,7},{5,6},{6,5},{7,4},{8,11},{9,10},{10,... | collective-permute-start | bytes 589832 | tf_op jit(solution)/shard_map/ppermute | solution.py:279
  78.9 1.9 %collective-permute-start.6 = (bf16[128,768]{1,0:T(8,128)(2,1)S(1)}, bf16[128,768]{1,0:T(8,128)(2,1)S(1)}, u32[]{:S(2)}, u32[]{:S(2)}) collective-permute-start(bf16[128,768]{1,0:T(8,128)(2,1)S(1)} %get-tuple-element.28), channel_id=1, source_target_pairs={{0,1},{1,0},{2,3},{3,2},{4,5},{5,4},{6,7},{7,6},{8,9},{9,8},{10,11... | collective-permute-start | bytes 589832 | tf_op jit(solution)/shard_map/ppermute | solution.py:279
  80.9 3.9 %collective-permute-start.7 = (bf16[128,768]{1,0:T(8,128)(2,1)S(1)}, bf16[128,768]{1,0:T(8,128)(2,1)S(1)}, u32[]{:S(2)}, u32[]{:S(2)}) collective-permute-start(bf16[128,768]{1,0:T(8,128)(2,1)S(1)} %get-tuple-element.33), channel_id=1, source_target_pairs={{0,1},{1,0},{2,3},{3,2},{4,5},{5,4},{6,7},{7,6},{8,9},{9,8},{10,11... | collective-permute-start | bytes 589832 | tf_op jit(solution)/shard_map/ppermute | solution.py:279
  84.8 0.0 collective-permute-done.12.refs_1_
  84.9 3.3 %collective-permute-start.13 = (bf16[768,128]{1,0:T(8,128)(2,1)S(1)}, bf16[768,128]{1,0:T(8,128)(2,1)S(1)}, u32[]{:S(2)}, u32[]{:S(2)}) collective-permute-start(bf16[768,128]{1,0:T(8,128)(2,1)S(1)} %shard_map.104.refs_0_), channel_id=1, source_target_pairs={{0,1},{1,0},{2,3},{3,2},{4,5},{5,4},{6,7},{7,6},{8,9},{9,8},{10,11... | collective-permute-start | bytes 589832 | tf_op jit(solution)/shard_map/ppermute | solution.py:279
  88.2 0.4 collective-permute-done.6.got_ref
  88.6 0.8 shard_map.97
  89.4 3.4 %collective-permute-done.7.got_ref = bf16[128,768]{1,0:T(8,128)(2,1)S(1)} collective-permute-done((bf16[128,768]{1,0:T(8,128)(2,1)S(1)}, bf16[128,768]{1,0:T(8,128)(2,1)S(1)}, u32[]{:S(2)}, u32[]{:S(2)}) %collective-permute-start.7) | collective-permute-done | bytes 196640 | tf_op jit(solution)/shard_map/ppermute | solution.py:279
  92.8 0.8 shard_map.102
  93.6 1.8 %collective-permute-done.13.refs_1_ = bf16[768,128]{1,0:T(8,128)(2,1)S(1)} collective-permute-done((bf16[768,128]{1,0:T(8,128)(2,1)S(1)}, bf16[768,128]{1,0:T(8,128)(2,1)S(1)}, u32[]{:S(2)}, u32[]{:S(2)}) %collective-permute-start.13) | collective-permute-done | bytes 196640 | tf_op jit(solution)/shard_map/ppermute | solution.py:279
  95.4 0.7 shard_map.105
  (1 shorter events, 0.0 us)
Async XLA Ops:
  2.5 21.3 %copy-start = (bf16[1536,128]{1,0:T(8,128)(2,1)S(1)}, bf16[1536,128]{1,0:T(8,128)(2,1)}, u32[]{:S(2)}) copy-start(bf16[1536,128]{1,0:T(8,128)(2,1)} %get-tuple-element.22.refs_0_) | copy-start | bytes 1179652
  2.5 21.3 %collective-permute-start = (bf16[1536,128]{1,0:T(8,128)(2,1)}, bf16[1536,128]{1,0:T(8,128)(2,1)S(1)}, u32[]{:S(2)}, u32[]{:S(2)}) collective-permute-start(bf16[1536,128]{1,0:T(8,128)(2,1)} %get-tuple-element.22.refs_0_), channel_id=1, source_target_pairs={{0,1},{1,0},{2,3},{3,2},{4,5},{5,4},{6,7},{7,6},{8,9},{9,8},{10,11... | collective-permute-start | bytes 1179656 | tf_op jit(solution)/shard_map/ppermute | solution.py:279
  5.1 18.7 %collective-permute-start.4 = (bf16[768,128]{1,0:T(8,128)(2,1)}, bf16[768,128]{1,0:T(8,128)(2,1)S(1)}, u32[]{:S(2)}, u32[]{:S(2)}) collective-permute-start(bf16[768,128]{1,0:T(8,128)(2,1)} %get-tuple-element.23), channel_id=1, source_target_pairs={{0,4},{2,6},{4,8},{6,10},{8,12},{10,14},{12,16},{14,18},{16,20},{1... | collective-permute-start | bytes 589832 | tf_op jit(solution)/shard_map/ppermute | solution.py:279
  6.7 17.1 %collective-permute-start.3 = (bf16[768,128]{1,0:T(8,128)(2,1)}, bf16[768,128]{1,0:T(8,128)(2,1)S(1)}, u32[]{:S(2)}, u32[]{:S(2)}) collective-permute-start(bf16[768,128]{1,0:T(8,128)(2,1)} %get-tuple-element.23), channel_id=1, source_target_pairs={{0,32},{2,34},{4,36},{6,38},{8,40},{10,42},{12,44},{14,46},{16,48}... | collective-permute-start | bytes 589832 | tf_op jit(solution)/shard_map/ppermute | solution.py:279
  10.3 13.5 %collective-permute-start.2 = (bf16[768,128]{1,0:T(8,128)(2,1)}, bf16[768,128]{1,0:T(8,128)(2,1)S(1)}, u32[]{:S(2)}, u32[]{:S(2)}) collective-permute-start(bf16[768,128]{1,0:T(8,128)(2,1)} %get-tuple-element.23), channel_id=1, source_target_pairs={{0,256},{2,258},{4,260},{6,262},{8,264},{10,266},{12,268},{14,270}... | collective-permute-start | bytes 589832 | tf_op jit(solution)/shard_map/ppermute | solution.py:279
  17.6 9.3 %collective-permute-start.1 = (bf16[768,128]{1,0:T(8,128)(2,1)}, bf16[768,128]{1,0:T(8,128)(2,1)S(1)}, u32[]{:S(2)}, u32[]{:S(2)}) collective-permute-start(bf16[768,128]{1,0:T(8,128)(2,1)} %get-tuple-element.23), channel_id=1, source_target_pairs={{0,64},{2,66},{4,68},{6,70},{8,72},{10,74},{12,76},{14,78},{16,80}... | collective-permute-start | bytes 589832 | tf_op jit(solution)/shard_map/ppermute | solution.py:279
  21.1 0.7 copy-start.1
  21.8 0.7 copy-start.2
  28.0 10.4 %collective-permute-start.5 = (f32[4,1536]{1,0:T(4,128)S(1)}, f32[4,1536]{1,0:T(4,128)S(1)}, u32[]{:S(2)}, u32[]{:S(2)}) collective-permute-start(f32[4,1536]{1,0:T(4,128)S(1)} %get-tuple-element.26.stat_ref.refs_4_), channel_id=1, source_target_pairs={{0,1},{1,0},{2,3},{3,2},{4,5},{5,4},{6,7},{7,6},{8,9},{9,8},{10,11... | collective-permute-start | bytes 73736 | tf_op jit(solution)/shard_map/ppermute | solution.py:279
  45.8 10.9 %collective-permute-start.11 = (bf16[768,128]{1,0:T(8,128)(2,1)S(1)}, bf16[768,128]{1,0:T(8,128)(2,1)S(1)}, u32[]{:S(2)}, u32[]{:S(2)}) collective-permute-start(bf16[768,128]{1,0:T(8,128)(2,1)S(1)} %get-tuple-element.37), channel_id=1, source_target_pairs={{4,0},{6,2},{8,4},{10,6},{12,8},{14,10},{16,12},{18,14},{20,16},{2... | collective-permute-start | bytes 589832 | tf_op jit(solution)/shard_map/ppermute | solution.py:279
  46.5 10.3 %collective-permute-start.10 = (bf16[768,128]{1,0:T(8,128)(2,1)S(1)}, bf16[768,128]{1,0:T(8,128)(2,1)S(1)}, u32[]{:S(2)}, u32[]{:S(2)}) collective-permute-start(bf16[768,128]{1,0:T(8,128)(2,1)S(1)} %get-tuple-element.36), channel_id=1, source_target_pairs={{64,0},{66,2},{68,4},{70,6},{72,8},{74,10},{76,12},{78,14},{80,16}... | collective-permute-start | bytes 589832 | tf_op jit(solution)/shard_map/ppermute | solution.py:279
  48.8 16.8 %collective-permute-start.9 = (bf16[768,128]{1,0:T(8,128)(2,1)S(1)}, bf16[768,128]{1,0:T(8,128)(2,1)S(1)}, u32[]{:S(2)}, u32[]{:S(2)}) collective-permute-start(bf16[768,128]{1,0:T(8,128)(2,1)S(1)} %get-tuple-element.35), channel_id=1, source_target_pairs={{32,0},{34,2},{36,4},{38,6},{40,8},{42,10},{44,12},{46,14},{48,16}... | collective-permute-start | bytes 589832 | tf_op jit(solution)/shard_map/ppermute | solution.py:279
  55.4 11.6 %collective-permute-start.8 = (bf16[768,128]{1,0:T(8,128)(2,1)S(1)}, bf16[768,128]{1,0:T(8,128)(2,1)S(1)}, u32[]{:S(2)}, u32[]{:S(2)}) collective-permute-start(bf16[768,128]{1,0:T(8,128)(2,1)S(1)} %get-tuple-element.34), channel_id=1, source_target_pairs={{256,0},{258,2},{260,4},{262,6},{264,8},{266,10},{268,12},{270,14}... | collective-permute-start | bytes 589832 | tf_op jit(solution)/shard_map/ppermute | solution.py:279
  67.1 17.7 %collective-permute-start.12 = (bf16[768,128]{1,0:T(8,128)(2,1)S(1)}, bf16[768,128]{1,0:T(8,128)(2,1)S(1)}, u32[]{:S(2)}, u32[]{:S(2)}) collective-permute-start(bf16[768,128]{1,0:T(8,128)(2,1)S(1)} %shard_map.103.refs_0_), channel_id=1, source_target_pairs={{0,3},{1,2},{2,1},{3,0},{4,7},{5,6},{6,5},{7,4},{8,11},{9,10},{10,... | collective-permute-start | bytes 589832 | tf_op jit(solution)/shard_map/ppermute | solution.py:279
  78.9 9.7 %collective-permute-start.6 = (bf16[128,768]{1,0:T(8,128)(2,1)S(1)}, bf16[128,768]{1,0:T(8,128)(2,1)S(1)}, u32[]{:S(2)}, u32[]{:S(2)}) collective-permute-start(bf16[128,768]{1,0:T(8,128)(2,1)S(1)} %get-tuple-element.28), channel_id=1, source_target_pairs={{0,1},{1,0},{2,3},{3,2},{4,5},{5,4},{6,7},{7,6},{8,9},{9,8},{10,11... | collective-permute-start | bytes 589832 | tf_op jit(solution)/shard_map/ppermute | solution.py:279
  80.9 12.0 %collective-permute-start.7 = (bf16[128,768]{1,0:T(8,128)(2,1)S(1)}, bf16[128,768]{1,0:T(8,128)(2,1)S(1)}, u32[]{:S(2)}, u32[]{:S(2)}) collective-permute-start(bf16[128,768]{1,0:T(8,128)(2,1)S(1)} %get-tuple-element.33), channel_id=1, source_target_pairs={{0,1},{1,0},{2,3},{3,2},{4,5},{5,4},{6,7},{7,6},{8,9},{9,8},{10,11... | collective-permute-start | bytes 589832 | tf_op jit(solution)/shard_map/ppermute | solution.py:279
  84.9 10.6 %collective-permute-start.13 = (bf16[768,128]{1,0:T(8,128)(2,1)S(1)}, bf16[768,128]{1,0:T(8,128)(2,1)S(1)}, u32[]{:S(2)}, u32[]{:S(2)}) collective-permute-start(bf16[768,128]{1,0:T(8,128)(2,1)S(1)} %shard_map.104.refs_0_), channel_id=1, source_target_pairs={{0,1},{1,0},{2,3},{3,2},{4,5},{5,4},{6,7},{7,6},{8,9},{9,8},{10,11... | collective-permute-start | bytes 589832 | tf_op jit(solution)/shard_map/ppermute | solution.py:279

commit v5 on v4

--- a/solution.py
+++ b/solution.py
@@ -192,39 +192,43 @@
     return top + jnp.log2(total), inner / total, fade_a / total, total_b / total
 
 
-def backward_kernel(slot, first, last, *refs):
+def backward_kernel(slots, first, last, *refs):
     sides = refs[:2]
-    bias_ref, kv_ref, stat_ref, other_stat_ref = refs[2:6]
-    rest = refs[6:]
+    bias_ref = refs[2]
+    kv_refs = refs[3 : 3 + len(slots)]
+    stat_ref, other_stat_ref, *rest = refs[3 + len(slots) :]
     rows = bias_ref.shape[1]
-    dim = kv_ref.shape[1]
+    dim = kv_refs[0].shape[1]
     if not first:
-        query_in, rest = rest[0], rest[1:]
-    grad_kv_ref, query_out = rest[:2]
+        query_in, *rest = rest
+    grad_refs, rest = rest[: len(slots)], rest[len(slots) :]
+    query_out = rest[0]
     factor = math.log2(math.e) / math.sqrt(dim)
     scale = 1.0 / math.sqrt(dim)
-    key = kv_ref[:rows, :]
-    value = kv_ref[rows:, :]
-    key_t = key.T
-    grad_key = jnp.zeros((rows, dim), F32)
-    grad_value = jnp.zeros((rows, dim), F32)
+    grad_keys = [jnp.zeros((rows, dim), F32) for _ in slots]
+    grad_values = [jnp.zeros((rows, dim), F32) for _ in slots]
     for part, side in enumerate(sides):
         cols = columns_of(stat_ref, part)
         query, grad = part_rows(side, 0), part_rows(side, 1)
         norm, inner, _, _ = merged(stat_ref, other_stat_ref, part)
-        scores = dot(key, query, NT) * factor + bias_ref[slot]
-        probs = jnp.exp2(scores - norm)
-        grad_value = grad_value + dot(probs.astype(BF16), grad, NN)
-        grad_score = (probs * (dot(value, grad, NT) - inner)).astype(BF16)
-        grad_key = grad_key + dot(grad_score, query, NN)
-        grad_query = dot(key_t, grad_score, NN) * scale
+        grad_query = 0.0
+        for place, slot in enumerate(slots):
+            key, value = kv_refs[place][:rows, :], kv_refs[place][rows:, :]
+            scores = dot(key, query, NT) * factor + bias_ref[slot]
+            probs = jnp.exp2(scores - norm)
+            grad_values[place] = grad_values[place] + dot(probs.astype(BF16), grad, NN)
+            grad_score = (probs * (dot(value, grad, NT) - inner)).astype(BF16)
+            grad_keys[place] = grad_keys[place] + dot(grad_score, query, NN)
+            grad_query = grad_query + dot(key.T, grad_score, NN)
+        grad_query = grad_query * scale
         if not first:
             grad_query = query_in[:, cols] + grad_query
         query_out[:, cols] = grad_query
         if last and part == 1:
-            rest[2][...] = grad_query.astype(BF16)
-    grad_kv_ref[:rows, :] = (grad_key * scale).astype(BF16)
-    grad_kv_ref[rows:, :] = grad_value.astype(BF16)
+            rest[1][...] = grad_query.astype(BF16)
+    for ref, grad_key, grad_value in zip(grad_refs, grad_keys, grad_values):
+        ref[:rows, :] = (grad_key * scale).astype(BF16)
+        ref[rows:, :] = grad_value.astype(BF16)
 
 
 def finish_out_kernel(stat_ref, other_stat_ref, out_ref, got_ref, attn_ref):
@@ -347,28 +351,29 @@
 
     returned = []
     query_grad = None
-    for slot in range(SLOTS):
-        first, last = slot == 0, slot == SLOTS - 1
-        kernel = functools.partial(backward_kernel, slot, first, last)
-        args = [own_qg, other_qg, bias, held[slot], stat, other_stat]
+    for slots in ((0,), (1,), (2, 3)):
+        first, last = slots[0] == 0, slots[-1] == SLOTS - 1
+        kernel = functools.partial(backward_kernel, slots, first, last)
+        args = [own_qg, other_qg, bias] + [held[s] for s in slots] + [stat, other_stat]
         if not first:
             args.append(query_grad)
-        shapes = (kv_shape, wide_shape) + ((send_shape,) if last else ())
+        shapes = (kv_shape,) * len(slots) + (wide_shape,) + ((send_shape,) if last else ())
         results = call(
-            kernel, shapes, [VMEM] * len(args), 5 * unit, 4 << 20, rows * columns
+            kernel, shapes, [VMEM] * len(args), 5 * unit * len(slots), 8 << 20, rows * columns * len(slots)
         )(*args)
-        grad_kv, query_grad = results[:2]
-        returned.append(send(grad_kv, lane_pairs(table[slot], True)))
-    got_query = send(results[2], near)
+        query_grad = results[len(slots)]
+        for slot, grad_kv in zip(slots, results):
+            returned.append(send(grad_kv, lane_pairs(table[slot], True)))
+    got_query = send(results[3], near)
 
     def add(pieces, shapes):
         kernel = functools.partial(sum_kernel, len(pieces))
         return call(kernel, shapes, [VMEM] * len(pieces), 0, 1 << 20, 0)(*pieces)
 
     total = add(returned, (kv_shape,))[0]
-    total = add((total, send(total, far)), (kv_shape,))[0]
+    total = add((total, send(total, near)), (kv_shape,))[0]
     key_shape = jax.ShapeDtypeStruct((rows, dim), BF16)
-    grad_keys, grad_values = add((total, send(total, near)), (key_shape, key_shape))
+    grad_keys, grad_values = add((total, send(total, far)), (key_shape, key_shape))
 
     flat = jax.ShapeDtypeStruct((heads * rows, dim), BF16)
     attn = call(finish_out_kernel, flat, [VMEM] * 4, 0, 1 << 20, 0)(

time: 96.6 us -> 95 us (0.983)
  the two profiles are of different devices: /device:TPU:114 before, /device:TPU:112 now
where the time goes in v5:
time: 95 us; the launch traced here: 94.5 us
  starting transfers between devices  44.5 us (47%)
  waiting for transfers between devices  31.2 us (33%)
  Pallas kernels  16.7 us (18%)
  local copies, waits for them, and re-layouts  1.35 us (1%)
    ppermute x14, starting transfers between devices, send(): return lax.ppermute(value, AXES, pairs)  44.5 us
    ppermute x14, waiting for transfers between devices, send(): return lax.ppermute(value, AXES, pairs)  31.2 us
    pallas_call x3, Pallas kernels, local(): call(kernel, shapes, [VMEM] * len(args), 5 * unit * len(slots), 8 << 20,...  6.81 us
    pallas_call x2, Pallas kernels, forward(): call(kernel, (stat_shape, wide_shape) + ((send_shape,) if last else ()),...  4.18 us
  transfers between devices with their start and end apart: 14, of which 9 were waited for; matrix products, arithmetic and copies ran while one was open for 0% of the time, Pallas kernels for 6%

profile of v5, /device:TPU:112, one launch (start us, length us, event | category | flops | bytes accessed | tf_op | source)
XLA Modules:
  0.0 94.5 jit_solution(287524241100410057)
XLA Ops:
  0.6 1.9 %shard_map.93 = (bf16[768,128]{1,0:T(8,128)(2,1)}, bf16[1536,128]{1,0:T(8,128)(2,1)}) custom-call(bf16[384,128]{1,0:T(8,128)(2,1)} %key_ref.1, bf16[384,128]{1,0:T(8,128)(2,1)} %value_ref.1, bf16[768,128]{1,0:T(8,128)(2,1)} %bitcast.6, bf16[768,128]{1,0:T(8,128)(2,1)} %bitcast.7), custom_call_target="tpu_custom_call" | custom-call | tf_op jit(solution)/shard_map/pallas_call | solution.py:290
  2.5 0.0 copy-start
  2.5 3.5 %collective-permute-start = (bf16[1536,128]{1,0:T(8,128)(2,1)}, bf16[1536,128]{1,0:T(8,128)(2,1)S(1)}, u32[]{:S(2)}, u32[]{:S(2)}) collective-permute-start(bf16[1536,128]{1,0:T(8,128)(2,1)} %get-tuple-element.21.refs_0_), channel_id=1, source_target_pairs={{0,1},{1,0},{2,3},{3,2},{4,5},{5,4},{6,7},{7,6},{8,9},{9,8},{10,11... | collective-permute-start | bytes 1179656 | tf_op jit(solution)/shard_map/ppermute | solution.py:283
  6.0 1.9 %collective-permute-start.4 = (bf16[768,128]{1,0:T(8,128)(2,1)}, bf16[768,128]{1,0:T(8,128)(2,1)S(1)}, u32[]{:S(2)}, u32[]{:S(2)}) collective-permute-start(bf16[768,128]{1,0:T(8,128)(2,1)} %get-tuple-element.22), channel_id=1, source_target_pairs={{0,4},{2,6},{4,8},{6,10},{8,12},{10,14},{12,16},{14,18},{16,20},{1... | collective-permute-start | bytes 589832 | tf_op jit(solution)/shard_map/ppermute | solution.py:283
  8.0 5.6 %collective-permute-start.3 = (bf16[768,128]{1,0:T(8,128)(2,1)}, bf16[768,128]{1,0:T(8,128)(2,1)S(1)}, u32[]{:S(2)}, u32[]{:S(2)}) collective-permute-start(bf16[768,128]{1,0:T(8,128)(2,1)} %get-tuple-element.22), channel_id=1, source_target_pairs={{0,32},{2,34},{4,36},{6,38},{8,40},{10,42},{12,44},{14,46},{16,48}... | collective-permute-start | bytes 589832 | tf_op jit(solution)/shard_map/ppermute | solution.py:283
  13.6 5.7 %collective-permute-start.2 = (bf16[768,128]{1,0:T(8,128)(2,1)}, bf16[768,128]{1,0:T(8,128)(2,1)S(1)}, u32[]{:S(2)}, u32[]{:S(2)}) collective-permute-start(bf16[768,128]{1,0:T(8,128)(2,1)} %get-tuple-element.22), channel_id=1, source_target_pairs={{0,256},{2,258},{4,260},{6,262},{8,264},{10,266},{12,268},{14,270}... | collective-permute-start | bytes 589832 | tf_op jit(solution)/shard_map/ppermute | solution.py:283
  19.3 1.9 %collective-permute-start.1 = (bf16[768,128]{1,0:T(8,128)(2,1)}, bf16[768,128]{1,0:T(8,128)(2,1)S(1)}, u32[]{:S(2)}, u32[]{:S(2)}) collective-permute-start(bf16[768,128]{1,0:T(8,128)(2,1)} %get-tuple-element.22), channel_id=1, source_target_pairs={{0,64},{2,66},{4,68},{6,70},{8,72},{10,74},{12,76},{14,78},{16,80}... | collective-permute-start | bytes 589832 | tf_op jit(solution)/shard_map/ppermute | solution.py:283
  21.2 0.0 copy-start.1
  21.2 0.7 copy-done.1
  21.9 0.0 copy-start.2
  21.9 0.7 copy-done.2
  22.6 1.3 %shard_map.94.refs_2_ = f32[4,384,768]{2,1,0:T(8,128)S(1)} custom-call(s32[64]{0:T(128)S(1)} %copy-done.2, s32[3,384]{1,0:T(4,128)S(1)} %copy-done.1), custom_call_target="tpu_custom_call" | custom-call | tf_op jit(solution)/shard_map/pallas_call | solution.py:314
  23.9 0.0 collective-permute-done.4.refs_5_.refs_4_
  23.9 1.8 %collective-permute-done.3.refs_4_.refs_3_ = bf16[768,128]{1,0:T(8,128)(2,1)S(1)} collective-permute-done((bf16[768,128]{1,0:T(8,128)(2,1)}, bf16[768,128]{1,0:T(8,128)(2,1)S(1)}, u32[]{:S(2)}, u32[]{:S(2)}) %collective-permute-start.3) | collective-permute-done | bytes 196640 | tf_op jit(solution)/shard_map/ppermute | solution.py:283
  25.8 0.0 collective-permute-done.2.refs_3_
  25.8 0.0 collective-permute-done.refs_1_
  25.8 0.0 copy-done
  25.8 3.0 %shard_map.95 = (f32[4,1536]{1,0:T(4,128)S(1)}, f32[128,1536]{1,0:T(8,128)S(1)}) custom-call(bf16[1536,128]{1,0:T(8,128)(2,1)S(1)} %copy-done, bf16[1536,128]{1,0:T(8,128)(2,1)S(1)} %collective-permute-done.refs_1_, f32[4,384,768]{2,1,0:T(8,128)S(1)} %shard_map.94.refs_2_, bf16[768,128]{1,0:T(8,128)(2,1)S(1)} %collective-permute-done.2.refs_3_, ...), custom_call_target="tpu_custom_call" | custom-call | flops 905969664 | bytes 4194304 | tf_op jit(solution)/shard_map/pallas_call | solution.py:338
  28.8 4.2 %collective-permute-done.1.refs_3_ = bf16[768,128]{1,0:T(8,128)(2,1)S(1)} collective-permute-done((bf16[768,128]{1,0:T(8,128)(2,1)}, bf16[768,128]{1,0:T(8,128)(2,1)S(1)}, u32[]{:S(2)}, u32[]{:S(2)}) %collective-permute-start.1) | collective-permute-done | bytes 196640 | tf_op jit(solution)/shard_map/ppermute | solution.py:283
  33.0 1.2 %shard_map.96 = (f32[4,1536]{1,0:T(4,128)S(1)}, f32[128,1536]{1,0:T(8,128)S(1)}, bf16[128,768]{1,0:T(8,128)(2,1)S(1)}) custom-call(bf16[1536,128]{1,0:T(8,128)(2,1)S(1)} %copy-done, bf16[1536,128]{1,0:T(8,128)(2,1)S(1)} %collective-permute-done.refs_1_, f32[4,384,768]{2,1,0:T(8,128)S(1)} %shard_map.94.refs_2_, ...), custom_call_target="tpu_custom_call" | custom-call | flops 301989888 | bytes 4194304 | tf_op jit(solution)/shard_map/pallas_call | solution.py:338
  34.2 1.9 %collective-permute-start.5 = (f32[4,1536]{1,0:T(4,128)S(1)}, f32[4,1536]{1,0:T(4,128)S(1)}, u32[]{:S(2)}, u32[]{:S(2)}) collective-permute-start(f32[4,1536]{1,0:T(4,128)S(1)} %get-tuple-element.25.stat_ref.refs_4_.refs_5_), channel_id=1, source_target_pairs={{0,1},{1,0},{2,3},{3,2},{4,5},{5,4},{6,7},{7,6},{8,9},{9,8},{10,11... | collective-permute-start | bytes 73736 | tf_op jit(solution)/shard_map/ppermute | solution.py:283
  36.2 3.8 %collective-permute-done.5.other_stat_ref.refs_5_.refs_6_ = f32[4,1536]{1,0:T(4,128)S(1)} collective-permute-done((f32[4,1536]{1,0:T(4,128)S(1)}, f32[4,1536]{1,0:T(4,128)S(1)}, u32[]{:S(2)}, u32[]{:S(2)}) %collective-permute-start.5) | collective-permute-done | bytes 24608 | tf_op jit(solution)/shard_map/ppermute | solution.py:283
  40.0 1.8 %shard_map.98 = (bf16[768,128]{1,0:T(8,128)(2,1)S(1)}, f32[128,1536]{1,0:T(8,128)S(1)}) custom-call(bf16[1536,128]{1,0:T(8,128)(2,1)S(1)} %copy-done, bf16[1536,128]{1,0:T(8,128)(2,1)S(1)} %collective-permute-done.refs_1_, f32[4,384,768]{2,1,0:T(8,128)S(1)} %shard_map.94.refs_2_, bf16[768,128]{1,0:T(8,128)(2,1)S(1)} %collective-permute-done.2.refs_3_, ...), custom_call_target="tpu_custom_call" | custom-call | flops 754974720 | bytes 8388608 | tf_op jit(solution)/shard_map/pallas_call | solution.py:361
  41.8 1.8 %shard_map.99 = (bf16[768,128]{1,0:T(8,128)(2,1)S(1)}, f32[128,1536]{1,0:T(8,128)S(1)}) custom-call(bf16[1536,128]{1,0:T(8,128)(2,1)S(1)} %copy-done, bf16[1536,128]{1,0:T(8,128)(2,1)S(1)} %collective-permute-done.refs_1_, f32[4,384,768]{2,1,0:T(8,128)S(1)} %shard_map.94.refs_2_, bf16[768,128]{1,0:T(8,128)(2,1)S(1)} %collective-permute-done.3.refs_4_.refs_3_, ...), custom_call_target="tpu_custom_call" | custom-call | flops 754974720 | bytes 8388608 | tf_op jit(solution)/shard_map/pallas_call | solution.py:361
  43.6 3.2 %shard_map.100 = (bf16[768,128]{1,0:T(8,128)(2,1)S(1)}, bf16[768,128]{1,0:T(8,128)(2,1)S(1)}, f32[128,1536]{1,0:T(8,128)S(1)}, bf16[128,768]{1,0:T(8,128)(2,1)S(1)}) custom-call(bf16[1536,128]{1,0:T(8,128)(2,1)S(1)} %copy-done, bf16[1536,128]{1,0:T(8,128)(2,1)S(1)} %collective-permute-done.refs_1_, f32[4,384,768]{2,1,0:T(8,128)S(1)} %shard_map.94.refs_2_, ...), custom_call_target="tpu_custom_call" | custom-call | flops 1509949440 | bytes 8388608 | tf_op jit(solution)/shard_map/pallas_call | solution.py:361
  46.8 1.9 %collective-permute-start.10 = (bf16[768,128]{1,0:T(8,128)(2,1)S(1)}, bf16[768,128]{1,0:T(8,128)(2,1)S(1)}, u32[]{:S(2)}, u32[]{:S(2)}) collective-permute-start(bf16[768,128]{1,0:T(8,128)(2,1)S(1)} %get-tuple-element.34), channel_id=1, source_target_pairs={{64,0},{66,2},{68,4},{70,6},{72,8},{74,10},{76,12},{78,14},{80,16}... | collective-permute-start | bytes 589832 | tf_op jit(solution)/shard_map/ppermute | solution.py:283
  48.7 1.9 %collective-permute-start.11 = (bf16[768,128]{1,0:T(8,128)(2,1)S(1)}, bf16[768,128]{1,0:T(8,128)(2,1)S(1)}, u32[]{:S(2)}, u32[]{:S(2)}) collective-permute-start(bf16[768,128]{1,0:T(8,128)(2,1)S(1)} %get-tuple-element.35), channel_id=1, source_target_pairs={{4,0},{6,2},{8,4},{10,6},{12,8},{14,10},{16,12},{18,14},{20,16},{2... | collective-permute-start | bytes 589832 | tf_op jit(solution)/shard_map/ppermute | solution.py:283
  50.7 7.6 %collective-permute-start.9 = (bf16[768,128]{1,0:T(8,128)(2,1)S(1)}, bf16[768,128]{1,0:T(8,128)(2,1)S(1)}, u32[]{:S(2)}, u32[]{:S(2)}) collective-permute-start(bf16[768,128]{1,0:T(8,128)(2,1)S(1)} %get-tuple-element.33), channel_id=1, source_target_pairs={{32,0},{34,2},{36,4},{38,6},{40,8},{42,10},{44,12},{46,14},{48,16}... | collective-permute-start | bytes 589832 | tf_op jit(solution)/shard_map/ppermute | solution.py:283
  58.3 1.3 %collective-permute-start.8 = (bf16[768,128]{1,0:T(8,128)(2,1)S(1)}, bf16[768,128]{1,0:T(8,128)(2,1)S(1)}, u32[]{:S(2)}, u32[]{:S(2)}) collective-permute-start(bf16[768,128]{1,0:T(8,128)(2,1)S(1)} %get-tuple-element.32), channel_id=1, source_target_pairs={{256,0},{258,2},{260,4},{262,6},{264,8},{266,10},{268,12},{270,14}... | collective-permute-start | bytes 589832 | tf_op jit(solution)/shard_map/ppermute | solution.py:283
  59.6 0.0 collective-permute-done.10.refs_2_
  59.6 0.0 collective-permute-done.11.refs_3_
  59.6 11.0 %collective-permute-done.9.refs_1_ = bf16[768,128]{1,0:T(8,128)(2,1)S(1)} collective-permute-done((bf16[768,128]{1,0:T(8,128)(2,1)S(1)}, bf16[768,128]{1,0:T(8,128)(2,1)S(1)}, u32[]{:S(2)}, u32[]{:S(2)}) %collective-permute-start.9) | collective-permute-done | bytes 196640 | tf_op jit(solution)/shard_map/ppermute | solution.py:283
  70.6 4.7 %collective-permute-done.8.refs_0_ = bf16[768,128]{1,0:T(8,128)(2,1)S(1)} collective-permute-done((bf16[768,128]{1,0:T(8,128)(2,1)S(1)}, bf16[768,128]{1,0:T(8,128)(2,1)S(1)}, u32[]{:S(2)}, u32[]{:S(2)}) %collective-permute-start.8) | collective-permute-done | bytes 196640 | tf_op jit(solution)/shard_map/ppermute | solution.py:283
  75.2 0.1 shard_map.102.refs_0_
  75.3 1.9 %collective-permute-start.12 = (bf16[768,128]{1,0:T(8,128)(2,1)S(1)}, bf16[768,128]{1,0:T(8,128)(2,1)S(1)}, u32[]{:S(2)}, u32[]{:S(2)}) collective-permute-start(bf16[768,128]{1,0:T(8,128)(2,1)S(1)} %shard_map.102.refs_0_), channel_id=1, source_target_pairs={{0,1},{1,0},{2,3},{3,2},{4,5},{5,4},{6,7},{7,6},{8,9},{9,8},{10,11... | collective-permute-start | bytes 589832 | tf_op jit(solution)/shard_map/ppermute | solution.py:283
  77.3 3.9 %collective-permute-start.6 = (bf16[128,768]{1,0:T(8,128)(2,1)S(1)}, bf16[128,768]{1,0:T(8,128)(2,1)S(1)}, u32[]{:S(2)}, u32[]{:S(2)}) collective-permute-start(bf16[128,768]{1,0:T(8,128)(2,1)S(1)} %get-tuple-element.27), channel_id=1, source_target_pairs={{0,1},{1,0},{2,3},{3,2},{4,5},{5,4},{6,7},{7,6},{8,9},{9,8},{10,11... | collective-permute-start | bytes 589832 | tf_op jit(solution)/shard_map/ppermute | solution.py:283
  81.2 1.9 %collective-permute-start.7 = (bf16[128,768]{1,0:T(8,128)(2,1)S(1)}, bf16[128,768]{1,0:T(8,128)(2,1)S(1)}, u32[]{:S(2)}, u32[]{:S(2)}) collective-permute-start(bf16[128,768]{1,0:T(8,128)(2,1)S(1)} %get-tuple-element.31), channel_id=1, source_target_pairs={{0,1},{1,0},{2,3},{3,2},{4,5},{5,4},{6,7},{7,6},{8,9},{9,8},{10,11... | collective-permute-start | bytes 589832 | tf_op jit(solution)/shard_map/ppermute | solution.py:283
  83.1 1.9 %collective-permute-done.12.refs_1_ = bf16[768,128]{1,0:T(8,128)(2,1)S(1)} collective-permute-done((bf16[768,128]{1,0:T(8,128)(2,1)S(1)}, bf16[768,128]{1,0:T(8,128)(2,1)S(1)}, u32[]{:S(2)}, u32[]{:S(2)}) %collective-permute-start.12) | collective-permute-done | bytes 196640 | tf_op jit(solution)/shard_map/ppermute | solution.py:283
  85.1 3.3 %collective-permute-start.13 = (bf16[768,128]{1,0:T(8,128)(2,1)S(1)}, bf16[768,128]{1,0:T(8,128)(2,1)S(1)}, u32[]{:S(2)}, u32[]{:S(2)}) collective-permute-start(bf16[768,128]{1,0:T(8,128)(2,1)S(1)} %shard_map.103.refs_0_), channel_id=1, source_target_pairs={{0,3},{1,2},{2,1},{3,0},{4,7},{5,6},{6,5},{7,4},{8,11},{9,10},{10,... | collective-permute-start | bytes 589832 | tf_op jit(solution)/shard_map/ppermute | solution.py:283
  88.4 0.8 collective-permute-done.6.got_ref
  89.2 0.8 shard_map.97
  90.1 2.1 %collective-permute-done.7.got_ref = bf16[128,768]{1,0:T(8,128)(2,1)S(1)} collective-permute-done((bf16[128,768]{1,0:T(8,128)(2,1)S(1)}, bf16[128,768]{1,0:T(8,128)(2,1)S(1)}, u32[]{:S(2)}, u32[]{:S(2)}) %collective-permute-start.7) | collective-permute-done | bytes 196640 | tf_op jit(solution)/shard_map/ppermute | solution.py:283
  92.2 0.8 shard_map.101
  93.0 0.8 collective-permute-done.13.refs_1_
  93.8 0.7 shard_map.104
  (1 shorter events, 0.0 us)
Async XLA Ops:
  2.5 23.3 %copy-start = (bf16[1536,128]{1,0:T(8,128)(2,1)S(1)}, bf16[1536,128]{1,0:T(8,128)(2,1)}, u32[]{:S(2)}) copy-start(bf16[1536,128]{1,0:T(8,128)(2,1)} %get-tuple-element.21.refs_0_) | copy-start | bytes 1179652
  2.5 23.3 %collective-permute-start = (bf16[1536,128]{1,0:T(8,128)(2,1)}, bf16[1536,128]{1,0:T(8,128)(2,1)S(1)}, u32[]{:S(2)}, u32[]{:S(2)}) collective-permute-start(bf16[1536,128]{1,0:T(8,128)(2,1)} %get-tuple-element.21.refs_0_), channel_id=1, source_target_pairs={{0,1},{1,0},{2,3},{3,2},{4,5},{5,4},{6,7},{7,6},{8,9},{9,8},{10,11... | collective-permute-start | bytes 1179656 | tf_op jit(solution)/shard_map/ppermute | solution.py:283
  6.0 17.9 %collective-permute-start.4 = (bf16[768,128]{1,0:T(8,128)(2,1)}, bf16[768,128]{1,0:T(8,128)(2,1)S(1)}, u32[]{:S(2)}, u32[]{:S(2)}) collective-permute-start(bf16[768,128]{1,0:T(8,128)(2,1)} %get-tuple-element.22), channel_id=1, source_target_pairs={{0,4},{2,6},{4,8},{6,10},{8,12},{10,14},{12,16},{14,18},{16,20},{1... | collective-permute-start | bytes 589832 | tf_op jit(solution)/shard_map/ppermute | solution.py:283
  8.0 17.8 %collective-permute-start.3 = (bf16[768,128]{1,0:T(8,128)(2,1)}, bf16[768,128]{1,0:T(8,128)(2,1)S(1)}, u32[]{:S(2)}, u32[]{:S(2)}) collective-permute-start(bf16[768,128]{1,0:T(8,128)(2,1)} %get-tuple-element.22), channel_id=1, source_target_pairs={{0,32},{2,34},{4,36},{6,38},{8,40},{10,42},{12,44},{14,46},{16,48}... | collective-permute-start | bytes 589832 | tf_op jit(solution)/shard_map/ppermute | solution.py:283
  13.6 12.2 %collective-permute-start.2 = (bf16[768,128]{1,0:T(8,128)(2,1)}, bf16[768,128]{1,0:T(8,128)(2,1)S(1)}, u32[]{:S(2)}, u32[]{:S(2)}) collective-permute-start(bf16[768,128]{1,0:T(8,128)(2,1)} %get-tuple-element.22), channel_id=1, source_target_pairs={{0,256},{2,258},{4,260},{6,262},{8,264},{10,266},{12,268},{14,270}... | collective-permute-start | bytes 589832 | tf_op jit(solution)/shard_map/ppermute | solution.py:283
  19.3 13.7 %collective-permute-start.1 = (bf16[768,128]{1,0:T(8,128)(2,1)}, bf16[768,128]{1,0:T(8,128)(2,1)S(1)}, u32[]{:S(2)}, u32[]{:S(2)}) collective-permute-start(bf16[768,128]{1,0:T(8,128)(2,1)} %get-tuple-element.22), channel_id=1, source_target_pairs={{0,64},{2,66},{4,68},{6,70},{8,72},{10,74},{12,76},{14,78},{16,80}... | collective-permute-start | bytes 589832 | tf_op jit(solution)/shard_map/ppermute | solution.py:283
  21.2 0.7 copy-start.1
  21.9 0.7 copy-start.2
  34.2 5.7 %collective-permute-start.5 = (f32[4,1536]{1,0:T(4,128)S(1)}, f32[4,1536]{1,0:T(4,128)S(1)}, u32[]{:S(2)}, u32[]{:S(2)}) collective-permute-start(f32[4,1536]{1,0:T(4,128)S(1)} %get-tuple-element.25.stat_ref.refs_4_.refs_5_), channel_id=1, source_target_pairs={{0,1},{1,0},{2,3},{3,2},{4,5},{5,4},{6,7},{7,6},{8,9},{9,8},{10,11... | collective-permute-start | bytes 73736 | tf_op jit(solution)/shard_map/ppermute | solution.py:283
  46.8 12.8 %collective-permute-start.10 = (bf16[768,128]{1,0:T(8,128)(2,1)S(1)}, bf16[768,128]{1,0:T(8,128)(2,1)S(1)}, u32[]{:S(2)}, u32[]{:S(2)}) collective-permute-start(bf16[768,128]{1,0:T(8,128)(2,1)S(1)} %get-tuple-element.34), channel_id=1, source_target_pairs={{64,0},{66,2},{68,4},{70,6},{72,8},{74,10},{76,12},{78,14},{80,16}... | collective-permute-start | bytes 589832 | tf_op jit(solution)/shard_map/ppermute | solution.py:283
  48.7 10.9 %collective-permute-start.11 = (bf16[768,128]{1,0:T(8,128)(2,1)S(1)}, bf16[768,128]{1,0:T(8,128)(2,1)S(1)}, u32[]{:S(2)}, u32[]{:S(2)}) collective-permute-start(bf16[768,128]{1,0:T(8,128)(2,1)S(1)} %get-tuple-element.35), channel_id=1, source_target_pairs={{4,0},{6,2},{8,4},{10,6},{12,8},{14,10},{16,12},{18,14},{20,16},{2... | collective-permute-start | bytes 589832 | tf_op jit(solution)/shard_map/ppermute | solution.py:283
  50.7 19.9 %collective-permute-start.9 = (bf16[768,128]{1,0:T(8,128)(2,1)S(1)}, bf16[768,128]{1,0:T(8,128)(2,1)S(1)}, u32[]{:S(2)}, u32[]{:S(2)}) collective-permute-start(bf16[768,128]{1,0:T(8,128)(2,1)S(1)} %get-tuple-element.33), channel_id=1, source_target_pairs={{32,0},{34,2},{36,4},{38,6},{40,8},{42,10},{44,12},{46,14},{48,16}... | collective-permute-start | bytes 589832 | tf_op jit(solution)/shard_map/ppermute | solution.py:283
  58.3 16.9 %collective-permute-start.8 = (bf16[768,128]{1,0:T(8,128)(2,1)S(1)}, bf16[768,128]{1,0:T(8,128)(2,1)S(1)}, u32[]{:S(2)}, u32[]{:S(2)}) collective-permute-start(bf16[768,128]{1,0:T(8,128)(2,1)S(1)} %get-tuple-element.32), channel_id=1, source_target_pairs={{256,0},{258,2},{260,4},{262,6},{264,8},{266,10},{268,12},{270,14}... | collective-permute-start | bytes 589832 | tf_op jit(solution)/shard_map/ppermute | solution.py:283
  75.3 9.7 %collective-permute-start.12 = (bf16[768,128]{1,0:T(8,128)(2,1)S(1)}, bf16[768,128]{1,0:T(8,128)(2,1)S(1)}, u32[]{:S(2)}, u32[]{:S(2)}) collective-permute-start(bf16[768,128]{1,0:T(8,128)(2,1)S(1)} %shard_map.102.refs_0_), channel_id=1, source_target_pairs={{0,1},{1,0},{2,3},{3,2},{4,5},{5,4},{6,7},{7,6},{8,9},{9,8},{10,11... | collective-permute-start | bytes 589832 | tf_op jit(solution)/shard_map/ppermute | solution.py:283
  77.3 12.0 %collective-permute-start.6 = (bf16[128,768]{1,0:T(8,128)(2,1)S(1)}, bf16[128,768]{1,0:T(8,128)(2,1)S(1)}, u32[]{:S(2)}, u32[]{:S(2)}) collective-permute-start(bf16[128,768]{1,0:T(8,128)(2,1)S(1)} %get-tuple-element.27), channel_id=1, source_target_pairs={{0,1},{1,0},{2,3},{3,2},{4,5},{5,4},{6,7},{7,6},{8,9},{9,8},{10,11... | collective-permute-start | bytes 589832 | tf_op jit(solution)/shard_map/ppermute | solution.py:283
  81.2 11.0 %collective-permute-start.7 = (bf16[128,768]{1,0:T(8,128)(2,1)S(1)}, bf16[128,768]{1,0:T(8,128)(2,1)S(1)}, u32[]{:S(2)}, u32[]{:S(2)}) collective-permute-start(bf16[128,768]{1,0:T(8,128)(2,1)S(1)} %get-tuple-element.31), channel_id=1, source_target_pairs={{0,1},{1,0},{2,3},{3,2},{4,5},{5,4},{6,7},{7,6},{8,9},{9,8},{10,11... | collective-permute-start | bytes 589832 | tf_op jit(solution)/shard_map/ppermute | solution.py:283
  85.1 8.8 %collective-permute-start.13 = (bf16[768,128]{1,0:T(8,128)(2,1)S(1)}, bf16[768,128]{1,0:T(8,128)(2,1)S(1)}, u32[]{:S(2)}, u32[]{:S(2)}) collective-permute-start(bf16[768,128]{1,0:T(8,128)(2,1)S(1)} %shard_map.103.refs_0_), channel_id=1, source_target_pairs={{0,3},{1,2},{2,1},{3,0},{4,7},{5,6},{6,5},{7,4},{8,11},{9,10},{10,... | collective-permute-start | bytes 589832 | tf_op jit(solution)/shard_map/ppermute | solution.py:283
